TPU v7x, 256 devices: a whole 4x4x8 slice. The times are simulated.
256 devices in a mesh: grp: 8 (over x, core), uly: 32 (over z, y).
Axes of the slice: x: 4, y: 4, z: 8, core: 2. Of those that a mesh axis runs over, the one named last changes fastest.
Arguments:
- queries: bfloat16 [32768, 8192], P(('grp', 'uly')), may hold values from -6 to 6
- key_state_rows: bfloat16 [32768, 1024], P(('grp', 'uly')), may hold values from -6 to 6
- value_state_rows: bfloat16 [32768, 1024], P(('grp', 'uly')), may hold values from -6 to 6
- vert_blocks: int32 [64, 6], replicated, may hold values from -1 to 255, as said below
- slash_offsets: int32 [64, 3], replicated, may hold values from -1 to 16, as said below
Outputs:
- attended: bfloat16 [32768, 8192], P(('grp', 'uly'))
Inputs may be any that keep to these rules, and one draw needn't show every extreme that they name: `vert_blocks`: row h lists distinct block numbers first and -1 in the slots after them; every row lists one block or more and some row lists 6. `slash_offsets`: row h lists distinct offsets of at least 1 first and -1 in the slots after them; every row lists one offset or more and some row lists 3.
All inputs are finite; a program needn't handle non-finite values.
Results may differ from a plain program's by a relative error of at most 0.005.
Values may be sent and summed in bfloat16 or wider, within the bound.
No kernel may reach another device: no remote copies, remote signals or barrier semaphores. Data moves between devices by JAX's collectives and lax.ppermute only.
A program may use at most 128 MiB of HBM per device.

v0:
```python
import jax
import jax.numpy as jnp
import numpy as np
from jax import lax
from jax.sharding import PartitionSpec as P

QUERY_HEADS = 64
KEY_VALUE_HEADS = 8
HEAD_SIZE = 128
BLOCK_TOKENS = 128


neg_large = -1e30


def passed_along(value, axis, steps):
    count = lax.axis_size(axis)
    initial, last = (max(0, -steps), min(count, count - steps))
    return lax.ppermute(value, axis, [(source, source + steps) for source in range(initial, last)])


def add_slot(running, slot_scores, allowed, weigh):
    best, total, accum = running
    slot_scores = jnp.where(allowed, slot_scores, neg_large)
    new_best = jnp.maximum(best, jnp.max(slot_scores, axis=-1))
    factor = jnp.exp(best - new_best)
    weights = jnp.where(allowed, jnp.exp(slot_scores - new_best[..., None]), 0.0)
    total = total * factor + jnp.sum(weights, axis=-1)
    accum = accum * factor[..., None] + weigh(weights.astype(jnp.bfloat16))
    return (new_best, total, accum)


def shards(queries, key_state_rows, value_state_rows, vert_blocks, slash_offsets):
    ulysses_count = lax.axis_size("uly")
    group_id = lax.axis_index("grp")
    uly_id = lax.axis_index("uly")
    per_device = QUERY_HEADS // ulysses_count
    group_width = QUERY_HEADS // KEY_VALUE_HEADS
    token_rows = queries.shape[0]
    ordering = jnp.arange(QUERY_HEADS, dtype=jnp.int32)
    heads_per_slot = np.arange(ulysses_count) * per_device // group_width
    key_outgoing = key_state_rows.reshape(token_rows, KEY_VALUE_HEADS, HEAD_SIZE)[
        :, heads_per_slot
    ].reshape(token_rows, ulysses_count * HEAD_SIZE)
    value_outgoing = value_state_rows.reshape(token_rows, KEY_VALUE_HEADS, HEAD_SIZE)[
        :, heads_per_slot
    ].reshape(token_rows, ulysses_count * HEAD_SIZE)
    q_group, k_group, v_group = (
        lax.all_to_all(queries, "uly", split_axis=1, concat_axis=0, tiled=True),
        lax.all_to_all(key_outgoing, "uly", split_axis=1, concat_axis=0, tiled=True),
        lax.all_to_all(value_outgoing, "uly", split_axis=1, concat_axis=0, tiled=True),
    )
    seg_rows = q_group.shape[0]
    block_count = seg_rows // BLOCK_TOKENS
    reach = block_count // 2
    q_tiles = q_group.reshape(block_count, BLOCK_TOKENS, per_device, HEAD_SIZE)
    key_block_tiles = k_group.reshape(block_count, BLOCK_TOKENS, HEAD_SIZE)
    value_block_tiles = v_group.reshape(block_count, BLOCK_TOKENS, HEAD_SIZE)
    prior_k, prior_v = passed_along(
        (key_block_tiles[block_count - reach :], value_block_tiles[block_count - reach :]), "grp", 1
    )
    k_wide = jnp.concatenate([prior_k, key_block_tiles], axis=0)
    v_wide = jnp.concatenate([prior_v, value_block_tiles], axis=0)
    heads_here = lax.dynamic_slice_in_dim(ordering, uly_id * per_device, per_device)
    vert_list = jnp.take(vert_blocks, heads_here, axis=0)
    offset_list = jnp.take(slash_offsets, heads_here, axis=0)
    local_block = jnp.where(vert_list >= 0, vert_list % block_count, 0)
    owned = (vert_list >= 0) & (vert_list // block_count == group_id)
    pick_k = jnp.where(
        owned[:, :, None, None], key_block_tiles[local_block], jnp.zeros((), jnp.bfloat16)
    )
    pick_v = jnp.where(
        owned[:, :, None, None], value_block_tiles[local_block], jnp.zeros((), jnp.bfloat16)
    )
    every_k, every_v = (
        lax.all_gather(pick_k[None], "grp", axis=0, tiled=True),
        lax.all_gather(pick_v[None], "grp", axis=0, tiled=True),
    )
    vert_k = jnp.sum(every_k.astype(jnp.float32), axis=0).astype(jnp.bfloat16)
    vert_v = jnp.sum(every_v.astype(jnp.float32), axis=0).astype(jnp.bfloat16)
    query_blocks = group_id * block_count + jnp.arange(block_count, dtype=jnp.int32)
    score_scale = HEAD_SIZE ** (-0.5)
    causal = (jnp.arange(BLOCK_TOKENS)[:, None] >= jnp.arange(BLOCK_TOKENS)[None, :])[
        None, :, None, :
    ]
    diag_scores = (
        jnp.einsum("nqhd,nkd->nqhk", q_tiles, key_block_tiles, preferred_element_type=jnp.float32)
        * score_scale
    )
    diag_scores = jnp.where(causal, diag_scores, neg_large)
    best = jnp.max(diag_scores, axis=-1)
    diag_weights = jnp.where(causal, jnp.exp(diag_scores - best[..., None]), 0.0)
    total = jnp.sum(diag_weights, axis=-1)
    accum = jnp.einsum(
        "nqhk,nkd->nqhd",
        diag_weights.astype(jnp.bfloat16),
        value_block_tiles,
        preferred_element_type=jnp.float32,
    )
    running = (best, total, accum)

    def slash_slot(slot_index, running):
        offset_now = lax.dynamic_index_in_dim(offset_list, slot_index, axis=1, keepdims=False)
        starts = jnp.where(offset_now >= 1, reach - offset_now, 0)

        def near_slice(begin_at):
            return (
                lax.dynamic_slice_in_dim(k_wide, begin_at, block_count, 0),
                lax.dynamic_slice_in_dim(v_wide, begin_at, block_count, 0),
            )

        k_near, v_near = jax.vmap(near_slice)(starts)
        allowed = (offset_now[None, :] >= 1) & (query_blocks[:, None] - offset_now[None, :] >= 0)
        slot_scores = (
            jnp.einsum("nqhd,hnkd->nqhk", q_tiles, k_near, preferred_element_type=jnp.float32)
            * score_scale
        )

        def weigh_near(prob_low):
            return jnp.einsum(
                "nqhk,hnkd->nqhd", prob_low, v_near, preferred_element_type=jnp.float32
            )

        return add_slot(running, slot_scores, allowed[:, None, :, None], weigh_near)

    slash_turns = jnp.max(jnp.sum((offset_list >= 1).astype(jnp.int32), axis=1))
    running = lax.fori_loop(0, slash_turns, slash_slot, running)

    def vert_slot(slot_index, running):
        block_now = lax.dynamic_index_in_dim(vert_list, slot_index, axis=1, keepdims=False)
        k_far = lax.dynamic_index_in_dim(vert_k, slot_index, axis=1, keepdims=False)
        v_far = lax.dynamic_index_in_dim(vert_v, slot_index, axis=1, keepdims=False)
        hits = (offset_list[None, :, :] >= 1) & (
            query_blocks[:, None, None] - offset_list[None, :, :] == block_now[None, :, None]
        )
        allowed = (
            (block_now[None, :] >= 0)
            & (block_now[None, :] < query_blocks[:, None])
            & jnp.logical_not(jnp.any(hits, axis=2))
        )
        slot_scores = (
            jnp.einsum("nqhd,hkd->nqhk", q_tiles, k_far, preferred_element_type=jnp.float32)
            * score_scale
        )

        def weigh_far(prob_low):
            return jnp.einsum("nqhk,hkd->nqhd", prob_low, v_far, preferred_element_type=jnp.float32)

        return add_slot(running, slot_scores, allowed[:, None, :, None], weigh_far)

    vert_turns = jnp.max(jnp.sum((vert_list >= 0).astype(jnp.int32), axis=1))
    best, total, accum = lax.fori_loop(0, vert_turns, vert_slot, running)
    mixed = (
        (accum / total[..., None]).astype(jnp.bfloat16).reshape(seg_rows, per_device * HEAD_SIZE)
    )
    returned = lax.all_to_all(mixed, "uly", split_axis=0, concat_axis=1, tiled=True)
    return returned


def solution(mesh):
    return jax.shard_map(
        shards,
        mesh=mesh,
        in_specs=(
            P(("grp", "uly"), None),
            P(("grp", "uly"), None),
            P(("grp", "uly"), None),
            P(),
            P(),
        ),
        out_specs=P(("grp", "uly"), None),
        check_vma=False,
    )
```

profile of v0, /device:TPU:1, one launch (start us, length us, event | category | flops | bytes accessed | tf_op | source)
XLA Modules:
  0.0 322.3 jit_solution(7145582446813823165)
XLA Ops:
  10.2 12.2 %all-to-all-start.2 = ((bf16[128,32,128]{2,0,1:T(8,128)(2,1)}), bf16[128,32,128]{2,0,1:T(8,128)(2,1)S(1)}, u32[]{:S(2)}, u32[]{:S(2)}) async-start(bf16[128,32,128]{2,0,1:T(8,128)(2,1)} %bitcast.10), calls=%async_computation.2 | async-start | bytes 2097152 | tf_op jit(solution)/shard_map/all_to_all | solution.py:51
  24.4 24.2 %all-to-all-done.2 = bf16[128,32,128]{2,0,1:T(8,128)(2,1)S(1)} async-done(((bf16[128,32,128]{2,0,1:T(8,128)(2,1)}), bf16[128,32,128]{2,0,1:T(8,128)(2,1)S(1)}, u32[]{:S(2)}, u32[]{:S(2)}) %all-to-all-start.2) | async-done | bytes 1048608 | tf_op jit(solution)/shard_map/all_to_all | solution.py:51
  48.6 6.4 %all-to-all-start = ((bf16[128,32,128]{2,0,1:T(8,128)(2,1)}), bf16[128,32,128]{2,0,1:T(8,128)(2,1)S(1)}, u32[]{:S(2)}, u32[]{:S(2)}) async-start(bf16[128,32,128]{2,0,1:T(8,128)(2,1)} %bitcast.1), calls=%async_computation | async-start | bytes 2097152 | tf_op jit(solution)/shard_map/all_to_all | solution.py:50
  56.7 23.6 %all-to-all-done = bf16[128,32,128]{2,0,1:T(8,128)(2,1)S(1)} async-done(((bf16[128,32,128]{2,0,1:T(8,128)(2,1)}), bf16[128,32,128]{2,0,1:T(8,128)(2,1)S(1)}, u32[]{:S(2)}, u32[]{:S(2)}) %all-to-all-start) | async-done | bytes 1048608 | tf_op jit(solution)/shard_map/all_to_all | solution.py:50
  81.9 4.1 %copy.127 = bf16[128,8192]{0,1:T(8,128)(2,1)} copy(bf16[128,8192]{1,0:T(8,128)(2,1)} %param.12) | data formatting | bytes 4194304 | tf_op args[0]
  86.0 7.0 %all-to-all-start.1 = ((bf16[128,32,256]{0,2,1:T(8,128)(2,1)}), bf16[128,32,256]{0,2,1:T(8,128)(2,1)S(1)}, u32[]{:S(2)}, u32[]{:S(2)}) async-start(bf16[128,32,256]{0,2,1:T(8,128)(2,1)} %bitcast.157), calls=%async_computation.1 | async-start | bytes 4194304 | tf_op jit(solution)/shard_map/all_to_all | solution.py:49
  94.9 5.5 %collective-permute-start = (bf16[16,128,128]{2,1,0:T(8,128)(2,1)}, bf16[16,128,128]{2,1,0:T(8,128)(2,1)}, u32[]{:S(2)}, u32[]{:S(2)}) collective-permute-start(bf16[16,128,128]{2,1,0:T(8,128)(2,1)} %slice.26), channel_id=1, source_target_pairs={{0,32},{32,64},{64,96},{96,128},{128,160},{160,192},{192,224},{1,3... | collective-permute-start | bytes 1572872 | tf_op jit(solution)/shard_map/ppermute | solution.py:19
  105.7 9.0 %collective-permute-done = bf16[16,128,128]{2,1,0:T(8,128)(2,1)} collective-permute-done((bf16[16,128,128]{2,1,0:T(8,128)(2,1)}, bf16[16,128,128]{2,1,0:T(8,128)(2,1)}, u32[]{:S(2)}, u32[]{:S(2)}) %collective-permute-start) | collective-permute-done | bytes 524320 | tf_op jit(solution)/shard_map/ppermute | solution.py:19
  114.8 2.6 pad_maximum_fusion
  117.4 3.0 collective-permute-done.1
  122.7 16.3 %all-to-all-done.1 = bf16[128,32,256]{0,2,1:T(8,128)(2,1)S(1)} async-done(((bf16[128,32,256]{0,2,1:T(8,128)(2,1)}), bf16[128,32,256]{0,2,1:T(8,128)(2,1)S(1)}, u32[]{:S(2)}, u32[]{:S(2)}) %all-to-all-start.1) | async-done | bytes 2097184 | tf_op jit(solution)/shard_map/all_to_all | solution.py:49
  139.0 2.9 copy.135
  141.9 2.9 copy.142
  148.1 3.2 fusion.48
  151.3 34.6 %while.30 = (s32[]{:T(128)}, f32[32,128,2]{1,2,0:T(2,128)S(1)}, f32[32,128,2]{1,2,0:T(2,128)S(1)}, f32[32,128,2,128]{1,3,2,0:T(8,128)}, s32[]{:T(128)}, /*index=...) while((s32[]{:T(128)}, f32[32,128,2]{1,2,0:T(2,128)S(1)}, ...), condition=%wide.region_7.8_spmd.clone, body=%wide.region_4.7_spmd.clone.sunk | while | flops 552616192 | bytes 69731264 | solution.py:127
  154.8 3.6 %gather_fusion = bf16[2,32,128,128]{3,2,1,0:T(8,128)(2,1)} fusion(bf16[48,128,128]{2,1,0:T(8,128)(2,1)} %get-tuple-element.554, s32[2]{0:T(128)S(1)} %shift-left_bitcast_fusion.2), kind=kCustom, calls=%fused_computation.clone.clone.1 | custom fusion | bytes 4194328 | tf_op jit(solution)/shard_map/while/body/vmap()/gather | solution.py:108
  158.3 3.8 %bitcast_reduce_fusion.2 = (f32[32,128,2]{1,2,0:T(2,128)S(1)}, f32[32,2,128,128]{3,2,1,0:T(8,128)S(1)}) fusion(pred[32,2]{1,0:T(8,128)(4,1)S(1)} %copy.174, bf16[32,128,2,128]{3,1,2,0:T(8,128)(2,1)} %get-tuple-element.555, bf16[2,32,128,128]{3,2,1,0:T(8,128)(2,1)} %gather_fusion), kind=kOutput, calls=%fused_computation.12.clone.1 | convolution fusion | flops 271572992 | bytes 8421440 | tf_op jit(solution)/shard_map/while/body/nqhd,hnkd->nqhk/dot_general | solution.py:115
  171.6 3.6 %gather_fusion = bf16[2,32,128,128]{3,2,1,0:T(8,128)(2,1)} fusion(bf16[48,128,128]{2,1,0:T(8,128)(2,1)} %get-tuple-element.554, s32[2]{0:T(128)S(1)} %shift-left_bitcast_fusion.2), kind=kCustom, calls=%fused_computation.clone.clone.1 | custom fusion | bytes 4194328 | tf_op jit(solution)/shard_map/while/body/vmap()/gather | solution.py:108
  175.2 3.8 %bitcast_reduce_fusion.2 = (f32[32,128,2]{1,2,0:T(2,128)S(1)}, f32[32,2,128,128]{3,2,1,0:T(8,128)S(1)}) fusion(pred[32,2]{1,0:T(8,128)(4,1)S(1)} %copy.174, bf16[32,128,2,128]{3,1,2,0:T(8,128)(2,1)} %get-tuple-element.555, bf16[2,32,128,128]{3,2,1,0:T(8,128)(2,1)} %gather_fusion), kind=kOutput, calls=%fused_computation.12.clone.1 | convolution fusion | flops 271572992 | bytes 8421440 | tf_op jit(solution)/shard_map/while/body/nqhd,hnkd->nqhk/dot_general | solution.py:115
  185.9 4.6 %copy.139 = f32[32,128,2,128]{1,3,0,2:T(8,128)} copy(f32[32,128,2,128]{1,3,2,0:T(8,128)} %get-tuple-element.292) | data formatting | bytes 8388608
  195.7 15.2 %while.31 = (s32[]{:T(128)}, f32[32,128,2]{1,0,2:T(8,128)S(1)}, f32[32,128,2]{1,0,2:T(8,128)S(1)}, f32[32,128,2,128]{1,3,0,2:T(8,128)}, s32[]{:T(128)}, /*index=...) while((s32[]{:T(128)}, f32[32,128,2]{1,0,2:T(8,128)S(1)}, ...), condition=%wide.region_16.17_spmd.clone, body=%wide.region_12.16_spmd.clone.sunk | while | flops 552616960 | bytes 57280468 | solution.py:152
  210.9 2.8 fusion.44
  213.7 98.9 %all_to_all.61 = bf16[32,128,256]{1,2,0:T(8,128)(2,1)S(1)} all-to-all(bf16[32,128,256]{1,2,0:T(8,128)(2,1)S(1)} %bitcast.156), channel_id=1, replica_groups=mesh['grp'=8,'uly'=32] {'uly'}, dimensions={0} | all-to-all | bytes 4194304 | tf_op jit(solution)/shard_map/all_to_all | solution.py:156
  312.6 2.9 copy.146
  (115 shorter events, 57.6 us)
Async XLA Ops:
  6.5 15.9 %copy-start.6 = (bf16[128,1024]{1,0:T(8,128)(2,1)S(1)}, bf16[128,1024]{1,0:T(8,128)(2,1)}, u32[]{:S(2)}) copy-start(bf16[128,1024]{1,0:T(8,128)(2,1)} %param.13) | copy-start | bytes 786436
  10.2 44.8 %copy-start.7 = (s32[64,6]{0,1:T(8,128)S(1)}, s32[64,6]{0,1:T(8,128)}, u32[]{:S(2)}) copy-start(s32[64,6]{0,1:T(8,128)} %param.15) | copy-start | bytes 4612
  10.2 38.4 %all-to-all-start.2 = ((bf16[128,32,128]{2,0,1:T(8,128)(2,1)}), bf16[128,32,128]{2,0,1:T(8,128)(2,1)S(1)}, u32[]{:S(2)}, u32[]{:S(2)}) async-start(bf16[128,32,128]{2,0,1:T(8,128)(2,1)} %bitcast.10), calls=%async_computation.2 | async-start | bytes 2097152 | tf_op jit(solution)/shard_map/all_to_all | solution.py:51
  48.6 31.6 %all-to-all-start = ((bf16[128,32,128]{2,0,1:T(8,128)(2,1)}), bf16[128,32,128]{2,0,1:T(8,128)(2,1)S(1)}, u32[]{:S(2)}, u32[]{:S(2)}) async-start(bf16[128,32,128]{2,0,1:T(8,128)(2,1)} %bitcast.1), calls=%async_computation | async-start | bytes 2097152 | tf_op jit(solution)/shard_map/all_to_all | solution.py:50
  55.0 135.6 %all-gather.5.cloned.1.call-start = ((), (), s32[]{:S(2)}) async-start(), calls=%async_computation.5 | async-start | bytes 3538944 | tf_op jit(solution)/shard_map/all_gather | solution.py:77
  80.3 5.7 %copy-start.5 = (bf16[128,32,128]{2,0,1:T(8,128)(2,1)}, bf16[128,32,128]{2,0,1:T(8,128)(2,1)S(1)}, u32[]{:S(2)}) copy-start(bf16[128,32,128]{2,0,1:T(8,128)(2,1)S(1)} %all-to-all-done) | copy-start | bytes 3145732
  86.0 17.4 %copy-start.8 = (s32[64,3]{0,1:T(4,128)S(1)}, s32[64,3]{0,1:T(4,128)}, u32[]{:S(2)}) copy-start(s32[64,3]{0,1:T(4,128)} %param.16) | copy-start | bytes 2308
  86.0 53.0 %all-to-all-start.1 = ((bf16[128,32,256]{0,2,1:T(8,128)(2,1)}), bf16[128,32,256]{0,2,1:T(8,128)(2,1)S(1)}, u32[]{:S(2)}, u32[]{:S(2)}) async-start(bf16[128,32,256]{0,2,1:T(8,128)(2,1)} %bitcast.157), calls=%async_computation.1 | async-start | bytes 4194304 | tf_op jit(solution)/shard_map/all_to_all | solution.py:49
  93.0 100.2 %all-gather.3.cloned.1.call-start = ((), (), s32[]{:S(2)}) async-start(), calls=%async_computation.4 | async-start | bytes 3538944 | tf_op jit(solution)/shard_map/all_gather | solution.py:76
  94.9 19.8 %collective-permute-start = (bf16[16,128,128]{2,1,0:T(8,128)(2,1)}, bf16[16,128,128]{2,1,0:T(8,128)(2,1)}, u32[]{:S(2)}, u32[]{:S(2)}) collective-permute-start(bf16[16,128,128]{2,1,0:T(8,128)(2,1)} %slice.26), channel_id=1, source_target_pairs={{0,32},{32,64},{64,96},{96,128},{128,160},{160,192},{192,224},{1,3... | collective-permute-start | bytes 1572872 | tf_op jit(solution)/shard_map/ppermute | solution.py:19
  101.3 19.1 %collective-permute-start.1 = (bf16[16,128,128]{2,1,0:T(8,128)(2,1)}, bf16[16,128,128]{2,1,0:T(8,128)(2,1)}, u32[]{:S(2)}, u32[]{:S(2)}) collective-permute-start(bf16[16,128,128]{2,1,0:T(8,128)(2,1)} %slice.27), channel_id=1, source_target_pairs={{0,32},{32,64},{64,96},{96,128},{128,160},{160,192},{192,224},{1,3... | collective-permute-start | bytes 1572872 | tf_op jit(solution)/shard_map/ppermute | solution.py:19
  162.2 2.2 copy-start
  166.3 2.0 copy-start.1
  179.0 2.2 copy-start
  183.2 2.0 copy-start.1
  190.5 5.2 %copy-start.4 = (bf16[32,128,2,128]{3,1,0,2:T(8,128)(2,1)S(1)}, bf16[32,128,2,128]{3,1,0,2:T(8,128)(2,1)}, u32[]{:S(2)}) copy-start(bf16[32,128,2,128]{3,1,0,2:T(8,128)(2,1)} %copy.142) | copy-start | bytes 6291460
  196.5 2.6 copy-start.2
  201.1 1.9 copy-start.3
  203.8 2.6 copy-start.2
  208.4 1.9 copy-start.3
Sparse Core Ops, SparseCore 0:
  82.0 31.9 all-gather.4
  115.8 32.0 all-gather.2
where the time goes:
time: 327 us; the launch traced here: 322 us
  blocking collectives  98.9 us (30%)
  waiting for transfers between devices  76.1 us (23%)
  local copies, waits for them, and re-layouts  49.6 us (15%)
  starting transfers between devices  33 us (10%)
  other arithmetic  24.4 us (7%)
  matrix products  22.3 us (7%)
  between operations  13.6 us (4%)
  loops' own time  4.37 us (1%)
    all_to_all x1, blocking collectives, shards(): lax.all_to_all(mixed, 'uly', split_axis=0, concat_axis=1, tiled=True)  98.9 us
    all_to_all x1, waiting for transfers between devices, shards(): lax.all_to_all(value_outgoing, 'uly', split_axis=1, concat_axis=0, tiled=...  24.2 us
    all_to_all x1, waiting for transfers between devices, shards(): lax.all_to_all(key_outgoing, 'uly', split_axis=1, concat_axis=0, tiled=True)  23.6 us
    all_to_all x1, waiting for transfers between devices, shards(): lax.all_to_all(queries, 'uly', split_axis=1, concat_axis=0, tiled=True)  16.3 us
    unnamed x22, local copies, waits for them, and re-layouts  16.1 us
    all_to_all x1, starting transfers between devices, shards(): lax.all_to_all(value_outgoing, 'uly', split_axis=1, concat_axis=0, tiled=...  12.2 us
    ppermute x2, waiting for transfers between devices, passed_along(): lax.ppermute(value, axis, [(source, source + steps) for source in range(i...  12 us
    while x20, local copies, waits for them, and re-layouts  9.63 us
  transfers between devices with their start and end apart: 7, of which 5 were waited for; matrix products, arithmetic and copies ran while one was open for 20% of the time, Pallas kernels for 0%

commit v1 on v0

v1 whole, which is shorter than its diff:
```python
import functools

import jax
import jax.numpy as jnp
import numpy as np
from jax import lax
from jax.experimental import pallas as pl
from jax.experimental.pallas import tpu as pltpu
from jax.sharding import Mesh, PartitionSpec as P

QUERY_HEADS = 64
KEY_VALUE_HEADS = 8
HEAD_SIZE = 128
BLOCK_TOKENS = 128
NV = 6
NS = 3
SPAN = 16

CHIPS_X, CORES, CHIPS_Z, CHIPS_Y = 4, 2, 8, 4
ALL_AXES = ("x", "c", "z", "y")
HEAD_AXES = ("c", "y")
ROW_AXES = ("x", "z")
PARTS = CORES * CHIPS_Y
GROUP = QUERY_HEADS // KEY_VALUE_HEADS
ROW = CHIPS_Y
STEPS = SPAN // ROW
WINDOW = SPAN + ROW
SLICES = CHIPS_X * CHIPS_Z
PAIR_ROWS = 2 * BLOCK_TOKENS
SLICE_ROWS = PAIR_ROWS // SLICES
PICKS = GROUP * NV
SLOTS = 1 + NS + NV
TILES = CORES * WINDOW + PICKS

NEG = -1e30
LOG2_SCALE = float(HEAD_SIZE**-0.5 * np.log2(np.e))


def attend_kernel(turns, tile_of, bias_of, q_ref, *rest):
    near = rest[: 1 + 2 * STEPS]
    vert_ref, out_ref, tiles, sem = rest[1 + 2 * STEPS :]
    head = pl.program_id(0)

    @pl.when(head == 0)
    def _():
        copies = []
        for run in range(CORES):
            first = run * WINDOW
            copies.append((near[0].at[run], tiles.at[pl.ds(first + SPAN, ROW)]))
            for step in range(STEPS):
                source = near[1 + 2 * step + run]
                at = first + SPAN - ROW * (step + 1)
                copies.append((source, tiles.at[pl.ds(at, ROW)]))
        for part in range(SLICES):
            target = tiles.at[
                pl.ds(CORES * WINDOW, PICKS), pl.ds(part * SLICE_ROWS, SLICE_ROWS)
            ]
            copies.append((vert_ref.at[part], target))
        copies = [
            pltpu.make_async_copy(source, target, sem.at[n])
            for n, (source, target) in enumerate(copies)
        ]
        for copy in copies:
            copy.start()
        for copy in copies:
            copy.wait()

    rows = lax.broadcasted_iota(jnp.int32, (BLOCK_TOKENS, BLOCK_TOKENS), 0)
    cols = lax.broadcasted_iota(jnp.int32, (BLOCK_TOKENS, BLOCK_TOKENS), 1)
    causal = rows >= cols

    def attend(block, count):
        base = (head * PARTS + block) * SLOTS
        where = [tile_of[base + slot] for slot in range(count)]
        keys = jnp.concatenate([tiles[w, :BLOCK_TOKENS, :] for w in where], axis=0)
        values = jnp.concatenate([tiles[w, BLOCK_TOKENS:, :] for w in where], axis=0)
        raw = lax.dot_general(
            q_ref[block], keys, (((1,), (1,)), ((), ())), preferred_element_type=jnp.float32
        )
        scores = [raw[:, s * BLOCK_TOKENS : (s + 1) * BLOCK_TOKENS] for s in range(count)]
        scores[0] = jnp.where(causal, scores[0], NEG)
        for slot in range(1, count):
            scores[slot] = scores[slot] + bias_of[base + slot]
        best = jnp.max(functools.reduce(jnp.maximum, scores), axis=1, keepdims=True)
        weights = [jnp.exp2((s - best) * LOG2_SCALE) for s in scores]
        total = jnp.sum(functools.reduce(jnp.add, weights), axis=1, keepdims=True)
        probs = jnp.concatenate([w.astype(jnp.bfloat16) for w in weights], axis=1)
        mixed = jnp.dot(probs, values, preferred_element_type=jnp.float32)
        out_ref[block] = (mixed * (1.0 / total)).astype(jnp.bfloat16)

    for count in range(2, SLOTS + 1, 2):

        @pl.when(turns[head] == count)
        def _():
            @pl.loop(0, CORES)
            def _(run):
                for place in range(ROW):
                    attend(run * ROW + place, count)


def attend_all(turns, tile_of, bias_of, q, near, vert):
    head_spec = pl.BlockSpec(
        (PARTS, BLOCK_TOKENS, HEAD_SIZE), lambda head, *_: (0, 0, head)
    )
    anywhere = pl.BlockSpec(memory_space=pl.ANY)
    return pl.pallas_call(
        attend_kernel,
        out_shape=jax.ShapeDtypeStruct(q.shape, jnp.bfloat16),
        grid_spec=pltpu.PrefetchScalarGridSpec(
            num_scalar_prefetch=3,
            grid=(GROUP,),
            in_specs=[head_spec] + [anywhere] * (len(near) + 1),
            out_specs=head_spec,
            scratch_shapes=[
                pltpu.VMEM((TILES, PAIR_ROWS, HEAD_SIZE), jnp.bfloat16),
                pltpu.SemaphoreType.DMA((CORES * (1 + STEPS) + SLICES,)),
            ],
        ),
        compiler_params=pltpu.CompilerParams(
            dimension_semantics=("arbitrary",), vmem_limit_bytes=40 << 20
        ),
        cost_estimate=pl.CostEstimate(
            flops=4 * 64 * 6 * 128**3, bytes_accessed=10 << 20, transcendentals=64 * 6 * 128**2
        ),
        name="attend",
    )(turns, tile_of, bias_of, q, *near, vert)


def slot_tables(vert, slash, first_blocks):
    slash_count = jnp.sum((slash >= 1).astype(jnp.int32), axis=1)
    vert_count = jnp.sum((vert >= 0).astype(jnp.int32), axis=1)
    turns = 1 + slash_count + vert_count
    turns = (turns + 1) // 2 * 2
    part = np.arange(PARTS)
    numbers = first_blocks[part // ROW] + (part % ROW)
    own = jnp.asarray(part // ROW * WINDOW + SPAN + part % ROW, jnp.int32)
    near_tile = own[None, :, None] - jnp.maximum(slash, 0)[:, None, :]
    near_ok = (slash[:, None, :] >= 1) & (numbers[None, :, None] >= slash[:, None, :])
    far_tile = CORES * WINDOW + np.arange(PICKS, dtype=np.int32).reshape(GROUP, 1, NV)
    far_tile = jnp.broadcast_to(far_tile, (GROUP, PARTS, NV))
    hit = jnp.any(
        near_ok[:, :, :, None]
        & (
            numbers[None, :, None, None] - slash[:, None, :, None]
            == vert[:, None, None, :]
        ),
        axis=2,
    )
    far_ok = (
        (vert[:, None, :] >= 0)
        & (vert[:, None, :] < numbers[None, :, None])
        & jnp.logical_not(hit)
    )
    own_tile = jnp.broadcast_to(own[None, :, None], (GROUP, PARTS, 1))
    tile = jnp.concatenate([own_tile, near_tile, far_tile], axis=2)
    fine = jnp.concatenate([jnp.ones((GROUP, PARTS, 1), bool), near_ok, far_ok], axis=2)
    slot = np.arange(SLOTS)
    listed = jnp.concatenate(
        [jnp.ones((GROUP, 1), bool), slash >= 1, vert >= 0], axis=1
    )
    place = jnp.cumsum(listed.astype(jnp.int32), axis=1) - 1
    chosen = listed[:, :, None] & (place[:, :, None] == slot[None, None, :])
    chosen = chosen[:, None, :, :]
    tile_of = jnp.sum(jnp.where(chosen, tile[:, :, :, None], 0), axis=2)
    good = jnp.any(chosen & fine[:, :, :, None], axis=2)
    bias_of = jnp.where(good, 0.0, NEG).astype(jnp.float32)
    return turns, tile_of.reshape(-1), bias_of.reshape(-1)


def shards(queries, key_state_rows, value_state_rows, vert_blocks, slash_offsets):
    x, z = lax.axis_index("x"), lax.axis_index("z")
    key_head = lax.axis_index("c") * CHIPS_Y + lax.axis_index("y")
    tokens = BLOCK_TOKENS

    def by_head(rows, width):
        return rows.reshape(tokens, KEY_VALUE_HEADS, width).transpose(1, 0, 2)

    pairs = jnp.concatenate(
        [by_head(key_state_rows, HEAD_SIZE), by_head(value_state_rows, HEAD_SIZE)], axis=1
    )
    pairs = lax.all_to_all(pairs, HEAD_AXES, 0, 0, tiled=True)
    own = pairs.reshape(CORES, ROW, PAIR_ROWS, HEAD_SIZE)

    last = z == CHIPS_Z - 1
    on = [(n, n + 1) for n in range(SLICES - 1)]
    around = [
        (a * CHIPS_Z + b, a * CHIPS_Z + (b + 1) % CHIPS_Z)
        for a in range(CHIPS_X)
        for b in range(CHIPS_Z)
    ]
    near = [own]
    even, odd = own[0], own[1]
    for _ in range(STEPS):
        to_even = jnp.where(last, odd, even)
        to_odd = jnp.where(last, even, odd)
        even = lax.ppermute(to_even, ROW_AXES, on)
        odd = lax.ppermute(to_odd, ROW_AXES, around)
        near += [even, odd]

    sliced = pairs.reshape(PARTS, SLICES, SLICE_ROWS, HEAD_SIZE).transpose(1, 0, 2, 3)
    sliced = lax.all_to_all(sliced, ROW_AXES, 0, 0, tiled=True)
    vert = lax.dynamic_slice_in_dim(vert_blocks, key_head * GROUP, GROUP, 0)
    slash = lax.dynamic_slice_in_dim(slash_offsets, key_head * GROUP, GROUP, 0)
    listed = jnp.maximum(vert, 0).reshape(-1)
    place, at_z, at_run = listed % ROW, listed // ROW % CHIPS_Z, listed // (ROW * CHIPS_Z)
    at = (at_run // CORES * CHIPS_Z + at_z) * PARTS + at_run % CORES * ROW + place
    picked = sliced.reshape(SLICES * PARTS, SLICE_ROWS, HEAD_SIZE)[at]
    far = lax.all_gather(picked, ROW_AXES, axis=0, tiled=False)

    q = lax.all_to_all(by_head(queries, GROUP * HEAD_SIZE), HEAD_AXES, 0, 0, tiled=True)

    runs = jnp.arange(CORES, dtype=jnp.int32)
    first_blocks = ((x * CORES + runs) * CHIPS_Z + z) * ROW
    turns, tile_of, bias_of = slot_tables(vert, slash, first_blocks)
    mixed = attend_all(turns, tile_of, bias_of, q, near, far)

    returned = lax.all_to_all(mixed, HEAD_AXES, 0, 0, tiled=True)
    return returned.transpose(1, 0, 2).reshape(tokens, QUERY_HEADS * HEAD_SIZE)


def solution(mesh):
    split = Mesh(mesh.devices.reshape(CHIPS_X, CORES, CHIPS_Z, CHIPS_Y), ALL_AXES)
    rows = P(ALL_AXES, None)
    return jax.shard_map(
        shards,
        mesh=split,
        in_specs=(rows, rows, rows, P(), P()),
        out_specs=rows,
        check_vma=False,
    )
```

time: 327 us -> 221 us (0.68); the launches traced: 322 us -> 221 us
  blocking collectives: 98.9 us -> 49.8 us
  Pallas kernels: 0 us -> 27.1 us
  local copies, waits for them, and re-layouts: 49.6 us -> 23 us
  matrix products: 22.3 us -> 0 us
  other arithmetic: 24.4 us -> 4.06 us
  loops' own time: 4.37 us -> 0 us
  starting transfers between devices: 33 us -> 28.8 us
    all_to_all x3 -> x2, waiting for transfers between devices: 64.1 us -> 13.8 us  [the longest x1 13.8 us: shards(): sliced = lax.all_to_all(sliced, ROW_AXES, 0, 0, tiled=True)]
    all_to_all x1 -> x2, blocking collectives: 98.9 us -> 49.8 us  [the longest x1 34.7 us: shards(): returned = lax.all_to_all(mixed, HEAD_AXES, 0, 0, tiled=True)]
    ppermute x2 -> x8, waiting for transfers between devices: 12 us -> 60.6 us  [the longest x4 40 us: shards(): odd = lax.ppermute(to_odd, ROW_AXES, around)]
    pallas_call x0 -> x1, Pallas kernels: none -> 27.1 us  [attend_all(): pl.pallas_call(attend_kernel, out_shape=jax.ShapeDtypeStruct(q.shape, jnp...]
    dot_general x10 -> x0, matrix products: 22.3 us -> none  [the longest x2 7.65 us: slash_slot(): jnp.einsum('nqhd,hnkd->nqhk', q_tiles, k_near, preferred_element_type=jnp...]
    gather x10 -> x2, local copies, waits for them, and re-layouts: 17.6 us -> 1.87 us  [the longest x1 1.23 us: shards(): picked = sliced.reshape(SLICES * PARTS, SLICE_ROWS, HEAD_SIZE)[at]]
    reduce_sum x9 -> x3, other arithmetic: 12.6 us -> 0.19 us  [the longest x1 0.15 us: slot_tables(): tile_of = jnp.sum(jnp.where(chosen, tile[:, :, :, None], 0), axis=2)]
    while x21 -> x0, local copies, waits for them, and re-layouts: 9.65 us -> none
  transfers between devices with their start and end apart: 7 -> 11, of which waited for: 5 -> 9; matrix products, arithmetic and copies ran while one was open for 20% -> 5% of each run, Pallas kernels for 0% -> 0%
where the time goes in v1:
time: 221 us
  waiting for transfers between devices  74.4 us (34%)
  blocking collectives  49.8 us (23%)
  starting transfers between devices  28.8 us (13%)
  Pallas kernels  27.1 us (12%)
  local copies, waits for them, and re-layouts  23 us (10%)
  between operations  13.7 us (6%)
  other arithmetic  4.06 us (2%)
    ppermute x4, waiting for transfers between devices, shards(): odd = lax.ppermute(to_odd, ROW_AXES, around)  40 us
    all_to_all x1, blocking collectives, shards(): returned = lax.all_to_all(mixed, HEAD_AXES, 0, 0, tiled=True)  34.7 us
    pallas_call x1, Pallas kernels, attend_all(): pl.pallas_call(attend_kernel, out_shape=jax.ShapeDtypeStruct(q.shape, jnp...  27.1 us
    ppermute x4, waiting for transfers between devices, shards(): even = lax.ppermute(to_even, ROW_AXES, on)  20.6 us
    all_to_all x1, blocking collectives, shards(): pairs = lax.all_to_all(pairs, HEAD_AXES, 0, 0, tiled=True)  15.1 us
    all_to_all x1, waiting for transfers between devices, shards(): sliced = lax.all_to_all(sliced, ROW_AXES, 0, 0, tiled=True)  13.8 us
    all_to_all x1, starting transfers between devices, shards(): sliced = lax.all_to_all(sliced, ROW_AXES, 0, 0, tiled=True)  11 us
    ppermute x4, starting transfers between devices, shards(): even = lax.ppermute(to_even, ROW_AXES, on)  9.99 us
  transfers between devices with their start and end apart: 11, of which 9 were waited for; matrix products, arithmetic and copies ran while one was open for 5% of the time, Pallas kernels for 0%

profile of v1, /device:TPU:1, one launch (start us, length us, event | category | flops | bytes accessed | tf_op | source)
XLA Modules:
  0.0 220.9 jit_solution(1316735525151322033)
XLA Ops:
  9.2 15.1 %all_to_all.20 = bf16[8,256,128]{2,1,0:T(8,128)(2,1)S(1)} all-to-all(bf16[8,256,128]{2,1,0:T(8,128)(2,1)S(1)} %pad_maximum_fusion), channel_id=1, replica_groups=mesh['x'=4,'c'=2,'z'=8,'y'=4] {'c','y'}, dimensions={0} | all-to-all | bytes 1048576 | tf_op jit(solution)/shard_map/all_to_all | solution.py:181
  25.3 11.0 %all-to-all-start.2 = ((bf16[32,8,8,128]{3,2,1,0:T(8,128)(2,1)}), bf16[32,8,8,128]{3,2,1,0:T(8,128)(2,1)S(1)}, u32[]{:S(2)}, u32[]{:S(2)}) async-start(bf16[32,8,8,128]{3,2,1,0:T(8,128)(2,1)} %copy_bitcast_fusion), calls=%async_computation.2 | async-start | bytes 1048576 | tf_op jit(solution)/shard_map/all_to_all | solution.py:201
  36.7 13.8 %all-to-all-done.2 = bf16[32,8,8,128]{3,2,1,0:T(8,128)(2,1)S(1)} async-done(((bf16[32,8,8,128]{3,2,1,0:T(8,128)(2,1)}), bf16[32,8,8,128]{3,2,1,0:T(8,128)(2,1)S(1)}, u32[]{:S(2)}, u32[]{:S(2)}) %all-to-all-start.2) | async-done | bytes 524320 | tf_op jit(solution)/shard_map/all_to_all | solution.py:201
  50.5 1.2 gather_fusion.1
  51.7 3.2 %copy.61 = bf16[128,8192]{0,1:T(8,128)(2,1)S(1)} copy(bf16[128,8192]{1,0:T(8,128)(2,1)} %param.11) | data formatting | bytes 4194304 | tf_op args[0]
  54.9 2.6 %copy.62 = bf16[128,8,1024]{2,0,1:T(8,128)(2,1)} copy(bf16[128,8,1024]{0,2,1:T(8,128)(2,1)S(1)} %bitcast.25) | data formatting | bytes 4194304 | tf_op jit(solution)/shard_map/reshape | solution.py:176
  57.5 7.2 %all-to-all-start = ((bf16[8,128,1024]{2,1,0:T(8,128)(2,1)}), bf16[8,128,1024]{2,1,0:T(8,128)(2,1)S(1)}, u32[]{:S(2)}, u32[]{:S(2)}) async-start(bf16[8,128,1024]{2,1,0:T(8,128)(2,1)} %bitcast.22), calls=%async_computation | async-start | bytes 4194304 | tf_op jit(solution)/shard_map/all_to_all | solution.py:210
  66.3 4.4 %collective-permute-start = (bf16[4,256,128]{2,1,0:T(8,128)(2,1)S(1)}, bf16[4,256,128]{2,1,0:T(8,128)(2,1)S(1)}, u32[]{:S(2)}, u32[]{:S(2)}) collective-permute-start(bf16[4,256,128]{2,1,0:T(8,128)(2,1)S(1)} %get-tuple-element.20), channel_id=1, source_target_pairs={{0,4},{4,8},{8,12},{12,16},{16,20},{20,24},{24,28},{28,64},{64,68}... | collective-permute-start | bytes 786440 | tf_op jit(solution)/shard_map/ppermute | solution.py:196
  70.9 6.1 %collective-permute-done.rest_1_ = bf16[4,256,128]{2,1,0:T(8,128)(2,1)S(1)} collective-permute-done((bf16[4,256,128]{2,1,0:T(8,128)(2,1)S(1)}, bf16[4,256,128]{2,1,0:T(8,128)(2,1)S(1)}, u32[]{:S(2)}, u32[]{:S(2)}) %collective-permute-start) | collective-permute-done | bytes 262176 | tf_op jit(solution)/shard_map/ppermute | solution.py:196
  77.1 8.5 %collective-permute-done.1.rest_2_ = bf16[4,256,128]{2,1,0:T(8,128)(2,1)S(1)} collective-permute-done((bf16[4,256,128]{2,1,0:T(8,128)(2,1)S(1)}, bf16[4,256,128]{2,1,0:T(8,128)(2,1)S(1)}, u32[]{:S(2)}, u32[]{:S(2)}) %collective-permute-start.1) | collective-permute-done | bytes 262176 | tf_op jit(solution)/shard_map/ppermute | solution.py:197
  86.4 2.3 %collective-permute-start.2 = (bf16[4,256,128]{2,1,0:T(8,128)(2,1)}, bf16[4,256,128]{2,1,0:T(8,128)(2,1)S(1)}, u32[]{:S(2)}, u32[]{:S(2)}) collective-permute-start(bf16[4,256,128]{2,1,0:T(8,128)(2,1)} %get-tuple-element.18), channel_id=1, source_target_pairs={{0,4},{4,8},{8,12},{12,16},{16,20},{20,24},{24,28},{28,64},{64,68}... | collective-permute-start | bytes 786440 | tf_op jit(solution)/shard_map/ppermute | solution.py:196
  89.2 4.4 %collective-permute-done.2.rest_3_ = bf16[4,256,128]{2,1,0:T(8,128)(2,1)S(1)} collective-permute-done((bf16[4,256,128]{2,1,0:T(8,128)(2,1)}, bf16[4,256,128]{2,1,0:T(8,128)(2,1)S(1)}, u32[]{:S(2)}, u32[]{:S(2)}) %collective-permute-start.2) | collective-permute-done | bytes 262176 | tf_op jit(solution)/shard_map/ppermute | solution.py:196
  93.6 8.6 %collective-permute-done.3.rest_4_ = bf16[4,256,128]{2,1,0:T(8,128)(2,1)} collective-permute-done((bf16[4,256,128]{2,1,0:T(8,128)(2,1)}, bf16[4,256,128]{2,1,0:T(8,128)(2,1)}, u32[]{:S(2)}, u32[]{:S(2)}) %collective-permute-start.3) | collective-permute-done | bytes 262176 | tf_op jit(solution)/shard_map/ppermute | solution.py:197
  103.2 1.3 collective-permute-start.4
  104.9 7.6 %collective-permute-done.4.rest_5_ = bf16[4,256,128]{2,1,0:T(8,128)(2,1)S(1)} collective-permute-done((bf16[4,256,128]{2,1,0:T(8,128)(2,1)S(1)}, bf16[4,256,128]{2,1,0:T(8,128)(2,1)S(1)}, u32[]{:S(2)}, u32[]{:S(2)}) %collective-permute-start.4) | collective-permute-done | bytes 262176 | tf_op jit(solution)/shard_map/ppermute | solution.py:196
  112.5 16.8 %collective-permute-done.5.rest_6_ = bf16[4,256,128]{2,1,0:T(8,128)(2,1)S(1)} collective-permute-done((bf16[4,256,128]{2,1,0:T(8,128)(2,1)S(1)}, bf16[4,256,128]{2,1,0:T(8,128)(2,1)S(1)}, u32[]{:S(2)}, u32[]{:S(2)}) %collective-permute-start.5) | collective-permute-done | bytes 262176 | tf_op jit(solution)/shard_map/ppermute | solution.py:197
  131.0 2.0 collective-permute-start.6
  133.4 2.5 %collective-permute-done.6.rest_7_ = bf16[4,256,128]{2,1,0:T(8,128)(2,1)} collective-permute-done((bf16[4,256,128]{2,1,0:T(8,128)(2,1)}, bf16[4,256,128]{2,1,0:T(8,128)(2,1)}, u32[]{:S(2)}, u32[]{:S(2)}) %collective-permute-start.6) | collective-permute-done | bytes 262176 | tf_op jit(solution)/shard_map/ppermute | solution.py:196
  135.9 6.1 %collective-permute-done.7.rest_8_ = bf16[4,256,128]{2,1,0:T(8,128)(2,1)} collective-permute-done((bf16[4,256,128]{2,1,0:T(8,128)(2,1)}, bf16[4,256,128]{2,1,0:T(8,128)(2,1)}, u32[]{:S(2)}, u32[]{:S(2)}) %collective-permute-start.7) | collective-permute-done | bytes 262176 | tf_op jit(solution)/shard_map/ppermute | solution.py:197
  143.9 1.9 copy-done.4
  145.8 27.1 %attend.1 = bf16[8,128,1024]{2,1,0:T(8,128)(2,1)S(1)} custom-call(s32[8]{0:T(128)S(1)} %fusion.7.turns, s32[640]{0:T(1024)S(1)} %reshape.338.tile_of, f32[640]{0:T(1024)S(1)} %select_n.143.bias_of, bf16[8,128,1024]{2,1,0:T(8,128)(2,1)S(1)} %all-to-all-done.q_ref, bf16[2,4,256,128]{3,2,1,0:T(8,128)(2,1)S(1)} %bitcast.20, ...), custom_call_target="tpu_custom_call" | custom-call | flops 3221225472 | bytes 10485760 | tf_op jit(solution)/shard_map/attend/pallas_call | solution.py:106
  172.9 34.7 %all_to_all.21 = bf16[8,128,1024]{2,1,0:T(8,128)(2,1)S(1)} all-to-all(bf16[8,128,1024]{2,1,0:T(8,128)(2,1)S(1)} %attend.1), channel_id=1, replica_groups=mesh['x'=4,'c'=2,'z'=8,'y'=4] {'c','y'}, dimensions={0} | all-to-all | bytes 4194304 | tf_op jit(solution)/shard_map/all_to_all | solution.py:217
  207.6 2.4 %copy.69 = bf16[128,8,1024]{0,2,1:T(8,128)(2,1)} copy(bf16[128,8,1024]{2,0,1:T(8,128)(2,1)S(1)} %bitcast.23) | data formatting | bytes 4194304 | tf_op jit(solution)/shard_map/transpose | solution.py:218
  210.0 4.1 %copy.70 = bf16[128,8192]{1,0:T(8,128)(2,1)} copy(bf16[128,8192]{0,1:T(8,128)(2,1)} %bitcast.24) | data formatting | bytes 4194304 | tf_op jit(solution)/shard_map/reshape | solution.py:218
  (75 shorter events, 12.2 us)
Async XLA Ops:
  9.2 27.2 %copy-start.5 = (s32[64,6]{0,1:T(8,128)S(1)}, s32[64,6]{0,1:T(8,128)}, u32[]{:S(2)}) copy-start(s32[64,6]{0,1:T(8,128)} %param.14) | copy-start | bytes 4612
  25.3 25.2 %all-to-all-start.2 = ((bf16[32,8,8,128]{3,2,1,0:T(8,128)(2,1)}), bf16[32,8,8,128]{3,2,1,0:T(8,128)(2,1)S(1)}, u32[]{:S(2)}, u32[]{:S(2)}) async-start(bf16[32,8,8,128]{3,2,1,0:T(8,128)(2,1)} %copy_bitcast_fusion), calls=%async_computation.2 | async-start | bytes 1048576 | tf_op jit(solution)/shard_map/all_to_all | solution.py:201
  36.3 105.7 %all-gather.3.cloned.1.call-start = ((), (), s32[]{:S(2)}) async-start(), calls=%async_computation.4 | async-start | bytes 3244032 | tf_op jit(solution)/shard_map/all_gather | solution.py:208
  57.5 7.3 %copy-start.7 = (s32[64,3]{0,1:T(4,128)S(1)}, s32[64,3]{0,1:T(4,128)}, u32[]{:S(2)}) copy-start(s32[64,3]{0,1:T(4,128)} %param.15) | copy-start | bytes 2308
  57.5 7.7 %copy-start.9 = (s32[8]{0:T(128)S(1)}, s32[8]{0:T(128)}, u32[]{:S(2)}) copy-start(s32[8]{0:T(128)} %constant.151) | copy-start | bytes 100
  57.5 8.3 %copy-start.10 = (s32[8]{0:T(128)S(1)}, s32[8]{0:T(128)}, u32[]{:S(2)}) copy-start(s32[8]{0:T(128)} %constant.141.clone) | copy-start | bytes 100
  57.5 84.5 %all-to-all-start = ((bf16[8,128,1024]{2,1,0:T(8,128)(2,1)}), bf16[8,128,1024]{2,1,0:T(8,128)(2,1)S(1)}, u32[]{:S(2)}, u32[]{:S(2)}) async-start(bf16[8,128,1024]{2,1,0:T(8,128)(2,1)} %bitcast.22), calls=%async_computation | async-start | bytes 4194304 | tf_op jit(solution)/shard_map/all_to_all | solution.py:210
  64.8 24.4 %copy-start.8 = (s32[8]{0:T(128)S(1)}, s32[8]{0:T(128)}, u32[]{:S(2)}) copy-start(s32[8]{0:T(128)} %constant.142.clone) | copy-start | bytes 100
  64.8 40.0 %copy-start.6 = (s32[8,6]{1,0:T(8,128)S(1)}, s32[8,6]{1,0:T(8,128)}, u32[]{:S(2)}) copy-start(s32[8,6]{1,0:T(8,128)} %constant.149) | copy-start | bytes 580
  66.3 10.8 %collective-permute-start = (bf16[4,256,128]{2,1,0:T(8,128)(2,1)S(1)}, bf16[4,256,128]{2,1,0:T(8,128)(2,1)S(1)}, u32[]{:S(2)}, u32[]{:S(2)}) collective-permute-start(bf16[4,256,128]{2,1,0:T(8,128)(2,1)S(1)} %get-tuple-element.20), channel_id=1, source_target_pairs={{0,4},{4,8},{8,12},{12,16},{16,20},{20,24},{24,28},{28,64},{64,68}... | collective-permute-start | bytes 786440 | tf_op jit(solution)/shard_map/ppermute | solution.py:196
  70.7 14.9 %collective-permute-start.1 = (bf16[4,256,128]{2,1,0:T(8,128)(2,1)S(1)}, bf16[4,256,128]{2,1,0:T(8,128)(2,1)S(1)}, u32[]{:S(2)}, u32[]{:S(2)}) collective-permute-start(bf16[4,256,128]{2,1,0:T(8,128)(2,1)S(1)} %get-tuple-element.19), channel_id=1, source_target_pairs={{0,4},{4,8},{8,12},{12,16},{16,20},{20,24},{24,28},{28,0},{64,68},... | collective-permute-start | bytes 786440 | tf_op jit(solution)/shard_map/ppermute | solution.py:197
  86.4 7.2 %collective-permute-start.2 = (bf16[4,256,128]{2,1,0:T(8,128)(2,1)}, bf16[4,256,128]{2,1,0:T(8,128)(2,1)S(1)}, u32[]{:S(2)}, u32[]{:S(2)}) collective-permute-start(bf16[4,256,128]{2,1,0:T(8,128)(2,1)} %get-tuple-element.18), channel_id=1, source_target_pairs={{0,4},{4,8},{8,12},{12,16},{16,20},{20,24},{24,28},{28,64},{64,68}... | collective-permute-start | bytes 786440 | tf_op jit(solution)/shard_map/ppermute | solution.py:196
  88.7 13.5 %collective-permute-start.3 = (bf16[4,256,128]{2,1,0:T(8,128)(2,1)}, bf16[4,256,128]{2,1,0:T(8,128)(2,1)}, u32[]{:S(2)}, u32[]{:S(2)}) collective-permute-start(bf16[4,256,128]{2,1,0:T(8,128)(2,1)} %get-tuple-element.17), channel_id=1, source_target_pairs={{0,4},{4,8},{8,12},{12,16},{16,20},{20,24},{24,28},{28,0},{64,68},... | collective-permute-start | bytes 786440 | tf_op jit(solution)/shard_map/ppermute | solution.py:197
  103.2 9.3 %collective-permute-start.4 = (bf16[4,256,128]{2,1,0:T(8,128)(2,1)S(1)}, bf16[4,256,128]{2,1,0:T(8,128)(2,1)S(1)}, u32[]{:S(2)}, u32[]{:S(2)}) collective-permute-start(bf16[4,256,128]{2,1,0:T(8,128)(2,1)S(1)} %get-tuple-element.16), channel_id=1, source_target_pairs={{0,4},{4,8},{8,12},{12,16},{16,20},{20,24},{24,28},{28,64},{64,68}... | collective-permute-start | bytes 786440 | tf_op jit(solution)/shard_map/ppermute | solution.py:196
  104.5 24.9 %collective-permute-start.5 = (bf16[4,256,128]{2,1,0:T(8,128)(2,1)S(1)}, bf16[4,256,128]{2,1,0:T(8,128)(2,1)S(1)}, u32[]{:S(2)}, u32[]{:S(2)}) collective-permute-start(bf16[4,256,128]{2,1,0:T(8,128)(2,1)S(1)} %get-tuple-element.15), channel_id=1, source_target_pairs={{0,4},{4,8},{8,12},{12,16},{16,20},{20,24},{24,28},{28,0},{64,68},... | collective-permute-start | bytes 786440 | tf_op jit(solution)/shard_map/ppermute | solution.py:197
  129.4 0.9 copy-start.2
  130.3 0.7 copy-start
  131.0 4.9 %collective-permute-start.6 = (bf16[4,256,128]{2,1,0:T(8,128)(2,1)}, bf16[4,256,128]{2,1,0:T(8,128)(2,1)}, u32[]{:S(2)}, u32[]{:S(2)}) collective-permute-start(bf16[4,256,128]{2,1,0:T(8,128)(2,1)} %get-tuple-element.14), channel_id=1, source_target_pairs={{0,4},{4,8},{8,12},{12,16},{16,20},{20,24},{24,28},{28,64},{64,68}... | collective-permute-start | bytes 786440 | tf_op jit(solution)/shard_map/ppermute | solution.py:196
  133.0 9.0 %collective-permute-start.7 = (bf16[4,256,128]{2,1,0:T(8,128)(2,1)}, bf16[4,256,128]{2,1,0:T(8,128)(2,1)}, u32[]{:S(2)}, u32[]{:S(2)}) collective-permute-start(bf16[4,256,128]{2,1,0:T(8,128)(2,1)} %get-tuple-element.13), channel_id=1, source_target_pairs={{0,4},{4,8},{8,12},{12,16},{16,20},{20,24},{24,28},{28,0},{64,68},... | collective-permute-start | bytes 786440 | tf_op jit(solution)/shard_map/ppermute | solution.py:197
  142.0 1.0 copy-start.1
  143.0 0.9 copy-start.3
  143.9 1.9 copy-start.4
Sparse Core Ops, SparseCore 0:
  51.8 80.9 all-gather.2

commit v2 on v1

--- a/solution.py
+++ b/solution.py
@@ -31,14 +31,18 @@
 PICKS = GROUP * NV
 SLOTS = 1 + NS + NV
 TILES = CORES * WINDOW + PICKS
+HALF = CHIPS_Z // 2
+FAR_X = (0, 1, -1, 2, 2)
+FAR_Z = (0, 0, 0, 0, HALF)
 
 NEG = -1e30
 LOG2_SCALE = float(HEAD_SIZE**-0.5 * np.log2(np.e))
 
 
-def attend_kernel(turns, tile_of, bias_of, q_ref, *rest):
+def attend_kernel(turns, tile_of, bias_of, spot, q_ref, *rest):
     near = rest[: 1 + 2 * STEPS]
-    vert_ref, out_ref, tiles, sem = rest[1 + 2 * STEPS :]
+    far = rest[1 + 2 * STEPS : -3]
+    out_ref, tiles, sem = rest[-3:]
     head = pl.program_id(0)
 
     @pl.when(head == 0)
@@ -51,11 +55,14 @@
                 source = near[1 + 2 * step + run]
                 at = first + SPAN - ROW * (step + 1)
                 copies.append((source, tiles.at[pl.ds(at, ROW)]))
-        for part in range(SLICES):
-            target = tiles.at[
-                pl.ds(CORES * WINDOW, PICKS), pl.ds(part * SLICE_ROWS, SLICE_ROWS)
-            ]
-            copies.append((vert_ref.at[part], target))
+        x, z = spot[0], spot[1]
+        for ref, x_back, z_back in zip(far, FAR_X, FAR_Z):
+            for n in range(ref.shape[0]):
+                at_x = (x - x_back + CHIPS_X) % CHIPS_X
+                at_z = (z - z_back - n + CHIPS_Z) % CHIPS_Z
+                first = pl.multiple_of((at_x * CHIPS_Z + at_z) * SLICE_ROWS, SLICE_ROWS)
+                target = tiles.at[pl.ds(CORES * WINDOW, PICKS), pl.ds(first, SLICE_ROWS)]
+                copies.append((ref.at[n], target))
         copies = [
             pltpu.make_async_copy(source, target, sem.at[n])
             for n, (source, target) in enumerate(copies)
@@ -98,7 +105,7 @@
                     attend(run * ROW + place, count)
 
 
-def attend_all(turns, tile_of, bias_of, q, near, vert):
+def attend_all(turns, tile_of, bias_of, spot, q, near, far):
     head_spec = pl.BlockSpec(
         (PARTS, BLOCK_TOKENS, HEAD_SIZE), lambda head, *_: (0, 0, head)
     )
@@ -107,9 +114,9 @@
         attend_kernel,
         out_shape=jax.ShapeDtypeStruct(q.shape, jnp.bfloat16),
         grid_spec=pltpu.PrefetchScalarGridSpec(
-            num_scalar_prefetch=3,
+            num_scalar_prefetch=4,
             grid=(GROUP,),
-            in_specs=[head_spec] + [anywhere] * (len(near) + 1),
+            in_specs=[head_spec] + [anywhere] * (len(near) + len(far)),
             out_specs=head_spec,
             scratch_shapes=[
                 pltpu.VMEM((TILES, PAIR_ROWS, HEAD_SIZE), jnp.bfloat16),
@@ -123,10 +130,58 @@
             flops=4 * 64 * 6 * 128**3, bytes_accessed=10 << 20, transcendentals=64 * 6 * 128**2
         ),
         name="attend",
-    )(turns, tile_of, bias_of, q, *near, vert)
-
-
-def slot_tables(vert, slash, first_blocks):
+    )(turns, tile_of, bias_of, spot, q, *near, *far)
+
+
+def split_pairs_kernel(key_ref, value_ref, out_ref):
+    for head in range(KEY_VALUE_HEADS):
+        columns = slice(head * HEAD_SIZE, (head + 1) * HEAD_SIZE)
+        out_ref[head, :BLOCK_TOKENS, :] = key_ref[:, columns]
+        out_ref[head, BLOCK_TOKENS:, :] = value_ref[:, columns]
+
+
+def split_pairs(keys, values):
+    return pl.pallas_call(
+        split_pairs_kernel,
+        out_shape=jax.ShapeDtypeStruct(
+            (KEY_VALUE_HEADS, PAIR_ROWS, HEAD_SIZE), jnp.bfloat16
+        ),
+        cost_estimate=pl.CostEstimate(flops=0, bytes_accessed=1 << 20, transcendentals=0),
+        name="split_pairs",
+    )(keys, values)
+
+
+def move_kernel(from_ref, to_ref):
+    to_ref[...] = from_ref[...]
+
+
+def split_heads(rows):
+    width = rows.shape[1] // PARTS
+    return pl.pallas_call(
+        move_kernel,
+        out_shape=jax.ShapeDtypeStruct((PARTS, BLOCK_TOKENS, width), rows.dtype),
+        grid=(PARTS,),
+        in_specs=[pl.BlockSpec((BLOCK_TOKENS, width), lambda n: (0, n))],
+        out_specs=pl.BlockSpec((None, BLOCK_TOKENS, width), lambda n: (n, 0, 0)),
+        cost_estimate=pl.CostEstimate(flops=0, bytes_accessed=4 << 20, transcendentals=0),
+        name="split_heads",
+    )(rows)
+
+
+def merge_heads(parts):
+    width = parts.shape[2]
+    return pl.pallas_call(
+        move_kernel,
+        out_shape=jax.ShapeDtypeStruct((BLOCK_TOKENS, PARTS * width), parts.dtype),
+        grid=(PARTS,),
+        in_specs=[pl.BlockSpec((None, BLOCK_TOKENS, width), lambda n: (n, 0, 0))],
+        out_specs=pl.BlockSpec((BLOCK_TOKENS, width), lambda n: (0, n)),
+        cost_estimate=pl.CostEstimate(flops=0, bytes_accessed=4 << 20, transcendentals=0),
+        name="merge_heads",
+    )(parts)
+
+
+def slot_tables(vert, slash, first_blocks, z):
     slash_count = jnp.sum((slash >= 1).astype(jnp.int32), axis=1)
     vert_count = jnp.sum((vert >= 0).astype(jnp.int32), axis=1)
     turns = 1 + slash_count + vert_count
@@ -134,7 +189,12 @@
     part = np.arange(PARTS)
     numbers = first_blocks[part // ROW] + (part % ROW)
     own = jnp.asarray(part // ROW * WINDOW + SPAN + part % ROW, jnp.int32)
-    near_tile = own[None, :, None] - jnp.maximum(slash, 0)[:, None, :]
+    inside = jnp.asarray(SPAN + part % ROW, jnp.int32)[None, :, None]
+    inside = inside - jnp.maximum(slash, 0)[:, None, :]
+    back = STEPS - inside // ROW
+    run = jnp.asarray(part // ROW, jnp.int32)[None, :, None]
+    held_in = jnp.where(z < back, CORES - 1 - run, run)
+    near_tile = held_in * WINDOW + inside
     near_ok = (slash[:, None, :] >= 1) & (numbers[None, :, None] >= slash[:, None, :])
     far_tile = CORES * WINDOW + np.arange(PICKS, dtype=np.int32).reshape(GROUP, 1, NV)
     far_tile = jnp.broadcast_to(far_tile, (GROUP, PARTS, NV))
@@ -170,32 +230,26 @@
 def shards(queries, key_state_rows, value_state_rows, vert_blocks, slash_offsets):
     x, z = lax.axis_index("x"), lax.axis_index("z")
     key_head = lax.axis_index("c") * CHIPS_Y + lax.axis_index("y")
-    tokens = BLOCK_TOKENS
-
-    def by_head(rows, width):
-        return rows.reshape(tokens, KEY_VALUE_HEADS, width).transpose(1, 0, 2)
-
-    pairs = jnp.concatenate(
-        [by_head(key_state_rows, HEAD_SIZE), by_head(value_state_rows, HEAD_SIZE)], axis=1
-    )
+
+    def shifted(value, axis, by):
+        count = lax.axis_size(axis)
+        return lax.ppermute(value, axis, [(n, (n + by) % count) for n in range(count)])
+
+    pairs = split_pairs(key_state_rows, value_state_rows)
     pairs = lax.all_to_all(pairs, HEAD_AXES, 0, 0, tiled=True)
     own = pairs.reshape(CORES, ROW, PAIR_ROWS, HEAD_SIZE)
 
-    last = z == CHIPS_Z - 1
-    on = [(n, n + 1) for n in range(SLICES - 1)]
-    around = [
-        (a * CHIPS_Z + b, a * CHIPS_Z + (b + 1) % CHIPS_Z)
+    onward = [
+        (a * CHIPS_Z + b, (a + (b + 1) // CHIPS_Z) % CHIPS_X * CHIPS_Z + (b + 1) % CHIPS_Z)
         for a in range(CHIPS_X)
         for b in range(CHIPS_Z)
     ]
     near = [own]
-    even, odd = own[0], own[1]
+    first, second = own[0], own[1]
     for _ in range(STEPS):
-        to_even = jnp.where(last, odd, even)
-        to_odd = jnp.where(last, even, odd)
-        even = lax.ppermute(to_even, ROW_AXES, on)
-        odd = lax.ppermute(to_odd, ROW_AXES, around)
-        near += [even, odd]
+        first = shifted(first, "z", 1)
+        second = lax.ppermute(second, ROW_AXES, onward)
+        near += [first, second]
 
     sliced = pairs.reshape(PARTS, SLICES, SLICE_ROWS, HEAD_SIZE).transpose(1, 0, 2, 3)
     sliced = lax.all_to_all(sliced, ROW_AXES, 0, 0, tiled=True)
@@ -205,17 +259,24 @@
     place, at_z, at_run = listed % ROW, listed // ROW % CHIPS_Z, listed // (ROW * CHIPS_Z)
     at = (at_run // CORES * CHIPS_Z + at_z) * PARTS + at_run % CORES * ROW + place
     picked = sliced.reshape(SLICES * PARTS, SLICE_ROWS, HEAD_SIZE)[at]
-    far = lax.all_gather(picked, ROW_AXES, axis=0, tiled=False)
-
-    q = lax.all_to_all(by_head(queries, GROUP * HEAD_SIZE), HEAD_AXES, 0, 0, tiled=True)
+
+    queries = split_heads(queries)
+    queries, picked = lax.optimization_barrier((queries, picked))
+    q = lax.all_to_all(queries, HEAD_AXES, 0, 0, tiled=True)
+
+    column = jnp.stack([picked] + [shifted(picked, "z", n) for n in range(1, CHIPS_Z)])
+    right, left = shifted(column, "x", 1), shifted(column, "x", -1)
+    far = [column, right, left]
+    far += [shifted(right[:HALF], "x", 1), shifted(left[HALF:], "x", -1)]
 
     runs = jnp.arange(CORES, dtype=jnp.int32)
     first_blocks = ((x * CORES + runs) * CHIPS_Z + z) * ROW
-    turns, tile_of, bias_of = slot_tables(vert, slash, first_blocks)
-    mixed = attend_all(turns, tile_of, bias_of, q, near, far)
+    turns, tile_of, bias_of = slot_tables(vert, slash, first_blocks, z)
+    spot = jnp.stack([x, z]).astype(jnp.int32)
+    mixed = attend_all(turns, tile_of, bias_of, spot, q, near, far)
 
     returned = lax.all_to_all(mixed, HEAD_AXES, 0, 0, tiled=True)
-    return returned.transpose(1, 0, 2).reshape(tokens, QUERY_HEADS * HEAD_SIZE)
+    return merge_heads(returned)
 
 
 def solution(mesh):

time: 221 us -> 208 us (0.941)
  blocking collectives: 49.8 us -> 31.3 us
  starting transfers between devices: 28.8 us -> 43.7 us
  Pallas kernels: 27.1 us -> 40.9 us
  between operations: 13.7 us -> 0.26 us
  local copies, waits for them, and re-layouts: 23 us -> 11.5 us
  waiting for transfers between devices: 74.4 us -> 77.5 us
  other arithmetic: 4.06 us -> 1.37 us
    all_to_all x1 -> x0, blocking collectives: 15.1 us -> none  [shards(): pairs = lax.all_to_all(pairs, HEAD_AXES, 0, 0, tiled=True)]
    pallas_call x0 -> x3, Pallas kernels: none -> 13.2 us  [the longest x1 5.64 us: split_heads(): pl.pallas_call(move_kernel, out_shape=jax.ShapeDtypeStruct((PARTS, BLOCK_...]
    ppermute x8 -> x19, starting transfers between devices: 10.5 us -> 19.7 us  [the longest x15 18.3 us: shifted(): lax.ppermute(value, axis, [(n, (n + by) % count) for n in range(count)])]
    reshape x4 -> x0, local copies, waits for them, and re-layouts: 7.03 us -> none  [the longest x1 4.06 us: shards(): return returned.transpose(1, 0, 2).reshape(tokens, QUERY_HEADS * HEAD_SIZE)]
    all_to_all x1 -> x2, starting transfers between devices: 7.24 us -> 13.6 us  [the longest x1 6.96 us: shards(): q = lax.all_to_all(queries, HEAD_AXES, 0, 0, tiled=True)]
    unnamed x25 -> x23, local copies, waits for them, and re-layouts: 9.98 us -> 4.53 us
    ppermute x8 -> x19, waiting for transfers between devices: 60.6 us -> 64.7 us  [the longest x15 47.6 us: shifted(): lax.ppermute(value, axis, [(n, (n + by) % count) for n in range(count)])]
    all_to_all x1, blocking collectives: 34.7 us -> 31.3 us  [shards(): returned = lax.all_to_all(mixed, HEAD_AXES, 0, 0, tiled=True)]
  transfers between devices with their start and end apart: 11 -> 22, of which waited for: 9 -> 13; matrix products, arithmetic and copies ran while one was open for 5% -> 6% of each run, Pallas kernels for 0% -> 3%
where the time goes in v2:
time: 208 us; the launch traced here: 207 us
  waiting for transfers between devices  77.5 us (37%)
  starting transfers between devices  43.7 us (21%)
  Pallas kernels  40.9 us (20%)
  blocking collectives  31.3 us (15%)
  local copies, waits for them, and re-layouts  11.5 us (6%)
    ppermute x15, waiting for transfers between devices, shifted(): lax.ppermute(value, axis, [(n, (n + by) % count) for n in range(count)])  47.6 us
    all_to_all x1, blocking collectives, shards(): returned = lax.all_to_all(mixed, HEAD_AXES, 0, 0, tiled=True)  31.3 us
    pallas_call x1, Pallas kernels, attend_all(): pl.pallas_call(attend_kernel, out_shape=jax.ShapeDtypeStruct(q.shape, jnp...  27.6 us
    ppermute x15, starting transfers between devices, shifted(): lax.ppermute(value, axis, [(n, (n + by) % count) for n in range(count)])  18.3 us
    ppermute x4, waiting for transfers between devices, shards(): second = lax.ppermute(second, ROW_AXES, onward)  17.1 us
    all_to_all x1, waiting for transfers between devices, shards(): sliced = lax.all_to_all(sliced, ROW_AXES, 0, 0, tiled=True)  10.5 us
    all_to_all x1, starting transfers between devices, shards(): sliced = lax.all_to_all(sliced, ROW_AXES, 0, 0, tiled=True)  10.4 us
    all_to_all x1, starting transfers between devices, shards(): q = lax.all_to_all(queries, HEAD_AXES, 0, 0, tiled=True)  6.96 us
  transfers between devices with their start and end apart: 22, of which 13 were waited for; matrix products, arithmetic and copies ran while one was open for 6% of the time, Pallas kernels for 3%

profile of v2, /device:TPU:1, one launch (start us, length us, event | category | flops | bytes accessed | tf_op | source)
XLA Modules:
  0.0 206.5 jit_solution(2975566792459148479)
XLA Ops:
  0.0 2.0 split_pairs.1
  2.0 6.7 %all-to-all-start = ((bf16[8,256,128]{2,1,0:T(8,128)(2,1)}), bf16[8,256,128]{2,1,0:T(8,128)(2,1)S(1)}, u32[]{:S(2)}, u32[]{:S(2)}) async-start(bf16[8,256,128]{2,1,0:T(8,128)(2,1)} %split_pairs.1), calls=%async_computation | async-start | bytes 1048576 | tf_op jit(solution)/shard_map/all_to_all | solution.py:239
  9.3 5.6 %split_heads.1 = bf16[8,128,1024]{2,1,0:T(8,128)(2,1)} custom-call(bf16[128,8192]{1,0:T(8,128)(2,1)} %from_ref.1), custom_call_target="tpu_custom_call" | custom-call | bytes 4194304 | tf_op jit(solution)/shard_map/split_heads/pallas_call | solution.py:160
  15.7 2.3 %all-to-all-done = bf16[8,256,128]{2,1,0:T(8,128)(2,1)S(1)} async-done(((bf16[8,256,128]{2,1,0:T(8,128)(2,1)}), bf16[8,256,128]{2,1,0:T(8,128)(2,1)S(1)}, u32[]{:S(2)}, u32[]{:S(2)}) %all-to-all-start) | async-done | bytes 524320 | tf_op jit(solution)/shard_map/all_to_all | solution.py:239
  19.0 10.4 %all-to-all-start.1 = ((bf16[32,8,8,128]{3,2,1,0:T(8,128)(2,1)}), bf16[32,8,8,128]{3,2,1,0:T(8,128)(2,1)S(1)}, u32[]{:S(2)}, u32[]{:S(2)}) async-start(bf16[32,8,8,128]{3,2,1,0:T(8,128)(2,1)} %copy_bitcast_fusion), calls=%async_computation.1 | async-start | bytes 1048576 | tf_op jit(solution)/shard_map/all_to_all | solution.py:255
  32.9 10.5 %all-to-all-done.1 = bf16[32,8,8,128]{3,2,1,0:T(8,128)(2,1)S(1)} async-done(((bf16[32,8,8,128]{3,2,1,0:T(8,128)(2,1)}), bf16[32,8,8,128]{3,2,1,0:T(8,128)(2,1)S(1)}, u32[]{:S(2)}, u32[]{:S(2)}) %all-to-all-start.1) | async-done | bytes 524320 | tf_op jit(solution)/shard_map/all_to_all | solution.py:255
  44.0 2.4 %collective-permute-start.14 = (bf16[48,8,128]{2,1,0:T(8,128)(2,1)S(1)}, bf16[48,8,128]{2,1,0:T(8,128)(2,1)S(1)}, u32[]{:S(2)}, u32[]{:S(2)}) collective-permute-start(bf16[48,8,128]{2,1,0:T(8,128)(2,1)S(1)} %gather_fusion.1), channel_id=1, source_target_pairs={{0,28},{4,0},{8,4},{12,8},{16,12},{20,16},{24,20},{28,24},{1,29},{... | collective-permute-start | bytes 294920 | tf_op jit(solution)/shard_map/ppermute | solution.py:236
  49.8 7.0 %all-to-all-start.2 = ((bf16[8,128,1024]{2,1,0:T(8,128)(2,1)}), bf16[8,128,1024]{2,1,0:T(8,128)(2,1)S(1)}, u32[]{:S(2)}, u32[]{:S(2)}) async-start(bf16[8,128,1024]{2,1,0:T(8,128)(2,1)} %split_heads.1), calls=%async_computation.2 | async-start | bytes 4194304 | tf_op jit(solution)/shard_map/all_to_all | solution.py:265
  56.8 2.2 %collective-permute-start.9 = (bf16[48,8,128]{2,1,0:T(8,128)(2,1)S(1)}, bf16[48,8,128]{2,1,0:T(8,128)(2,1)S(1)}, u32[]{:S(2)}, u32[]{:S(2)}) collective-permute-start(bf16[48,8,128]{2,1,0:T(8,128)(2,1)S(1)} %gather_fusion.1), channel_id=1, source_target_pairs={{0,8},{4,12},{8,16},{12,20},{16,24},{20,28},{24,0},{28,4},{1,9},{5... | collective-permute-start | bytes 294920 | tf_op jit(solution)/shard_map/ppermute | solution.py:236
  59.6 3.5 %collective-permute-done.9 = bf16[48,8,128]{2,1,0:T(8,128)(2,1)S(1)} collective-permute-done((bf16[48,8,128]{2,1,0:T(8,128)(2,1)S(1)}, bf16[48,8,128]{2,1,0:T(8,128)(2,1)S(1)}, u32[]{:S(2)}, u32[]{:S(2)}) %collective-permute-start.9) | collective-permute-done | bytes 98336 | tf_op jit(solution)/shard_map/ppermute | solution.py:236
  63.2 4.5 %collective-permute-start.10 = (bf16[48,8,128]{2,1,0:T(8,128)(2,1)S(1)}, bf16[48,8,128]{2,1,0:T(8,128)(2,1)S(1)}, u32[]{:S(2)}, u32[]{:S(2)}) collective-permute-start(bf16[48,8,128]{2,1,0:T(8,128)(2,1)S(1)} %gather_fusion.1), channel_id=1, source_target_pairs={{0,12},{4,16},{8,20},{12,24},{16,28},{20,0},{24,4},{28,8},{1,13},{... | collective-permute-start | bytes 294920 | tf_op jit(solution)/shard_map/ppermute | solution.py:236
  68.3 7.4 %collective-permute-done.10 = bf16[48,8,128]{2,1,0:T(8,128)(2,1)S(1)} collective-permute-done((bf16[48,8,128]{2,1,0:T(8,128)(2,1)S(1)}, bf16[48,8,128]{2,1,0:T(8,128)(2,1)S(1)}, u32[]{:S(2)}, u32[]{:S(2)}) %collective-permute-start.10) | collective-permute-done | bytes 98336 | tf_op jit(solution)/shard_map/ppermute | solution.py:236
  76.3 8.9 %collective-permute-done.11 = bf16[48,8,128]{2,1,0:T(8,128)(2,1)S(1)} collective-permute-done((bf16[48,8,128]{2,1,0:T(8,128)(2,1)S(1)}, bf16[48,8,128]{2,1,0:T(8,128)(2,1)S(1)}, u32[]{:S(2)}, u32[]{:S(2)}) %collective-permute-start.11) | collective-permute-done | bytes 98336 | tf_op jit(solution)/shard_map/ppermute | solution.py:236
  86.5 5.1 %collective-permute-done.12 = bf16[48,8,128]{2,1,0:T(8,128)(2,1)S(1)} collective-permute-done((bf16[48,8,128]{2,1,0:T(8,128)(2,1)S(1)}, bf16[48,8,128]{2,1,0:T(8,128)(2,1)S(1)}, u32[]{:S(2)}, u32[]{:S(2)}) %collective-permute-start.12) | collective-permute-done | bytes 98336 | tf_op jit(solution)/shard_map/ppermute | solution.py:236
  95.5 8.6 %collective-permute-done.3.rest_4_ = bf16[4,256,128]{2,1,0:T(8,128)(2,1)} collective-permute-done((bf16[4,256,128]{2,1,0:T(8,128)(2,1)}, bf16[4,256,128]{2,1,0:T(8,128)(2,1)}, u32[]{:S(2)}, u32[]{:S(2)}) %collective-permute-start.3) | collective-permute-done | bytes 262176 | tf_op jit(solution)/shard_map/ppermute | solution.py:251
  104.1 2.3 %collective-permute-done.2.rest_3_ = bf16[4,256,128]{2,1,0:T(8,128)(2,1)} collective-permute-done((bf16[4,256,128]{2,1,0:T(8,128)(2,1)}, bf16[4,256,128]{2,1,0:T(8,128)(2,1)}, u32[]{:S(2)}, u32[]{:S(2)}) %collective-permute-start.2) | collective-permute-done | bytes 262176 | tf_op jit(solution)/shard_map/ppermute | solution.py:236
  106.7 3.0 %collective-permute-done.16.rest_11_ = bf16[8,48,8,128]{3,2,1,0:T(8,128)(2,1)S(1)} collective-permute-done((bf16[8,48,8,128]{3,2,1,0:T(8,128)(2,1)}, bf16[8,48,8,128]{3,2,1,0:T(8,128)(2,1)S(1)}, u32[]{:S(2)}, u32[]{:S(2)}) %collective-permute-start.16) | collective-permute-done | bytes 786464 | tf_op jit(solution)/shard_map/ppermute | solution.py:236
  110.5 3.1 %collective-permute-start.18 = (bf16[4,48,8,128]{3,2,1,0:T(8,128)(2,1)}, bf16[4,48,8,128]{3,2,1,0:T(8,128)(2,1)}, u32[]{:S(2)}, u32[]{:S(2)}) collective-permute-start(bf16[4,48,8,128]{3,2,1,0:T(8,128)(2,1)} %slice.25), channel_id=1, source_target_pairs={{0,192},{64,0},{128,64},{192,128},{1,193},{65,1},{129,65},{193,129... | collective-permute-start | bytes 1179656 | tf_op jit(solution)/shard_map/ppermute | solution.py:236
  113.6 10.8 %collective-permute-done.15.rest_10_ = bf16[8,48,8,128]{3,2,1,0:T(8,128)(2,1)} collective-permute-done((bf16[8,48,8,128]{3,2,1,0:T(8,128)(2,1)}, bf16[8,48,8,128]{3,2,1,0:T(8,128)(2,1)}, u32[]{:S(2)}, u32[]{:S(2)}) %collective-permute-start.15) | collective-permute-done | bytes 786464 | tf_op jit(solution)/shard_map/ppermute | solution.py:236
  126.9 8.5 %collective-permute-done.7.rest_8_ = bf16[4,256,128]{2,1,0:T(8,128)(2,1)} collective-permute-done((bf16[4,256,128]{2,1,0:T(8,128)(2,1)}, bf16[4,256,128]{2,1,0:T(8,128)(2,1)}, u32[]{:S(2)}, u32[]{:S(2)}) %collective-permute-start.7) | collective-permute-done | bytes 262176 | tf_op jit(solution)/shard_map/ppermute | solution.py:251
  137.2 4.7 %collective-permute-done.17.rest_12_ = bf16[4,48,8,128]{3,2,1,0:T(8,128)(2,1)} collective-permute-done((bf16[4,48,8,128]{3,2,1,0:T(8,128)(2,1)}, bf16[4,48,8,128]{3,2,1,0:T(8,128)(2,1)}, u32[]{:S(2)}, u32[]{:S(2)}) %collective-permute-start.17) | collective-permute-done | bytes 393248 | tf_op jit(solution)/shard_map/ppermute | solution.py:236
  141.9 27.6 %attend.1 = bf16[8,128,1024]{2,1,0:T(8,128)(2,1)S(1)} custom-call(s32[8]{0:T(128)S(1)} %fusion.12.turns, s32[640]{0:T(1024)S(1)} %reshape.329.tile_of, f32[640]{0:T(1024)S(1)} %select_n.118.bias_of, s32[2]{0:T(128)S(1)} %pad_add_fusion.3.spot, bf16[8,128,1024]{2,1,0:T(8,128)(2,1)S(1)} %all-to-all-done.2.q_ref, bf16[2,4,256,128]{3,2,1,0:T(8,128)(2,1)S(1)} %bitcast.29, ...), custom_call_target="tpu_custom_call" | custom-call | flops 3221225472 | bytes 10485760 | tf_op jit(solution)/shard_map/attend/pallas_call | solution.py:113
  169.6 31.3 %all_to_all.20.from_ref = bf16[8,128,1024]{2,1,0:T(8,128)(2,1)} all-to-all(bf16[8,128,1024]{2,1,0:T(8,128)(2,1)S(1)} %attend.1), channel_id=1, replica_groups=mesh['x'=4,'c'=2,'z'=8,'y'=4] {'c','y'}, dimensions={0} | all-to-all | bytes 4194304 | tf_op jit(solution)/shard_map/all_to_all | solution.py:278
  200.9 5.6 %merge_heads.1 = bf16[128,8192]{1,0:T(8,128)(2,1)} custom-call(bf16[8,128,1024]{2,1,0:T(8,128)(2,1)} %all_to_all.20.from_ref), custom_call_target="tpu_custom_call" | custom-call | bytes 4194304 | tf_op jit(solution)/shard_map/merge_heads/pallas_call | solution.py:173
  (91 shorter events, 22.3 us)
Async XLA Ops:
  2.0 16.0 %all-to-all-start = ((bf16[8,256,128]{2,1,0:T(8,128)(2,1)}), bf16[8,256,128]{2,1,0:T(8,128)(2,1)S(1)}, u32[]{:S(2)}, u32[]{:S(2)}) async-start(bf16[8,256,128]{2,1,0:T(8,128)(2,1)} %split_pairs.1), calls=%async_computation | async-start | bytes 1048576 | tf_op jit(solution)/shard_map/all_to_all | solution.py:239
  19.0 24.5 %all-to-all-start.1 = ((bf16[32,8,8,128]{3,2,1,0:T(8,128)(2,1)}), bf16[32,8,8,128]{3,2,1,0:T(8,128)(2,1)S(1)}, u32[]{:S(2)}, u32[]{:S(2)}) async-start(bf16[32,8,8,128]{3,2,1,0:T(8,128)(2,1)} %copy_bitcast_fusion), calls=%async_computation.1 | async-start | bytes 1048576 | tf_op jit(solution)/shard_map/all_to_all | solution.py:255
  30.5 64.6 %collective-permute-start.1 = (bf16[4,256,128]{2,1,0:T(8,128)(2,1)}, bf16[4,256,128]{2,1,0:T(8,128)(2,1)}, u32[]{:S(2)}, u32[]{:S(2)}) collective-permute-start(bf16[4,256,128]{2,1,0:T(8,128)(2,1)} %get-tuple-element.17), channel_id=1, source_target_pairs={{0,4},{4,8},{8,12},{12,16},{16,20},{20,24},{24,28},{28,64},{64,68}... | collective-permute-start | bytes 786440 | tf_op jit(solution)/shard_map/ppermute | solution.py:251
  31.7 63.4 %collective-permute-start = (bf16[4,256,128]{2,1,0:T(8,128)(2,1)}, bf16[4,256,128]{2,1,0:T(8,128)(2,1)}, u32[]{:S(2)}, u32[]{:S(2)}) collective-permute-start(bf16[4,256,128]{2,1,0:T(8,128)(2,1)} %get-tuple-element.18), channel_id=1, source_target_pairs={{0,4},{4,8},{8,12},{12,16},{16,20},{20,24},{24,28},{28,0},{1,5},{5... | collective-permute-start | bytes 786440 | tf_op jit(solution)/shard_map/ppermute | solution.py:236
  44.0 48.8 %collective-permute-start.14 = (bf16[48,8,128]{2,1,0:T(8,128)(2,1)S(1)}, bf16[48,8,128]{2,1,0:T(8,128)(2,1)S(1)}, u32[]{:S(2)}, u32[]{:S(2)}) collective-permute-start(bf16[48,8,128]{2,1,0:T(8,128)(2,1)S(1)} %gather_fusion.1), channel_id=1, source_target_pairs={{0,28},{4,0},{8,4},{12,8},{16,12},{20,16},{24,20},{28,24},{1,29},{... | collective-permute-start | bytes 294920 | tf_op jit(solution)/shard_map/ppermute | solution.py:236
  46.4 45.8 %collective-permute-start.13 = (bf16[48,8,128]{2,1,0:T(8,128)(2,1)S(1)}, bf16[48,8,128]{2,1,0:T(8,128)(2,1)S(1)}, u32[]{:S(2)}, u32[]{:S(2)}) collective-permute-start(bf16[48,8,128]{2,1,0:T(8,128)(2,1)S(1)} %gather_fusion.1), channel_id=1, source_target_pairs={{0,24},{4,28},{8,0},{12,4},{16,8},{20,12},{24,16},{28,20},{1,25},{... | collective-permute-start | bytes 294920 | tf_op jit(solution)/shard_map/ppermute | solution.py:236
  48.0 8.8 %collective-permute-start.8 = (bf16[48,8,128]{2,1,0:T(8,128)(2,1)S(1)}, bf16[48,8,128]{2,1,0:T(8,128)(2,1)S(1)}, u32[]{:S(2)}, u32[]{:S(2)}) collective-permute-start(bf16[48,8,128]{2,1,0:T(8,128)(2,1)S(1)} %gather_fusion.1), channel_id=1, source_target_pairs={{0,4},{4,8},{8,12},{12,16},{16,20},{20,24},{24,28},{28,0},{1,5},{5... | collective-permute-start | bytes 294920 | tf_op jit(solution)/shard_map/ppermute | solution.py:236
  49.8 56.8 %copy-start.4 = (s32[8]{0:T(128)S(1)}, s32[8]{0:T(128)}, u32[]{:S(2)}) copy-start(s32[8]{0:T(128)} %constant.156.clone) | copy-start | bytes 100
  49.8 56.8 %copy-start.1 = (s32[8,6]{1,0:T(8,128)S(1)}, s32[8,6]{1,0:T(8,128)}, u32[]{:S(2)}) copy-start(s32[8,6]{1,0:T(8,128)} %constant.166) | copy-start | bytes 580
  49.8 92.1 %all-to-all-start.2 = ((bf16[8,128,1024]{2,1,0:T(8,128)(2,1)}), bf16[8,128,1024]{2,1,0:T(8,128)(2,1)S(1)}, u32[]{:S(2)}, u32[]{:S(2)}) async-start(bf16[8,128,1024]{2,1,0:T(8,128)(2,1)} %split_heads.1), calls=%async_computation.2 | async-start | bytes 4194304 | tf_op jit(solution)/shard_map/all_to_all | solution.py:265
  56.8 6.4 %collective-permute-start.9 = (bf16[48,8,128]{2,1,0:T(8,128)(2,1)S(1)}, bf16[48,8,128]{2,1,0:T(8,128)(2,1)S(1)}, u32[]{:S(2)}, u32[]{:S(2)}) collective-permute-start(bf16[48,8,128]{2,1,0:T(8,128)(2,1)S(1)} %gather_fusion.1), channel_id=1, source_target_pairs={{0,8},{4,12},{8,16},{12,20},{16,24},{20,28},{24,0},{28,4},{1,9},{5... | collective-permute-start | bytes 294920 | tf_op jit(solution)/shard_map/ppermute | solution.py:236
  63.2 12.5 %collective-permute-start.10 = (bf16[48,8,128]{2,1,0:T(8,128)(2,1)S(1)}, bf16[48,8,128]{2,1,0:T(8,128)(2,1)S(1)}, u32[]{:S(2)}, u32[]{:S(2)}) collective-permute-start(bf16[48,8,128]{2,1,0:T(8,128)(2,1)S(1)} %gather_fusion.1), channel_id=1, source_target_pairs={{0,12},{4,16},{8,20},{12,24},{16,28},{20,0},{24,4},{28,8},{1,13},{... | collective-permute-start | bytes 294920 | tf_op jit(solution)/shard_map/ppermute | solution.py:236
  75.7 9.5 %collective-permute-start.11 = (bf16[48,8,128]{2,1,0:T(8,128)(2,1)S(1)}, bf16[48,8,128]{2,1,0:T(8,128)(2,1)S(1)}, u32[]{:S(2)}, u32[]{:S(2)}) collective-permute-start(bf16[48,8,128]{2,1,0:T(8,128)(2,1)S(1)} %gather_fusion.1), channel_id=1, source_target_pairs={{0,16},{4,20},{8,24},{12,28},{16,0},{20,4},{24,8},{28,12},{1,17},{... | collective-permute-start | bytes 294920 | tf_op jit(solution)/shard_map/ppermute | solution.py:236
  85.2 6.4 %collective-permute-start.12 = (bf16[48,8,128]{2,1,0:T(8,128)(2,1)S(1)}, bf16[48,8,128]{2,1,0:T(8,128)(2,1)S(1)}, u32[]{:S(2)}, u32[]{:S(2)}) collective-permute-start(bf16[48,8,128]{2,1,0:T(8,128)(2,1)S(1)} %gather_fusion.1), channel_id=1, source_target_pairs={{0,20},{4,24},{8,28},{12,0},{16,4},{20,8},{24,12},{28,16},{1,21},{... | collective-permute-start | bytes 294920 | tf_op jit(solution)/shard_map/ppermute | solution.py:236
  93.5 16.2 %collective-permute-start.16 = (bf16[8,48,8,128]{3,2,1,0:T(8,128)(2,1)}, bf16[8,48,8,128]{3,2,1,0:T(8,128)(2,1)S(1)}, u32[]{:S(2)}, u32[]{:S(2)}) collective-permute-start(bf16[8,48,8,128]{3,2,1,0:T(8,128)(2,1)} %bitcast_dynamic-update-slice_fusion.rest_9_), channel_id=1, source_target_pairs={{0,192},{64,0},{128,64},{192,128},{1,193},{65,1},{129,65},{193,129... | collective-permute-start | bytes 2359304 | tf_op jit(solution)/shard_map/ppermute | solution.py:236
  94.8 29.6 %collective-permute-start.15 = (bf16[8,48,8,128]{3,2,1,0:T(8,128)(2,1)}, bf16[8,48,8,128]{3,2,1,0:T(8,128)(2,1)}, u32[]{:S(2)}, u32[]{:S(2)}) collective-permute-start(bf16[8,48,8,128]{3,2,1,0:T(8,128)(2,1)} %bitcast_dynamic-update-slice_fusion.rest_9_), channel_id=1, source_target_pairs={{0,64},{64,128},{128,192},{192,0},{1,65},{65,129},{129,193},{193,1... | collective-permute-start | bytes 2359304 | tf_op jit(solution)/shard_map/ppermute | solution.py:236
  95.1 9.0 %collective-permute-start.3 = (bf16[4,256,128]{2,1,0:T(8,128)(2,1)}, bf16[4,256,128]{2,1,0:T(8,128)(2,1)}, u32[]{:S(2)}, u32[]{:S(2)}) collective-permute-start(bf16[4,256,128]{2,1,0:T(8,128)(2,1)} %collective-permute-done.1.rest_2_), channel_id=1, source_target_pairs={{0,4},{4,8},{8,12},{12,16},{16,20},{20,24},{24,28},{28,64},{64,68}... | collective-permute-start | bytes 786440 | tf_op jit(solution)/shard_map/ppermute | solution.py:251
  95.2 11.3 %collective-permute-start.2 = (bf16[4,256,128]{2,1,0:T(8,128)(2,1)}, bf16[4,256,128]{2,1,0:T(8,128)(2,1)}, u32[]{:S(2)}, u32[]{:S(2)}) collective-permute-start(bf16[4,256,128]{2,1,0:T(8,128)(2,1)} %collective-permute-done.rest_1_), channel_id=1, source_target_pairs={{0,4},{4,8},{8,12},{12,16},{16,20},{20,24},{24,28},{28,0},{1,5},{5... | collective-permute-start | bytes 786440 | tf_op jit(solution)/shard_map/ppermute | solution.py:236
  104.1 22.2 %collective-permute-start.5 = (bf16[4,256,128]{2,1,0:T(8,128)(2,1)}, bf16[4,256,128]{2,1,0:T(8,128)(2,1)}, u32[]{:S(2)}, u32[]{:S(2)}) collective-permute-start(bf16[4,256,128]{2,1,0:T(8,128)(2,1)} %collective-permute-done.3.rest_4_), channel_id=1, source_target_pairs={{0,4},{4,8},{8,12},{12,16},{16,20},{20,24},{24,28},{28,64},{64,68}... | collective-permute-start | bytes 786440 | tf_op jit(solution)/shard_map/ppermute | solution.py:251
  106.5 20.0 %collective-permute-start.4 = (bf16[4,256,128]{2,1,0:T(8,128)(2,1)}, bf16[4,256,128]{2,1,0:T(8,128)(2,1)}, u32[]{:S(2)}, u32[]{:S(2)}) collective-permute-start(bf16[4,256,128]{2,1,0:T(8,128)(2,1)} %collective-permute-done.2.rest_3_), channel_id=1, source_target_pairs={{0,4},{4,8},{8,12},{12,16},{16,20},{20,24},{24,28},{28,0},{1,5},{5... | collective-permute-start | bytes 786440 | tf_op jit(solution)/shard_map/ppermute | solution.py:236
  110.5 26.7 %collective-permute-start.18 = (bf16[4,48,8,128]{3,2,1,0:T(8,128)(2,1)}, bf16[4,48,8,128]{3,2,1,0:T(8,128)(2,1)}, u32[]{:S(2)}, u32[]{:S(2)}) collective-permute-start(bf16[4,48,8,128]{3,2,1,0:T(8,128)(2,1)} %slice.25), channel_id=1, source_target_pairs={{0,192},{64,0},{128,64},{192,128},{1,193},{65,1},{129,65},{193,129... | collective-permute-start | bytes 1179656 | tf_op jit(solution)/shard_map/ppermute | solution.py:236
  126.2 15.8 %collective-permute-start.17 = (bf16[4,48,8,128]{3,2,1,0:T(8,128)(2,1)}, bf16[4,48,8,128]{3,2,1,0:T(8,128)(2,1)}, u32[]{:S(2)}, u32[]{:S(2)}) collective-permute-start(bf16[4,48,8,128]{3,2,1,0:T(8,128)(2,1)} %slice.24), channel_id=1, source_target_pairs={{0,64},{64,128},{128,192},{192,0},{1,65},{65,129},{129,193},{193,1... | collective-permute-start | bytes 1179656 | tf_op jit(solution)/shard_map/ppermute | solution.py:236
  126.4 9.0 %collective-permute-start.7 = (bf16[4,256,128]{2,1,0:T(8,128)(2,1)}, bf16[4,256,128]{2,1,0:T(8,128)(2,1)}, u32[]{:S(2)}, u32[]{:S(2)}) collective-permute-start(bf16[4,256,128]{2,1,0:T(8,128)(2,1)} %collective-permute-done.5.rest_6_), channel_id=1, source_target_pairs={{0,4},{4,8},{8,12},{12,16},{16,20},{20,24},{24,28},{28,64},{64,68}... | collective-permute-start | bytes 786440 | tf_op jit(solution)/shard_map/ppermute | solution.py:251
  126.5 10.7 %collective-permute-start.6 = (bf16[4,256,128]{2,1,0:T(8,128)(2,1)}, bf16[4,256,128]{2,1,0:T(8,128)(2,1)}, u32[]{:S(2)}, u32[]{:S(2)}) collective-permute-start(bf16[4,256,128]{2,1,0:T(8,128)(2,1)} %collective-permute-done.4.rest_5_), channel_id=1, source_target_pairs={{0,4},{4,8},{8,12},{12,16},{16,20},{20,24},{24,28},{28,0},{1,5},{5... | collective-permute-start | bytes 786440 | tf_op jit(solution)/shard_map/ppermute | solution.py:236
  (6 other events, 145.6 us)

commit v3 on v2

--- a/solution.py
+++ b/solution.py
@@ -26,7 +26,7 @@
 STEPS = SPAN // ROW
 WINDOW = SPAN + ROW
 SLICES = CHIPS_X * CHIPS_Z
-PAIR_ROWS = 2 * BLOCK_TOKENS
+PAIR_ROWS = BLOCK_TOKENS + HEAD_SIZE
 SLICE_ROWS = PAIR_ROWS // SLICES
 PICKS = GROUP * NV
 SLOTS = 1 + NS + NV
@@ -74,42 +74,41 @@
 
     rows = lax.broadcasted_iota(jnp.int32, (BLOCK_TOKENS, BLOCK_TOKENS), 0)
     cols = lax.broadcasted_iota(jnp.int32, (BLOCK_TOKENS, BLOCK_TOKENS), 1)
-    causal = rows >= cols
+    causal = rows <= cols
 
     def attend(block, count):
         base = (head * PARTS + block) * SLOTS
         where = [tile_of[base + slot] for slot in range(count)]
         keys = jnp.concatenate([tiles[w, :BLOCK_TOKENS, :] for w in where], axis=0)
-        values = jnp.concatenate([tiles[w, BLOCK_TOKENS:, :] for w in where], axis=0)
+        values = jnp.concatenate([tiles[w, BLOCK_TOKENS:, :] for w in where], axis=1)
         raw = lax.dot_general(
-            q_ref[block], keys, (((1,), (1,)), ((), ())), preferred_element_type=jnp.float32
+            keys, q_ref[block], (((1,), (1,)), ((), ())), preferred_element_type=jnp.float32
         )
-        scores = [raw[:, s * BLOCK_TOKENS : (s + 1) * BLOCK_TOKENS] for s in range(count)]
+        scores = [raw[s * BLOCK_TOKENS : (s + 1) * BLOCK_TOKENS] for s in range(count)]
         scores[0] = jnp.where(causal, scores[0], NEG)
         for slot in range(1, count):
             scores[slot] = scores[slot] + bias_of[base + slot]
-        best = jnp.max(functools.reduce(jnp.maximum, scores), axis=1, keepdims=True)
+        best = jnp.max(functools.reduce(jnp.maximum, scores), axis=0, keepdims=True)
         weights = [jnp.exp2((s - best) * LOG2_SCALE) for s in scores]
-        total = jnp.sum(functools.reduce(jnp.add, weights), axis=1, keepdims=True)
-        probs = jnp.concatenate([w.astype(jnp.bfloat16) for w in weights], axis=1)
-        mixed = jnp.dot(probs, values, preferred_element_type=jnp.float32)
-        out_ref[block] = (mixed * (1.0 / total)).astype(jnp.bfloat16)
+        total = jnp.sum(functools.reduce(jnp.add, weights), axis=0, keepdims=True)
+        probs = jnp.concatenate([w.astype(jnp.bfloat16) for w in weights], axis=0)
+        mixed = jnp.dot(values, probs, preferred_element_type=jnp.float32)
+        mixed = mixed * (1.0 / total)
+        out_ref[block] = mixed.T.astype(jnp.bfloat16)
 
     for count in range(2, SLOTS + 1, 2):
 
         @pl.when(turns[head] == count)
         def _():
-            @pl.loop(0, CORES)
-            def _(run):
-                for place in range(ROW):
-                    attend(run * ROW + place, count)
+            for block in range(PARTS):
+                attend(block, count)
 
 
 def attend_all(turns, tile_of, bias_of, spot, q, near, far):
     head_spec = pl.BlockSpec(
         (PARTS, BLOCK_TOKENS, HEAD_SIZE), lambda head, *_: (0, 0, head)
     )
-    anywhere = pl.BlockSpec(memory_space=pl.ANY)
+    anywhere = pl.BlockSpec(memory_space=pltpu.HBM)
     return pl.pallas_call(
         attend_kernel,
         out_shape=jax.ShapeDtypeStruct(q.shape, jnp.bfloat16),
@@ -137,7 +136,7 @@
     for head in range(KEY_VALUE_HEADS):
         columns = slice(head * HEAD_SIZE, (head + 1) * HEAD_SIZE)
         out_ref[head, :BLOCK_TOKENS, :] = key_ref[:, columns]
-        out_ref[head, BLOCK_TOKENS:, :] = value_ref[:, columns]
+        out_ref[head, BLOCK_TOKENS:, :] = value_ref[:, columns].T
 
 
 def split_pairs(keys, values):
@@ -151,34 +150,32 @@
     )(keys, values)
 
 
-def move_kernel(from_ref, to_ref):
-    to_ref[...] = from_ref[...]
-
-
-def split_heads(rows):
-    width = rows.shape[1] // PARTS
+def move_heads_kernel(merge, from_ref, to_ref, sem):
+    parts, rows = (from_ref, to_ref) if merge else (to_ref, from_ref)
+    count, _, width = parts.shape
+    copies = []
+    for n in range(count):
+        part, columns = parts.at[n], rows.at[:, pl.ds(n * width, width)]
+        ends = (part, columns) if merge else (columns, part)
+        copies.append(pltpu.make_async_copy(*ends, sem.at[n]))
+    for copy in copies:
+        copy.start()
+    for copy in copies:
+        copy.wait()
+
+
+def move_heads(array, merge):
+    wide = (BLOCK_TOKENS, array.size // BLOCK_TOKENS)
+    split = (PARTS, BLOCK_TOKENS, wide[1] // PARTS)
     return pl.pallas_call(
-        move_kernel,
-        out_shape=jax.ShapeDtypeStruct((PARTS, BLOCK_TOKENS, width), rows.dtype),
-        grid=(PARTS,),
-        in_specs=[pl.BlockSpec((BLOCK_TOKENS, width), lambda n: (0, n))],
-        out_specs=pl.BlockSpec((None, BLOCK_TOKENS, width), lambda n: (n, 0, 0)),
+        functools.partial(move_heads_kernel, merge),
+        out_shape=jax.ShapeDtypeStruct(wide if merge else split, array.dtype),
+        in_specs=[pl.BlockSpec(memory_space=pl.ANY)],
+        out_specs=pl.BlockSpec(memory_space=pl.ANY),
+        scratch_shapes=[pltpu.SemaphoreType.DMA((PARTS,))],
         cost_estimate=pl.CostEstimate(flops=0, bytes_accessed=4 << 20, transcendentals=0),
-        name="split_heads",
-    )(rows)
-
-
-def merge_heads(parts):
-    width = parts.shape[2]
-    return pl.pallas_call(
-        move_kernel,
-        out_shape=jax.ShapeDtypeStruct((BLOCK_TOKENS, PARTS * width), parts.dtype),
-        grid=(PARTS,),
-        in_specs=[pl.BlockSpec((None, BLOCK_TOKENS, width), lambda n: (n, 0, 0))],
-        out_specs=pl.BlockSpec((BLOCK_TOKENS, width), lambda n: (0, n)),
-        cost_estimate=pl.CostEstimate(flops=0, bytes_accessed=4 << 20, transcendentals=0),
-        name="merge_heads",
-    )(parts)
+        name="merge_heads" if merge else "split_heads",
+    )(array)
 
 
 def slot_tables(vert, slash, first_blocks, z):
@@ -244,15 +241,14 @@
         for a in range(CHIPS_X)
         for b in range(CHIPS_Z)
     ]
-    near = [own]
-    first, second = own[0], own[1]
-    for _ in range(STEPS):
-        first = shifted(first, "z", 1)
-        second = lax.ppermute(second, ROW_AXES, onward)
-        near += [first, second]
+    def passed_on(first, second):
+        return shifted(first, "z", 1), lax.ppermute(second, ROW_AXES, onward)
 
     sliced = pairs.reshape(PARTS, SLICES, SLICE_ROWS, HEAD_SIZE).transpose(1, 0, 2, 3)
     sliced = lax.all_to_all(sliced, ROW_AXES, 0, 0, tiled=True)
+    one = passed_on(own[0], own[1])
+    two = passed_on(*one)
+    sliced, two = lax.optimization_barrier((sliced, two))
     vert = lax.dynamic_slice_in_dim(vert_blocks, key_head * GROUP, GROUP, 0)
     slash = lax.dynamic_slice_in_dim(slash_offsets, key_head * GROUP, GROUP, 0)
     listed = jnp.maximum(vert, 0).reshape(-1)
@@ -260,14 +256,24 @@
     at = (at_run // CORES * CHIPS_Z + at_z) * PARTS + at_run % CORES * ROW + place
     picked = sliced.reshape(SLICES * PARTS, SLICE_ROWS, HEAD_SIZE)[at]
 
-    queries = split_heads(queries)
+    queries = move_heads(queries, False)
     queries, picked = lax.optimization_barrier((queries, picked))
     q = lax.all_to_all(queries, HEAD_AXES, 0, 0, tiled=True)
 
-    column = jnp.stack([picked] + [shifted(picked, "z", n) for n in range(1, CHIPS_Z)])
+    three = passed_on(*two)
+    ahead, behind = [], []
+    for n in range(HALF):
+        behind += [shifted(behind[-1] if n else picked, "z", 1)]
+        if n < HALF - 1:
+            ahead += [shifted(ahead[-1] if n else picked, "z", -1)]
+    column = [picked] + behind + ahead[::-1]
+    column, three = lax.optimization_barrier((column, three))
+    column = jnp.stack(column)
+    four = passed_on(*three)
     right, left = shifted(column, "x", 1), shifted(column, "x", -1)
     far = [column, right, left]
     far += [shifted(right[:HALF], "x", 1), shifted(left[HALF:], "x", -1)]
+    near = [own, *one, *two, *three, *four]
 
     runs = jnp.arange(CORES, dtype=jnp.int32)
     first_blocks = ((x * CORES + runs) * CHIPS_Z + z) * ROW
@@ -276,7 +282,7 @@
     mixed = attend_all(turns, tile_of, bias_of, spot, q, near, far)
 
     returned = lax.all_to_all(mixed, HEAD_AXES, 0, 0, tiled=True)
-    return merge_heads(returned)
+    return move_heads(returned, True)
 
 
 def solution(mesh):

time: 208 us -> 327 us (1.57)
  Pallas kernels: 40.9 us -> 152 us
  waiting for transfers between devices: 77.5 us -> 65 us
  local copies, waits for them, and re-layouts: 11.5 us -> 22.5 us
  starting transfers between devices: 43.7 us -> 50 us
    pallas_call x2, Pallas kernels: 11.3 us -> 129 us  [move_heads(): pl.pallas_call(functools.partial(move_heads_kernel, merge), out_shape=jax...]
    ppermute x15, waiting for transfers between devices: 47.6 us -> 30.3 us  [shifted(): lax.ppermute(value, axis, [(n, (n + by) % count) for n in range(count)])]
    all_to_all x1, waiting for transfers between devices: 10.5 us -> 0.01 us  [shards(): sliced = lax.all_to_all(sliced, ROW_AXES, 0, 0, tiled=True)]
    unnamed x23 -> x47, local copies, waits for them, and re-layouts: 4.53 us -> 14.7 us
    ppermute x4, waiting for transfers between devices: 17.1 us -> 26.9 us  [passed_on(): return (shifted(first, 'z', 1), lax.ppermute(second, ROW_AXES, onward))]
    pallas_call x1, Pallas kernels: 27.6 us -> 20.5 us  [attend_all(): pl.pallas_call(attend_kernel, out_shape=jax.ShapeDtypeStruct(q.shape, jnp...]
    all_to_all x1, waiting for transfers between devices: 2.26 us -> 7.79 us  [shards(): pairs = lax.all_to_all(pairs, HEAD_AXES, 0, 0, tiled=True)]
    ppermute x4, starting transfers between devices: 1.4 us -> 5.4 us  [passed_on(): return (shifted(first, 'z', 1), lax.ppermute(second, ROW_AXES, onward))]
  transfers between devices with their start and end apart: 22 -> 22, of which waited for: 13 -> 9; matrix products, arithmetic and copies ran while one was open for 6% -> 6% of each run, Pallas kernels for 3% -> 20%
where the time goes in v3:
time: 327 us; the launch traced here: 326 us
  Pallas kernels  152 us (46%)
  waiting for transfers between devices  65 us (20%)
  starting transfers between devices  50 us (15%)
  blocking collectives  33 us (10%)
  local copies, waits for them, and re-layouts  22.5 us (7%)
    pallas_call x2, Pallas kernels, move_heads(): pl.pallas_call(functools.partial(move_heads_kernel, merge), out_shape=jax...  129 us
    all_to_all x1, blocking collectives, shards(): returned = lax.all_to_all(mixed, HEAD_AXES, 0, 0, tiled=True)  33 us
    ppermute x15, waiting for transfers between devices, shifted(): lax.ppermute(value, axis, [(n, (n + by) % count) for n in range(count)])  30.3 us
    ppermute x4, waiting for transfers between devices, passed_on(): return (shifted(first, 'z', 1), lax.ppermute(second, ROW_AXES, onward))  26.9 us
    pallas_call x1, Pallas kernels, attend_all(): pl.pallas_call(attend_kernel, out_shape=jax.ShapeDtypeStruct(q.shape, jnp...  20.5 us
    ppermute x15, starting transfers between devices, shifted(): lax.ppermute(value, axis, [(n, (n + by) % count) for n in range(count)])  19.6 us
    unnamed x47, local copies, waits for them, and re-layouts  14.7 us
    all_to_all x1, starting transfers between devices, shards(): sliced = lax.all_to_all(sliced, ROW_AXES, 0, 0, tiled=True)  10.4 us
  transfers between devices with their start and end apart: 22, of which 9 were waited for; matrix products, arithmetic and copies ran while one was open for 6% of the time, Pallas kernels for 20%

profile of v3, /device:TPU:1, one launch (start us, length us, event | category | flops | bytes accessed | tf_op | source)
XLA Modules:
  0.0 326.0 jit_solution(8516382325327338908)
XLA Ops:
  0.0 2.0 split_pairs.1
  2.0 6.6 %all-to-all-start = ((bf16[8,256,128]{2,1,0:T(8,128)(2,1)}), bf16[8,256,128]{2,1,0:T(8,128)(2,1)S(1)}, u32[]{:S(2)}, u32[]{:S(2)}) async-start(bf16[8,256,128]{2,1,0:T(8,128)(2,1)} %split_pairs.1), calls=%async_computation | async-start | bytes 1048576 | tf_op jit(solution)/shard_map/all_to_all | solution.py:236
  10.2 7.8 %all-to-all-done = bf16[8,256,128]{2,1,0:T(8,128)(2,1)S(1)} async-done(((bf16[8,256,128]{2,1,0:T(8,128)(2,1)}), bf16[8,256,128]{2,1,0:T(8,128)(2,1)S(1)}, u32[]{:S(2)}, u32[]{:S(2)}) %all-to-all-start) | async-done | bytes 524320 | tf_op jit(solution)/shard_map/all_to_all | solution.py:236
  18.9 10.4 %all-to-all-start.1 = ((bf16[32,8,8,128]{3,2,1,0:T(8,128)(2,1)}), bf16[32,8,8,128]{3,2,1,0:T(8,128)(2,1)S(1)}, u32[]{:S(2)}, u32[]{:S(2)}) async-start(bf16[32,8,8,128]{3,2,1,0:T(8,128)(2,1)} %copy_bitcast_fusion), calls=%async_computation.1 | async-start | bytes 1048576 | tf_op jit(solution)/shard_map/all_to_all | solution.py:248
  32.0 19.1 %collective-permute-done.2.rest_2_ = bf16[4,256,128]{2,1,0:T(8,128)(2,1)S(1)} collective-permute-done((bf16[4,256,128]{2,1,0:T(8,128)(2,1)S(1)}, bf16[4,256,128]{2,1,0:T(8,128)(2,1)S(1)}, u32[]{:S(2)}, u32[]{:S(2)}) %collective-permute-start.2) | collective-permute-done | bytes 262176 | tf_op jit(solution)/shard_map/ppermute | solution.py:245
  51.1 3.4 %collective-permute-done.rest_1_ = bf16[4,256,128]{2,1,0:T(8,128)(2,1)S(1)} collective-permute-done((bf16[4,256,128]{2,1,0:T(8,128)(2,1)S(1)}, bf16[4,256,128]{2,1,0:T(8,128)(2,1)S(1)}, u32[]{:S(2)}, u32[]{:S(2)}) %collective-permute-start) | collective-permute-done | bytes 262176 | tf_op jit(solution)/shard_map/ppermute | solution.py:233
  55.3 64.7 %split_heads.1 = bf16[8,128,1024]{2,1,0:T(8,128)(2,1)} custom-call(bf16[128,8192]{1,0:T(8,128)(2,1)} %from_ref.1), custom_call_target="tpu_custom_call" | custom-call | bytes 4194304 | tf_op jit(solution)/shard_map/split_heads/pallas_call | solution.py:170
  121.6 2.1 collective-permute-start.8
  123.7 1.8 collective-permute-done.4
  126.9 1.8 collective-permute-start.12
  131.3 1.9 collective-permute-done.9
  133.2 2.1 collective-permute-start.10
  135.3 5.5 %collective-permute-done.6 = bf16[48,8,128]{2,1,0:T(8,128)(2,1)} collective-permute-done((bf16[48,8,128]{2,1,0:T(8,128)(2,1)S(1)}, bf16[48,8,128]{2,1,0:T(8,128)(2,1)}, u32[]{:S(2)}, u32[]{:S(2)}) %collective-permute-start.6) | collective-permute-done | bytes 98336 | tf_op jit(solution)/shard_map/ppermute | solution.py:233
  141.0 8.0 %all-to-all-start.2 = ((bf16[8,128,1024]{2,1,0:T(8,128)(2,1)}), bf16[8,128,1024]{2,1,0:T(8,128)(2,1)S(1)}, u32[]{:S(2)}, u32[]{:S(2)}) async-start(bf16[8,128,1024]{2,1,0:T(8,128)(2,1)} %split_heads.1), calls=%async_computation.2 | async-start | bytes 4194304 | tf_op jit(solution)/shard_map/all_to_all | solution.py:261
  160.6 2.5 collective-permute-start.16
  164.4 13.4 %collective-permute-done.16.rest_11_ = bf16[8,48,8,128]{3,2,1,0:T(8,128)(2,1)S(1)} collective-permute-done((bf16[8,48,8,128]{3,2,1,0:T(8,128)(2,1)}, bf16[8,48,8,128]{3,2,1,0:T(8,128)(2,1)S(1)}, u32[]{:S(2)}, u32[]{:S(2)}) %collective-permute-start.16) | collective-permute-done | bytes 786464 | tf_op jit(solution)/shard_map/ppermute | solution.py:233
  178.5 3.3 %collective-permute-start.18 = (bf16[4,48,8,128]{3,2,1,0:T(8,128)(2,1)}, bf16[4,48,8,128]{3,2,1,0:T(8,128)(2,1)}, u32[]{:S(2)}, u32[]{:S(2)}) collective-permute-start(bf16[4,48,8,128]{3,2,1,0:T(8,128)(2,1)} %slice.25), channel_id=1, source_target_pairs={{0,192},{64,0},{128,64},{192,128},{1,193},{65,1},{129,65},{193,129... | collective-permute-start | bytes 1179656 | tf_op jit(solution)/shard_map/ppermute | solution.py:233
  183.8 3.8 %collective-permute-start.13 = (bf16[4,256,128]{2,1,0:T(8,128)(2,1)}, bf16[4,256,128]{2,1,0:T(8,128)(2,1)}, u32[]{:S(2)}, u32[]{:S(2)}) collective-permute-start(bf16[4,256,128]{2,1,0:T(8,128)(2,1)} %copy-done.8), channel_id=1, source_target_pairs={{0,4},{4,8},{8,12},{12,16},{16,20},{20,24},{24,28},{28,0},{1,5},{5... | collective-permute-start | bytes 786440 | tf_op jit(solution)/shard_map/ppermute | solution.py:233
  187.6 2.3 collective-permute-start.14
  190.9 4.2 %collective-permute-done.13.rest_7_ = bf16[4,256,128]{2,1,0:T(8,128)(2,1)} collective-permute-done((bf16[4,256,128]{2,1,0:T(8,128)(2,1)}, bf16[4,256,128]{2,1,0:T(8,128)(2,1)}, u32[]{:S(2)}, u32[]{:S(2)}) %collective-permute-start.13) | collective-permute-done | bytes 262176 | tf_op jit(solution)/shard_map/ppermute | solution.py:233
  195.1 7.7 %collective-permute-done.14.rest_8_ = bf16[4,256,128]{2,1,0:T(8,128)(2,1)} collective-permute-done((bf16[4,256,128]{2,1,0:T(8,128)(2,1)}, bf16[4,256,128]{2,1,0:T(8,128)(2,1)}, u32[]{:S(2)}, u32[]{:S(2)}) %collective-permute-start.14) | collective-permute-done | bytes 262176 | tf_op jit(solution)/shard_map/ppermute | solution.py:245
  207.6 20.5 %attend.1 = bf16[8,128,1024]{2,1,0:T(8,128)(2,1)S(1)} custom-call(s32[8]{0:T(128)S(1)} %fusion.12.turns, s32[640]{0:T(1024)S(1)} %reshape.329.tile_of, f32[640]{0:T(1024)S(1)} %select_n.118.bias_of, s32[2]{0:T(128)S(1)} %pad_add_fusion.3.spot, bf16[8,128,1024]{2,1,0:T(8,128)(2,1)S(1)} %all-to-all-done.2.q_ref, bf16[2,4,256,128]{3,2,1,0:T(8,128)(2,1)S(1)} %bitcast.29, ...), custom_call_target="tpu_custom_call" | custom-call | flops 3221225472 | bytes 10485760 | tf_op jit(solution)/shard_map/attend/pallas_call | solution.py:112
  228.1 33.0 %all_to_all.20.from_ref = bf16[8,128,1024]{2,1,0:T(8,128)(2,1)} all-to-all(bf16[8,128,1024]{2,1,0:T(8,128)(2,1)S(1)} %attend.1), channel_id=1, replica_groups=mesh['x'=4,'c'=2,'z'=8,'y'=4] {'c','y'}, dimensions={0} | all-to-all | bytes 4194304 | tf_op jit(solution)/shard_map/all_to_all | solution.py:284
  261.1 64.7 %merge_heads.1 = bf16[128,8192]{1,0:T(8,128)(2,1)} custom-call(bf16[8,128,1024]{2,1,0:T(8,128)(2,1)} %all_to_all.20.from_ref), custom_call_target="tpu_custom_call" | custom-call | bytes 4194304 | tf_op jit(solution)/shard_map/merge_heads/pallas_call | solution.py:170
  (114 shorter events, 32.7 us)
Async XLA Ops:
  2.0 16.0 %all-to-all-start = ((bf16[8,256,128]{2,1,0:T(8,128)(2,1)}), bf16[8,256,128]{2,1,0:T(8,128)(2,1)S(1)}, u32[]{:S(2)}, u32[]{:S(2)}) async-start(bf16[8,256,128]{2,1,0:T(8,128)(2,1)} %split_pairs.1), calls=%async_computation | async-start | bytes 1048576 | tf_op jit(solution)/shard_map/all_to_all | solution.py:236
  18.9 101.2 %all-to-all-start.1 = ((bf16[32,8,8,128]{3,2,1,0:T(8,128)(2,1)}), bf16[32,8,8,128]{3,2,1,0:T(8,128)(2,1)S(1)}, u32[]{:S(2)}, u32[]{:S(2)}) async-start(bf16[32,8,8,128]{3,2,1,0:T(8,128)(2,1)} %copy_bitcast_fusion), calls=%async_computation.1 | async-start | bytes 1048576 | tf_op jit(solution)/shard_map/all_to_all | solution.py:248
  29.4 21.8 %collective-permute-start.2 = (bf16[4,256,128]{2,1,0:T(8,128)(2,1)S(1)}, bf16[4,256,128]{2,1,0:T(8,128)(2,1)S(1)}, u32[]{:S(2)}, u32[]{:S(2)}) collective-permute-start(bf16[4,256,128]{2,1,0:T(8,128)(2,1)S(1)} %get-tuple-element.43), channel_id=1, source_target_pairs={{0,4},{4,8},{8,12},{12,16},{16,20},{20,24},{24,28},{28,64},{64,68}... | collective-permute-start | bytes 786440 | tf_op jit(solution)/shard_map/ppermute | solution.py:245
  30.7 23.9 %collective-permute-start = (bf16[4,256,128]{2,1,0:T(8,128)(2,1)S(1)}, bf16[4,256,128]{2,1,0:T(8,128)(2,1)S(1)}, u32[]{:S(2)}, u32[]{:S(2)}) collective-permute-start(bf16[4,256,128]{2,1,0:T(8,128)(2,1)S(1)} %get-tuple-element.44), channel_id=1, source_target_pairs={{0,4},{4,8},{8,12},{12,16},{16,20},{20,24},{24,28},{28,0},{1,5},{5... | collective-permute-start | bytes 786440 | tf_op jit(solution)/shard_map/ppermute | solution.py:233
  51.1 68.9 %copy-start = (bf16[4,256,128]{2,1,0:T(8,128)(2,1)}, bf16[4,256,128]{2,1,0:T(8,128)(2,1)S(1)}, u32[]{:S(2)}) copy-start(bf16[4,256,128]{2,1,0:T(8,128)(2,1)S(1)} %collective-permute-done.2.rest_2_) | copy-start | bytes 786436
  51.1 69.0 %collective-permute-start.3 = (bf16[4,256,128]{2,1,0:T(8,128)(2,1)S(1)}, bf16[4,256,128]{2,1,0:T(8,128)(2,1)S(1)}, u32[]{:S(2)}, u32[]{:S(2)}) collective-permute-start(bf16[4,256,128]{2,1,0:T(8,128)(2,1)S(1)} %collective-permute-done.2.rest_2_), channel_id=1, source_target_pairs={{0,4},{4,8},{8,12},{12,16},{16,20},{20,24},{24,28},{28,64},{64,68}... | collective-permute-start | bytes 786440 | tf_op jit(solution)/shard_map/ppermute | solution.py:245
  54.6 65.5 %copy-start.2 = (bf16[4,256,128]{2,1,0:T(8,128)(2,1)}, bf16[4,256,128]{2,1,0:T(8,128)(2,1)S(1)}, u32[]{:S(2)}) copy-start(bf16[4,256,128]{2,1,0:T(8,128)(2,1)S(1)} %collective-permute-done.rest_1_) | copy-start | bytes 786436
  54.6 65.6 %collective-permute-start.1 = (bf16[4,256,128]{2,1,0:T(8,128)(2,1)S(1)}, bf16[4,256,128]{2,1,0:T(8,128)(2,1)S(1)}, u32[]{:S(2)}, u32[]{:S(2)}) collective-permute-start(bf16[4,256,128]{2,1,0:T(8,128)(2,1)S(1)} %collective-permute-done.rest_1_), channel_id=1, source_target_pairs={{0,4},{4,8},{8,12},{12,16},{16,20},{20,24},{24,28},{28,0},{1,5},{5... | collective-permute-start | bytes 786440 | tf_op jit(solution)/shard_map/ppermute | solution.py:233
  120.8 4.8 %collective-permute-start.4 = (bf16[48,8,128]{2,1,0:T(8,128)(2,1)S(1)}, bf16[48,8,128]{2,1,0:T(8,128)(2,1)S(1)}, u32[]{:S(2)}, u32[]{:S(2)}) collective-permute-start(bf16[48,8,128]{2,1,0:T(8,128)(2,1)S(1)} %gather_fusion.1), channel_id=1, source_target_pairs={{0,4},{4,8},{8,12},{12,16},{16,20},{20,24},{24,28},{28,0},{1,5},{5... | collective-permute-start | bytes 294920 | tf_op jit(solution)/shard_map/ppermute | solution.py:233
  121.6 7.1 %collective-permute-start.8 = (bf16[48,8,128]{2,1,0:T(8,128)(2,1)S(1)}, bf16[48,8,128]{2,1,0:T(8,128)(2,1)S(1)}, u32[]{:S(2)}, u32[]{:S(2)}) collective-permute-start(bf16[48,8,128]{2,1,0:T(8,128)(2,1)S(1)} %gather_fusion.1), channel_id=1, source_target_pairs={{0,28},{4,0},{8,4},{12,8},{16,12},{20,16},{24,20},{28,24},{1,29},{... | collective-permute-start | bytes 294920 | tf_op jit(solution)/shard_map/ppermute | solution.py:233
  125.6 5.0 %collective-permute-start.5 = (bf16[48,8,128]{2,1,0:T(8,128)(2,1)S(1)}, bf16[48,8,128]{2,1,0:T(8,128)(2,1)S(1)}, u32[]{:S(2)}, u32[]{:S(2)}) collective-permute-start(bf16[48,8,128]{2,1,0:T(8,128)(2,1)S(1)} %collective-permute-done.4), channel_id=1, source_target_pairs={{0,4},{4,8},{8,12},{12,16},{16,20},{20,24},{24,28},{28,0},{1,5},{5... | collective-permute-start | bytes 294920 | tf_op jit(solution)/shard_map/ppermute | solution.py:233
  125.7 23.4 %collective-permute-start.11 = (bf16[4,256,128]{2,1,0:T(8,128)(2,1)S(1)}, bf16[4,256,128]{2,1,0:T(8,128)(2,1)S(1)}, u32[]{:S(2)}, u32[]{:S(2)}) collective-permute-start(bf16[4,256,128]{2,1,0:T(8,128)(2,1)S(1)} %collective-permute-done.1.rest_3_), channel_id=1, source_target_pairs={{0,4},{4,8},{8,12},{12,16},{16,20},{20,24},{24,28},{28,0},{1,5},{5... | collective-permute-start | bytes 786440 | tf_op jit(solution)/shard_map/ppermute | solution.py:233
  126.9 22.1 %collective-permute-start.12 = (bf16[4,256,128]{2,1,0:T(8,128)(2,1)S(1)}, bf16[4,256,128]{2,1,0:T(8,128)(2,1)}, u32[]{:S(2)}, u32[]{:S(2)}) collective-permute-start(bf16[4,256,128]{2,1,0:T(8,128)(2,1)S(1)} %collective-permute-done.3.rest_4_), channel_id=1, source_target_pairs={{0,4},{4,8},{8,12},{12,16},{16,20},{20,24},{24,28},{28,64},{64,68}... | collective-permute-start | bytes 786440 | tf_op jit(solution)/shard_map/ppermute | solution.py:245
  128.8 4.4 %collective-permute-start.9 = (bf16[48,8,128]{2,1,0:T(8,128)(2,1)S(1)}, bf16[48,8,128]{2,1,0:T(8,128)(2,1)}, u32[]{:S(2)}, u32[]{:S(2)}) collective-permute-start(bf16[48,8,128]{2,1,0:T(8,128)(2,1)S(1)} %collective-permute-done.8), channel_id=1, source_target_pairs={{0,28},{4,0},{8,4},{12,8},{16,12},{20,16},{24,20},{28,24},{1,29},{... | collective-permute-start | bytes 294920 | tf_op jit(solution)/shard_map/ppermute | solution.py:233
  130.5 10.3 %collective-permute-start.6 = (bf16[48,8,128]{2,1,0:T(8,128)(2,1)S(1)}, bf16[48,8,128]{2,1,0:T(8,128)(2,1)}, u32[]{:S(2)}, u32[]{:S(2)}) collective-permute-start(bf16[48,8,128]{2,1,0:T(8,128)(2,1)S(1)} %collective-permute-done.5), channel_id=1, source_target_pairs={{0,4},{4,8},{8,12},{12,16},{16,20},{20,24},{24,28},{28,0},{1,5},{5... | collective-permute-start | bytes 294920 | tf_op jit(solution)/shard_map/ppermute | solution.py:233
  133.2 15.9 %collective-permute-start.10 = (bf16[48,8,128]{2,1,0:T(8,128)(2,1)}, bf16[48,8,128]{2,1,0:T(8,128)(2,1)}, u32[]{:S(2)}, u32[]{:S(2)}) collective-permute-start(bf16[48,8,128]{2,1,0:T(8,128)(2,1)} %collective-permute-done.9), channel_id=1, source_target_pairs={{0,28},{4,0},{8,4},{12,8},{16,12},{20,16},{24,20},{28,24},{1,29},{... | collective-permute-start | bytes 294920 | tf_op jit(solution)/shard_map/ppermute | solution.py:233
  140.8 8.2 %collective-permute-start.7 = (bf16[48,8,128]{2,1,0:T(8,128)(2,1)}, bf16[48,8,128]{2,1,0:T(8,128)(2,1)}, u32[]{:S(2)}, u32[]{:S(2)}) collective-permute-start(bf16[48,8,128]{2,1,0:T(8,128)(2,1)} %collective-permute-done.6), channel_id=1, source_target_pairs={{0,4},{4,8},{8,12},{12,16},{16,20},{20,24},{24,28},{28,0},{1,5},{5... | collective-permute-start | bytes 294920 | tf_op jit(solution)/shard_map/ppermute | solution.py:233
  141.0 61.8 %all-to-all-start.2 = ((bf16[8,128,1024]{2,1,0:T(8,128)(2,1)}), bf16[8,128,1024]{2,1,0:T(8,128)(2,1)S(1)}, u32[]{:S(2)}, u32[]{:S(2)}) async-start(bf16[8,128,1024]{2,1,0:T(8,128)(2,1)} %split_heads.1), calls=%async_computation.2 | async-start | bytes 4194304 | tf_op jit(solution)/shard_map/all_to_all | solution.py:261
  160.6 17.2 %collective-permute-start.16 = (bf16[8,48,8,128]{3,2,1,0:T(8,128)(2,1)}, bf16[8,48,8,128]{3,2,1,0:T(8,128)(2,1)S(1)}, u32[]{:S(2)}, u32[]{:S(2)}) collective-permute-start(bf16[8,48,8,128]{3,2,1,0:T(8,128)(2,1)} %bitcast_dynamic-update-slice_fusion.rest_9_), channel_id=1, source_target_pairs={{0,192},{64,0},{128,64},{192,128},{1,193},{65,1},{129,65},{193,129... | collective-permute-start | bytes 2359304 | tf_op jit(solution)/shard_map/ppermute | solution.py:233
  163.0 18.8 %collective-permute-start.15 = (bf16[8,48,8,128]{3,2,1,0:T(8,128)(2,1)}, bf16[8,48,8,128]{3,2,1,0:T(8,128)(2,1)}, u32[]{:S(2)}, u32[]{:S(2)}) collective-permute-start(bf16[8,48,8,128]{3,2,1,0:T(8,128)(2,1)} %bitcast_dynamic-update-slice_fusion.rest_9_), channel_id=1, source_target_pairs={{0,64},{64,128},{128,192},{192,0},{1,65},{65,129},{129,193},{193,1... | collective-permute-start | bytes 2359304 | tf_op jit(solution)/shard_map/ppermute | solution.py:233
  178.5 24.3 %collective-permute-start.18 = (bf16[4,48,8,128]{3,2,1,0:T(8,128)(2,1)}, bf16[4,48,8,128]{3,2,1,0:T(8,128)(2,1)}, u32[]{:S(2)}, u32[]{:S(2)}) collective-permute-start(bf16[4,48,8,128]{3,2,1,0:T(8,128)(2,1)} %slice.25), channel_id=1, source_target_pairs={{0,192},{64,0},{128,64},{192,128},{1,193},{65,1},{129,65},{193,129... | collective-permute-start | bytes 1179656 | tf_op jit(solution)/shard_map/ppermute | solution.py:233
  183.6 19.2 %collective-permute-start.17 = (bf16[4,48,8,128]{3,2,1,0:T(8,128)(2,1)}, bf16[4,48,8,128]{3,2,1,0:T(8,128)(2,1)}, u32[]{:S(2)}, u32[]{:S(2)}) collective-permute-start(bf16[4,48,8,128]{3,2,1,0:T(8,128)(2,1)} %slice.24), channel_id=1, source_target_pairs={{0,64},{64,128},{128,192},{192,0},{1,65},{65,129},{129,193},{193,1... | collective-permute-start | bytes 1179656 | tf_op jit(solution)/shard_map/ppermute | solution.py:233
  183.8 11.3 %collective-permute-start.13 = (bf16[4,256,128]{2,1,0:T(8,128)(2,1)}, bf16[4,256,128]{2,1,0:T(8,128)(2,1)}, u32[]{:S(2)}, u32[]{:S(2)}) collective-permute-start(bf16[4,256,128]{2,1,0:T(8,128)(2,1)} %copy-done.8), channel_id=1, source_target_pairs={{0,4},{4,8},{8,12},{12,16},{16,20},{20,24},{24,28},{28,0},{1,5},{5... | collective-permute-start | bytes 786440 | tf_op jit(solution)/shard_map/ppermute | solution.py:233
  187.6 15.3 %collective-permute-start.14 = (bf16[4,256,128]{2,1,0:T(8,128)(2,1)}, bf16[4,256,128]{2,1,0:T(8,128)(2,1)}, u32[]{:S(2)}, u32[]{:S(2)}) collective-permute-start(bf16[4,256,128]{2,1,0:T(8,128)(2,1)} %collective-permute-done.12.rest_6_), channel_id=1, source_target_pairs={{0,4},{4,8},{8,12},{12,16},{16,20},{20,24},{24,28},{28,64},{64,68}... | collective-permute-start | bytes 786440 | tf_op jit(solution)/shard_map/ppermute | solution.py:245
  (18 other events, 283.7 us)

commit v4 on v3

--- a/solution.py
+++ b/solution.py
@@ -32,8 +32,8 @@
 SLOTS = 1 + NS + NV
 TILES = CORES * WINDOW + PICKS
 HALF = CHIPS_Z // 2
-FAR_X = (0, 1, -1, 2, 2)
-FAR_Z = (0, 0, 0, 0, HALF)
+FAR_X = (0, 0, 1, 1, -1, -1, 2, 2)
+FAR_Z = (0, HALF, 0, HALF, 0, HALF, 0, HALF)
 
 NEG = -1e30
 LOG2_SCALE = float(HEAD_SIZE**-0.5 * np.log2(np.e))
@@ -123,7 +123,7 @@
             ],
         ),
         compiler_params=pltpu.CompilerParams(
-            dimension_semantics=("arbitrary",), vmem_limit_bytes=40 << 20
+            dimension_semantics=("arbitrary",), vmem_limit_bytes=60 << 20
         ),
         cost_estimate=pl.CostEstimate(
             flops=4 * 64 * 6 * 128**3, bytes_accessed=10 << 20, transcendentals=64 * 6 * 128**2
@@ -146,6 +146,7 @@
             (KEY_VALUE_HEADS, PAIR_ROWS, HEAD_SIZE), jnp.bfloat16
         ),
         cost_estimate=pl.CostEstimate(flops=0, bytes_accessed=1 << 20, transcendentals=0),
+        compiler_params=pltpu.CompilerParams(vmem_limit_bytes=8 << 20),
         name="split_pairs",
     )(keys, values)
 
@@ -170,12 +171,30 @@
     return pl.pallas_call(
         functools.partial(move_heads_kernel, merge),
         out_shape=jax.ShapeDtypeStruct(wide if merge else split, array.dtype),
-        in_specs=[pl.BlockSpec(memory_space=pl.ANY)],
-        out_specs=pl.BlockSpec(memory_space=pl.ANY),
+        in_specs=[pl.BlockSpec(memory_space=pltpu.VMEM if merge else pltpu.HBM)],
+        out_specs=pl.BlockSpec(memory_space=pltpu.HBM if merge else pltpu.VMEM),
         scratch_shapes=[pltpu.SemaphoreType.DMA((PARTS,))],
         cost_estimate=pl.CostEstimate(flops=0, bytes_accessed=4 << 20, transcendentals=0),
+        compiler_params=pltpu.CompilerParams(vmem_limit_bytes=8 << 20),
         name="merge_heads" if merge else "split_heads",
     )(array)
+
+
+def stack_kernel(*refs):
+    halves = refs[CHIPS_Z:]
+    for n, ref in enumerate(refs[:CHIPS_Z]):
+        halves[n // HALF][n % HALF] = ref[...]
+
+
+def stack_halves(parts):
+    half = jax.ShapeDtypeStruct((HALF, *parts[0].shape), parts[0].dtype)
+    return pl.pallas_call(
+        stack_kernel,
+        out_shape=(half, half),
+        cost_estimate=pl.CostEstimate(flops=0, bytes_accessed=2 << 20, transcendentals=0),
+        compiler_params=pltpu.CompilerParams(vmem_limit_bytes=8 << 20),
+        name="stack_halves",
+    )(*parts)
 
 
 def slot_tables(vert, slash, first_blocks, z):
@@ -248,7 +267,6 @@
     sliced = lax.all_to_all(sliced, ROW_AXES, 0, 0, tiled=True)
     one = passed_on(own[0], own[1])
     two = passed_on(*one)
-    sliced, two = lax.optimization_barrier((sliced, two))
     vert = lax.dynamic_slice_in_dim(vert_blocks, key_head * GROUP, GROUP, 0)
     slash = lax.dynamic_slice_in_dim(slash_offsets, key_head * GROUP, GROUP, 0)
     listed = jnp.maximum(vert, 0).reshape(-1)
@@ -260,19 +278,19 @@
     queries, picked = lax.optimization_barrier((queries, picked))
     q = lax.all_to_all(queries, HEAD_AXES, 0, 0, tiled=True)
 
-    three = passed_on(*two)
     ahead, behind = [], []
     for n in range(HALF):
         behind += [shifted(behind[-1] if n else picked, "z", 1)]
         if n < HALF - 1:
             ahead += [shifted(ahead[-1] if n else picked, "z", -1)]
     column = [picked] + behind + ahead[::-1]
-    column, three = lax.optimization_barrier((column, three))
-    column = jnp.stack(column)
+    column, two = lax.optimization_barrier((column, two))
+    lower, upper = stack_halves(column)
+    three = passed_on(*two)
     four = passed_on(*three)
-    right, left = shifted(column, "x", 1), shifted(column, "x", -1)
-    far = [column, right, left]
-    far += [shifted(right[:HALF], "x", 1), shifted(left[HALF:], "x", -1)]
+    right, left = shifted(lower, "x", 1), shifted(upper, "x", -1)
+    far = [lower, upper, right, shifted(upper, "x", 1), shifted(lower, "x", -1), left]
+    far += [shifted(right, "x", 1), shifted(left, "x", -1)]
     near = [own, *one, *two, *three, *four]
 
     runs = jnp.arange(CORES, dtype=jnp.int32)

time: 327 us -> 190 us (0.58)
  Pallas kernels: 152 us -> 27 us
  local copies, waits for them, and re-layouts: 22.5 us -> 6.89 us
  waiting for transfers between devices: 65 us -> 74.8 us
  starting transfers between devices: 50 us -> 44.1 us
    pallas_call x2, Pallas kernels: 129 us -> 2.92 us  [move_heads(): pl.pallas_call(functools.partial(move_heads_kernel, merge), out_shape=jax...]
    ppermute x4, waiting for transfers between devices: 26.9 us -> 3.96 us  [passed_on(): return (shifted(first, 'z', 1), lax.ppermute(second, ROW_AXES, onward))]
    ppermute x15 -> x17, waiting for transfers between devices: 30.3 us -> 50.5 us  [shifted(): lax.ppermute(value, axis, [(n, (n + by) % count) for n in range(count)])]
    unnamed x47 -> x44, local copies, waits for them, and re-layouts: 14.7 us -> 2.66 us
    all_to_all x1, waiting for transfers between devices: 0.01 us -> 11.2 us  [shards(): sliced = lax.all_to_all(sliced, ROW_AXES, 0, 0, tiled=True)]
    ppermute x15 -> x17, starting transfers between devices: 19.6 us -> 16.5 us  [shifted(): lax.ppermute(value, axis, [(n, (n + by) % count) for n in range(count)])]
  transfers between devices with their start and end apart: 22 -> 24, of which waited for: 9 -> 13; matrix products, arithmetic and copies ran while one was open for 6% -> 3% of each run, Pallas kernels for 20% -> 1%
where the time goes in v4:
time: 190 us; the launch traced here: 188 us
  waiting for transfers between devices  74.8 us (39%)
  starting transfers between devices  44.1 us (23%)
  blocking collectives  32.6 us (17%)
  Pallas kernels  27 us (14%)
  local copies, waits for them, and re-layouts  6.89 us (4%)
  other arithmetic  2.51 us (1%)
    ppermute x17, waiting for transfers between devices, shifted(): lax.ppermute(value, axis, [(n, (n + by) % count) for n in range(count)])  50.5 us
    all_to_all x1, blocking collectives, shards(): returned = lax.all_to_all(mixed, HEAD_AXES, 0, 0, tiled=True)  32.6 us
    pallas_call x1, Pallas kernels, attend_all(): pl.pallas_call(attend_kernel, out_shape=jax.ShapeDtypeStruct(q.shape, jnp...  23.1 us
    ppermute x17, starting transfers between devices, shifted(): lax.ppermute(value, axis, [(n, (n + by) % count) for n in range(count)])  16.5 us
    all_to_all x1, waiting for transfers between devices, shards(): sliced = lax.all_to_all(sliced, ROW_AXES, 0, 0, tiled=True)  11.2 us
    all_to_all x1, starting transfers between devices, shards(): sliced = lax.all_to_all(sliced, ROW_AXES, 0, 0, tiled=True)  10.3 us
    all_to_all x1, waiting for transfers between devices, shards(): pairs = lax.all_to_all(pairs, HEAD_AXES, 0, 0, tiled=True)  9.03 us
    all_to_all x1, starting transfers between devices, shards(): q = lax.all_to_all(queries, HEAD_AXES, 0, 0, tiled=True)  7.96 us
  transfers between devices with their start and end apart: 24, of which 13 were waited for; matrix products, arithmetic and copies ran while one was open for 3% of the time, Pallas kernels for 1%

profile of v4, /device:TPU:1, one launch (start us, length us, event | category | flops | bytes accessed | tf_op | source)
XLA Modules:
  0.0 188.4 jit_solution(12981363583196567109)
XLA Ops:
  2.8 6.7 %all-to-all-start = ((bf16[8,256,128]{2,1,0:T(8,128)(2,1)}), bf16[8,256,128]{2,1,0:T(8,128)(2,1)S(1)}, u32[]{:S(2)}, u32[]{:S(2)}) async-start(bf16[8,256,128]{2,1,0:T(8,128)(2,1)} %split_pairs.1), calls=%async_computation | async-start | bytes 1048576 | tf_op jit(solution)/shard_map/all_to_all | solution.py:255
  9.8 9.0 %all-to-all-done = bf16[8,256,128]{2,1,0:T(8,128)(2,1)S(1)} async-done(((bf16[8,256,128]{2,1,0:T(8,128)(2,1)}), bf16[8,256,128]{2,1,0:T(8,128)(2,1)S(1)}, u32[]{:S(2)}, u32[]{:S(2)}) %all-to-all-start) | async-done | bytes 524320 | tf_op jit(solution)/shard_map/all_to_all | solution.py:255
  19.9 10.3 %all-to-all-start.1 = ((bf16[32,8,8,128]{3,2,1,0:T(8,128)(2,1)}), bf16[32,8,8,128]{3,2,1,0:T(8,128)(2,1)S(1)}, u32[]{:S(2)}, u32[]{:S(2)}) async-start(bf16[32,8,8,128]{3,2,1,0:T(8,128)(2,1)} %copy_bitcast_fusion), calls=%async_computation.1 | async-start | bytes 1048576 | tf_op jit(solution)/shard_map/all_to_all | solution.py:267
  30.6 1.5 split_heads.1
  33.1 11.2 %all-to-all-done.1 = bf16[32,8,8,128]{3,2,1,0:T(8,128)(2,1)S(1)} async-done(((bf16[32,8,8,128]{3,2,1,0:T(8,128)(2,1)}), bf16[32,8,8,128]{3,2,1,0:T(8,128)(2,1)S(1)}, u32[]{:S(2)}, u32[]{:S(2)}) %all-to-all-start.1) | async-done | bytes 524320 | tf_op jit(solution)/shard_map/all_to_all | solution.py:267
  45.0 8.0 %all-to-all-start.2 = ((bf16[8,128,1024]{2,1,0:T(8,128)(2,1)}), bf16[8,128,1024]{2,1,0:T(8,128)(2,1)}, u32[]{:S(2)}, u32[]{:S(2)}) async-start(bf16[8,128,1024]{2,1,0:T(8,128)(2,1)} %split_heads.1), calls=%async_computation.2 | async-start | bytes 4194304 | tf_op jit(solution)/shard_map/all_to_all | solution.py:279
  53.0 2.5 %collective-permute-start.1 = (bf16[4,256,128]{2,1,0:T(8,128)(2,1)S(1)}, bf16[4,256,128]{2,1,0:T(8,128)(2,1)S(1)}, u32[]{:S(2)}, u32[]{:S(2)}) collective-permute-start(bf16[4,256,128]{2,1,0:T(8,128)(2,1)S(1)} %get-tuple-element.41), channel_id=1, source_target_pairs={{0,4},{4,8},{8,12},{12,16},{16,20},{20,24},{24,28},{28,64},{64,68}... | collective-permute-start | bytes 786440 | tf_op jit(solution)/shard_map/ppermute | solution.py:264
  56.7 1.7 collective-permute-start.6
  58.4 11.5 %collective-permute-done.2.refs_1_ = bf16[48,8,128]{2,1,0:T(8,128)(2,1)S(1)} collective-permute-done((bf16[48,8,128]{2,1,0:T(8,128)(2,1)S(1)}, bf16[48,8,128]{2,1,0:T(8,128)(2,1)S(1)}, u32[]{:S(2)}, u32[]{:S(2)}) %collective-permute-start.2) | collective-permute-done | bytes 98336 | tf_op jit(solution)/shard_map/ppermute | solution.py:252
  72.4 1.7 collective-permute-start.7
  76.3 2.9 %collective-permute-start.8 = (bf16[48,8,128]{2,1,0:T(8,128)(2,1)S(1)}, bf16[48,8,128]{2,1,0:T(8,128)(2,1)S(1)}, u32[]{:S(2)}, u32[]{:S(2)}) collective-permute-start(bf16[48,8,128]{2,1,0:T(8,128)(2,1)S(1)} %collective-permute-done.7.refs_6_), channel_id=1, source_target_pairs={{0,28},{4,0},{8,4},{12,8},{16,12},{20,16},{24,20},{28,24},{1,29},{... | collective-permute-start | bytes 294920 | tf_op jit(solution)/shard_map/ppermute | solution.py:252
  79.2 9.4 %collective-permute-done.4.refs_3_ = bf16[48,8,128]{2,1,0:T(8,128)(2,1)S(1)} collective-permute-done((bf16[48,8,128]{2,1,0:T(8,128)(2,1)S(1)}, bf16[48,8,128]{2,1,0:T(8,128)(2,1)S(1)}, u32[]{:S(2)}, u32[]{:S(2)}) %collective-permute-start.4) | collective-permute-done | bytes 98336 | tf_op jit(solution)/shard_map/ppermute | solution.py:252
  88.8 4.5 %collective-permute-done.5.refs_4_ = bf16[48,8,128]{2,1,0:T(8,128)(2,1)S(1)} collective-permute-done((bf16[48,8,128]{2,1,0:T(8,128)(2,1)S(1)}, bf16[48,8,128]{2,1,0:T(8,128)(2,1)S(1)}, u32[]{:S(2)}, u32[]{:S(2)}) %collective-permute-start.5) | collective-permute-done | bytes 98336 | tf_op jit(solution)/shard_map/ppermute | solution.py:252
  93.6 2.5 %collective-permute-start.18 = (bf16[4,48,8,128]{3,2,1,0:T(8,128)(2,1)S(1)}, bf16[4,48,8,128]{3,2,1,0:T(8,128)(2,1)S(1)}, u32[]{:S(2)}, u32[]{:S(2)}) collective-permute-start(bf16[4,48,8,128]{3,2,1,0:T(8,128)(2,1)S(1)} %get-tuple-element.32.rest_10_), channel_id=1, source_target_pairs={{0,192},{64,0},{128,64},{192,128},{1,193},{65,1},{129,65},{193,129... | collective-permute-start | bytes 1179656 | tf_op jit(solution)/shard_map/ppermute | solution.py:252
  96.2 1.3 collective-permute-start.17
  97.8 6.5 %collective-permute-done.11.rest_5_ = bf16[4,256,128]{2,1,0:T(8,128)(2,1)} collective-permute-done((bf16[4,256,128]{2,1,0:T(8,128)(2,1)S(1)}, bf16[4,256,128]{2,1,0:T(8,128)(2,1)}, u32[]{:S(2)}, u32[]{:S(2)}) %collective-permute-start.11) | collective-permute-done | bytes 262176 | tf_op jit(solution)/shard_map/ppermute | solution.py:252
  104.4 2.6 %collective-permute-start.20 = (bf16[4,48,8,128]{3,2,1,0:T(8,128)(2,1)S(1)}, bf16[4,48,8,128]{3,2,1,0:T(8,128)(2,1)}, u32[]{:S(2)}, u32[]{:S(2)}) collective-permute-start(bf16[4,48,8,128]{3,2,1,0:T(8,128)(2,1)S(1)} %collective-permute-done.18.rest_14_), channel_id=1, source_target_pairs={{0,192},{64,0},{128,64},{192,128},{1,193},{65,1},{129,65},{193,129... | collective-permute-start | bytes 1179656 | tf_op jit(solution)/shard_map/ppermute | solution.py:252
  108.5 1.6 collective-permute-done.17.rest_13_
  112.8 3.6 %collective-permute-done.16.rest_12_ = bf16[4,48,8,128]{3,2,1,0:T(8,128)(2,1)S(1)} collective-permute-done((bf16[4,48,8,128]{3,2,1,0:T(8,128)(2,1)S(1)}, bf16[4,48,8,128]{3,2,1,0:T(8,128)(2,1)S(1)}, u32[]{:S(2)}, u32[]{:S(2)}) %collective-permute-start.16) | collective-permute-done | bytes 393248 | tf_op jit(solution)/shard_map/ppermute | solution.py:252
  116.4 2.7 %collective-permute-done.14.rest_8_ = bf16[4,256,128]{2,1,0:T(8,128)(2,1)} collective-permute-done((bf16[4,256,128]{2,1,0:T(8,128)(2,1)}, bf16[4,256,128]{2,1,0:T(8,128)(2,1)}, u32[]{:S(2)}, u32[]{:S(2)}) %collective-permute-start.14) | collective-permute-done | bytes 262176 | tf_op jit(solution)/shard_map/ppermute | solution.py:264
  119.1 11.3 %collective-permute-done.19.rest_15_ = bf16[4,48,8,128]{3,2,1,0:T(8,128)(2,1)S(1)} collective-permute-done((bf16[4,48,8,128]{3,2,1,0:T(8,128)(2,1)S(1)}, bf16[4,48,8,128]{3,2,1,0:T(8,128)(2,1)S(1)}, u32[]{:S(2)}, u32[]{:S(2)}) %collective-permute-start.19) | collective-permute-done | bytes 393248 | tf_op jit(solution)/shard_map/ppermute | solution.py:252
  131.2 23.1 %attend.1 = bf16[8,128,1024]{2,1,0:T(8,128)(2,1)} custom-call(s32[8]{0:T(128)} %fusion.12.turns, s32[640]{0:T(1024)} %reshape.329.tile_of, f32[640]{0:T(1024)} %select_n.118.bias_of, s32[2]{0:T(128)} %pad_add_fusion.3.spot, bf16[8,128,1024]{2,1,0:T(8,128)(2,1)} %all-to-all-done.2.q_ref, bf16[2,4,256,128]{3,2,1,0:T(8,128)(2,1)} %bitcast.13, ...), custom_call_target="tpu_custom_call" | custom-call | flops 3221225472 | bytes 10485760 | tf_op jit(solution)/shard_map/attend/pallas_call | solution.py:112
  154.3 32.6 %all_to_all.20.from_ref = bf16[8,128,1024]{2,1,0:T(8,128)(2,1)S(1)} all-to-all(bf16[8,128,1024]{2,1,0:T(8,128)(2,1)} %attend.1), channel_id=1, replica_groups=mesh['x'=4,'c'=2,'z'=8,'y'=4] {'c','y'}, dimensions={0} | all-to-all | bytes 4194304 | tf_op jit(solution)/shard_map/all_to_all | solution.py:302
  186.8 1.4 merge_heads.1
  (114 shorter events, 17.8 us)
Async XLA Ops:
  2.8 16.0 %all-to-all-start = ((bf16[8,256,128]{2,1,0:T(8,128)(2,1)}), bf16[8,256,128]{2,1,0:T(8,128)(2,1)S(1)}, u32[]{:S(2)}, u32[]{:S(2)}) async-start(bf16[8,256,128]{2,1,0:T(8,128)(2,1)} %split_pairs.1), calls=%async_computation | async-start | bytes 1048576 | tf_op jit(solution)/shard_map/all_to_all | solution.py:255
  19.9 24.5 %all-to-all-start.1 = ((bf16[32,8,8,128]{3,2,1,0:T(8,128)(2,1)}), bf16[32,8,8,128]{3,2,1,0:T(8,128)(2,1)S(1)}, u32[]{:S(2)}, u32[]{:S(2)}) async-start(bf16[32,8,8,128]{3,2,1,0:T(8,128)(2,1)} %copy_bitcast_fusion), calls=%async_computation.1 | async-start | bytes 1048576 | tf_op jit(solution)/shard_map/all_to_all | solution.py:267
  45.0 85.4 %all-to-all-start.2 = ((bf16[8,128,1024]{2,1,0:T(8,128)(2,1)}), bf16[8,128,1024]{2,1,0:T(8,128)(2,1)}, u32[]{:S(2)}, u32[]{:S(2)}) async-start(bf16[8,128,1024]{2,1,0:T(8,128)(2,1)} %split_heads.1), calls=%async_computation.2 | async-start | bytes 4194304 | tf_op jit(solution)/shard_map/all_to_all | solution.py:279
  53.0 18.2 %collective-permute-start.1 = (bf16[4,256,128]{2,1,0:T(8,128)(2,1)S(1)}, bf16[4,256,128]{2,1,0:T(8,128)(2,1)S(1)}, u32[]{:S(2)}, u32[]{:S(2)}) collective-permute-start(bf16[4,256,128]{2,1,0:T(8,128)(2,1)S(1)} %get-tuple-element.41), channel_id=1, source_target_pairs={{0,4},{4,8},{8,12},{12,16},{16,20},{20,24},{24,28},{28,64},{64,68}... | collective-permute-start | bytes 786440 | tf_op jit(solution)/shard_map/ppermute | solution.py:264
  55.5 15.8 %collective-permute-start = (bf16[4,256,128]{2,1,0:T(8,128)(2,1)S(1)}, bf16[4,256,128]{2,1,0:T(8,128)(2,1)S(1)}, u32[]{:S(2)}, u32[]{:S(2)}) collective-permute-start(bf16[4,256,128]{2,1,0:T(8,128)(2,1)S(1)} %get-tuple-element.42), channel_id=1, source_target_pairs={{0,4},{4,8},{8,12},{12,16},{16,20},{20,24},{24,28},{28,0},{1,5},{5... | collective-permute-start | bytes 786440 | tf_op jit(solution)/shard_map/ppermute | solution.py:252
  55.6 14.4 %collective-permute-start.2 = (bf16[48,8,128]{2,1,0:T(8,128)(2,1)S(1)}, bf16[48,8,128]{2,1,0:T(8,128)(2,1)S(1)}, u32[]{:S(2)}, u32[]{:S(2)}) collective-permute-start(bf16[48,8,128]{2,1,0:T(8,128)(2,1)S(1)} %gather_fusion.1), channel_id=1, source_target_pairs={{0,4},{4,8},{8,12},{12,16},{16,20},{20,24},{24,28},{28,0},{1,5},{5... | collective-permute-start | bytes 294920 | tf_op jit(solution)/shard_map/ppermute | solution.py:252
  56.7 15.7 %collective-permute-start.6 = (bf16[48,8,128]{2,1,0:T(8,128)(2,1)S(1)}, bf16[48,8,128]{2,1,0:T(8,128)(2,1)S(1)}, u32[]{:S(2)}, u32[]{:S(2)}) collective-permute-start(bf16[48,8,128]{2,1,0:T(8,128)(2,1)S(1)} %gather_fusion.1), channel_id=1, source_target_pairs={{0,28},{4,0},{8,4},{12,8},{16,12},{20,16},{24,20},{28,24},{1,29},{... | collective-permute-start | bytes 294920 | tf_op jit(solution)/shard_map/ppermute | solution.py:252
  69.9 5.1 %collective-permute-start.3 = (bf16[48,8,128]{2,1,0:T(8,128)(2,1)S(1)}, bf16[48,8,128]{2,1,0:T(8,128)(2,1)S(1)}, u32[]{:S(2)}, u32[]{:S(2)}) collective-permute-start(bf16[48,8,128]{2,1,0:T(8,128)(2,1)S(1)} %collective-permute-done.2.refs_1_), channel_id=1, source_target_pairs={{0,4},{4,8},{8,12},{12,16},{16,20},{20,24},{24,28},{28,0},{1,5},{5... | collective-permute-start | bytes 294920 | tf_op jit(solution)/shard_map/ppermute | solution.py:252
  71.2 17.5 %collective-permute-start.10 = (bf16[4,256,128]{2,1,0:T(8,128)(2,1)S(1)}, bf16[4,256,128]{2,1,0:T(8,128)(2,1)}, u32[]{:S(2)}, u32[]{:S(2)}) collective-permute-start(bf16[4,256,128]{2,1,0:T(8,128)(2,1)S(1)} %collective-permute-done.1.rest_2_), channel_id=1, source_target_pairs={{0,4},{4,8},{8,12},{12,16},{16,20},{20,24},{24,28},{28,64},{64,68}... | collective-permute-start | bytes 786440 | tf_op jit(solution)/shard_map/ppermute | solution.py:264
  71.3 17.4 %collective-permute-start.9 = (bf16[4,256,128]{2,1,0:T(8,128)(2,1)S(1)}, bf16[4,256,128]{2,1,0:T(8,128)(2,1)S(1)}, u32[]{:S(2)}, u32[]{:S(2)}) collective-permute-start(bf16[4,256,128]{2,1,0:T(8,128)(2,1)S(1)} %collective-permute-done.rest_1_), channel_id=1, source_target_pairs={{0,4},{4,8},{8,12},{12,16},{16,20},{20,24},{24,28},{28,0},{1,5},{5... | collective-permute-start | bytes 786440 | tf_op jit(solution)/shard_map/ppermute | solution.py:252
  72.4 3.9 %collective-permute-start.7 = (bf16[48,8,128]{2,1,0:T(8,128)(2,1)S(1)}, bf16[48,8,128]{2,1,0:T(8,128)(2,1)S(1)}, u32[]{:S(2)}, u32[]{:S(2)}) collective-permute-start(bf16[48,8,128]{2,1,0:T(8,128)(2,1)S(1)} %collective-permute-done.6.refs_7_), channel_id=1, source_target_pairs={{0,28},{4,0},{8,4},{12,8},{16,12},{20,16},{24,20},{28,24},{1,29},{... | collective-permute-start | bytes 294920 | tf_op jit(solution)/shard_map/ppermute | solution.py:252
  75.0 13.5 %collective-permute-start.4 = (bf16[48,8,128]{2,1,0:T(8,128)(2,1)S(1)}, bf16[48,8,128]{2,1,0:T(8,128)(2,1)S(1)}, u32[]{:S(2)}, u32[]{:S(2)}) collective-permute-start(bf16[48,8,128]{2,1,0:T(8,128)(2,1)S(1)} %collective-permute-done.3.refs_2_), channel_id=1, source_target_pairs={{0,4},{4,8},{8,12},{12,16},{16,20},{20,24},{24,28},{28,0},{1,5},{5... | collective-permute-start | bytes 294920 | tf_op jit(solution)/shard_map/ppermute | solution.py:252
  76.3 12.5 %collective-permute-start.8 = (bf16[48,8,128]{2,1,0:T(8,128)(2,1)S(1)}, bf16[48,8,128]{2,1,0:T(8,128)(2,1)S(1)}, u32[]{:S(2)}, u32[]{:S(2)}) collective-permute-start(bf16[48,8,128]{2,1,0:T(8,128)(2,1)S(1)} %collective-permute-done.7.refs_6_), channel_id=1, source_target_pairs={{0,28},{4,0},{8,4},{12,8},{16,12},{20,16},{24,20},{28,24},{1,29},{... | collective-permute-start | bytes 294920 | tf_op jit(solution)/shard_map/ppermute | solution.py:252
  88.6 4.7 %collective-permute-start.5 = (bf16[48,8,128]{2,1,0:T(8,128)(2,1)S(1)}, bf16[48,8,128]{2,1,0:T(8,128)(2,1)S(1)}, u32[]{:S(2)}, u32[]{:S(2)}) collective-permute-start(bf16[48,8,128]{2,1,0:T(8,128)(2,1)S(1)} %collective-permute-done.4.refs_3_), channel_id=1, source_target_pairs={{0,4},{4,8},{8,12},{12,16},{16,20},{20,24},{24,28},{28,0},{1,5},{5... | collective-permute-start | bytes 294920 | tf_op jit(solution)/shard_map/ppermute | solution.py:252
  93.3 11.0 %collective-permute-start.15 = (bf16[4,48,8,128]{3,2,1,0:T(8,128)(2,1)S(1)}, bf16[4,48,8,128]{3,2,1,0:T(8,128)(2,1)S(1)}, u32[]{:S(2)}, u32[]{:S(2)}) collective-permute-start(bf16[4,48,8,128]{3,2,1,0:T(8,128)(2,1)S(1)} %get-tuple-element.31.rest_9_), channel_id=1, source_target_pairs={{0,64},{64,128},{128,192},{192,0},{1,65},{65,129},{129,193},{193,1... | collective-permute-start | bytes 1179656 | tf_op jit(solution)/shard_map/ppermute | solution.py:252
  93.6 10.8 %collective-permute-start.18 = (bf16[4,48,8,128]{3,2,1,0:T(8,128)(2,1)S(1)}, bf16[4,48,8,128]{3,2,1,0:T(8,128)(2,1)S(1)}, u32[]{:S(2)}, u32[]{:S(2)}) collective-permute-start(bf16[4,48,8,128]{3,2,1,0:T(8,128)(2,1)S(1)} %get-tuple-element.32.rest_10_), channel_id=1, source_target_pairs={{0,192},{64,0},{128,64},{192,128},{1,193},{65,1},{129,65},{193,129... | collective-permute-start | bytes 1179656 | tf_op jit(solution)/shard_map/ppermute | solution.py:252
  96.2 13.9 %collective-permute-start.17 = (bf16[4,48,8,128]{3,2,1,0:T(8,128)(2,1)S(1)}, bf16[4,48,8,128]{3,2,1,0:T(8,128)(2,1)S(1)}, u32[]{:S(2)}, u32[]{:S(2)}) collective-permute-start(bf16[4,48,8,128]{3,2,1,0:T(8,128)(2,1)S(1)} %get-tuple-element.31.rest_9_), channel_id=1, source_target_pairs={{0,192},{64,0},{128,64},{192,128},{1,193},{65,1},{129,65},{193,129... | collective-permute-start | bytes 1179656 | tf_op jit(solution)/shard_map/ppermute | solution.py:252
  97.5 6.7 %collective-permute-start.11 = (bf16[4,256,128]{2,1,0:T(8,128)(2,1)S(1)}, bf16[4,256,128]{2,1,0:T(8,128)(2,1)}, u32[]{:S(2)}, u32[]{:S(2)}) collective-permute-start(bf16[4,256,128]{2,1,0:T(8,128)(2,1)S(1)} %collective-permute-done.9.rest_3_), channel_id=1, source_target_pairs={{0,4},{4,8},{8,12},{12,16},{16,20},{20,24},{24,28},{28,0},{1,5},{5... | collective-permute-start | bytes 786440 | tf_op jit(solution)/shard_map/ppermute | solution.py:252
  97.5 11.0 %collective-permute-start.12 = (bf16[4,256,128]{2,1,0:T(8,128)(2,1)}, bf16[4,256,128]{2,1,0:T(8,128)(2,1)}, u32[]{:S(2)}, u32[]{:S(2)}) collective-permute-start(bf16[4,256,128]{2,1,0:T(8,128)(2,1)} %collective-permute-done.10.rest_4_), channel_id=1, source_target_pairs={{0,4},{4,8},{8,12},{12,16},{16,20},{20,24},{24,28},{28,64},{64,68}... | collective-permute-start | bytes 786440 | tf_op jit(solution)/shard_map/ppermute | solution.py:264
  104.2 12.1 %collective-permute-start.16 = (bf16[4,48,8,128]{3,2,1,0:T(8,128)(2,1)S(1)}, bf16[4,48,8,128]{3,2,1,0:T(8,128)(2,1)S(1)}, u32[]{:S(2)}, u32[]{:S(2)}) collective-permute-start(bf16[4,48,8,128]{3,2,1,0:T(8,128)(2,1)S(1)} %get-tuple-element.32.rest_10_), channel_id=1, source_target_pairs={{0,64},{64,128},{128,192},{192,0},{1,65},{65,129},{129,193},{193,1... | collective-permute-start | bytes 1179656 | tf_op jit(solution)/shard_map/ppermute | solution.py:252
  104.4 26.0 %collective-permute-start.19 = (bf16[4,48,8,128]{3,2,1,0:T(8,128)(2,1)S(1)}, bf16[4,48,8,128]{3,2,1,0:T(8,128)(2,1)S(1)}, u32[]{:S(2)}, u32[]{:S(2)}) collective-permute-start(bf16[4,48,8,128]{3,2,1,0:T(8,128)(2,1)S(1)} %collective-permute-done.15.rest_11_), channel_id=1, source_target_pairs={{0,64},{64,128},{128,192},{192,0},{1,65},{65,129},{129,193},{193,1... | collective-permute-start | bytes 1179656 | tf_op jit(solution)/shard_map/ppermute | solution.py:252
  104.4 26.0 %collective-permute-start.20 = (bf16[4,48,8,128]{3,2,1,0:T(8,128)(2,1)S(1)}, bf16[4,48,8,128]{3,2,1,0:T(8,128)(2,1)}, u32[]{:S(2)}, u32[]{:S(2)}) collective-permute-start(bf16[4,48,8,128]{3,2,1,0:T(8,128)(2,1)S(1)} %collective-permute-done.18.rest_14_), channel_id=1, source_target_pairs={{0,192},{64,0},{128,64},{192,128},{1,193},{65,1},{129,65},{193,129... | collective-permute-start | bytes 1179656 | tf_op jit(solution)/shard_map/ppermute | solution.py:252
  108.5 7.9 %collective-permute-start.13 = (bf16[4,256,128]{2,1,0:T(8,128)(2,1)}, bf16[4,256,128]{2,1,0:T(8,128)(2,1)}, u32[]{:S(2)}, u32[]{:S(2)}) collective-permute-start(bf16[4,256,128]{2,1,0:T(8,128)(2,1)} %collective-permute-done.11.rest_5_), channel_id=1, source_target_pairs={{0,4},{4,8},{8,12},{12,16},{16,20},{20,24},{24,28},{28,0},{1,5},{5... | collective-permute-start | bytes 786440 | tf_op jit(solution)/shard_map/ppermute | solution.py:252
  110.1 9.0 %collective-permute-start.14 = (bf16[4,256,128]{2,1,0:T(8,128)(2,1)}, bf16[4,256,128]{2,1,0:T(8,128)(2,1)}, u32[]{:S(2)}, u32[]{:S(2)}) collective-permute-start(bf16[4,256,128]{2,1,0:T(8,128)(2,1)} %collective-permute-done.12.rest_6_), channel_id=1, source_target_pairs={{0,4},{4,8},{8,12},{12,16},{16,20},{20,24},{24,28},{28,64},{64,68}... | collective-permute-start | bytes 786440 | tf_op jit(solution)/shard_map/ppermute | solution.py:264
  (22 other events, 591.4 us)

commit v5 on v4

--- a/solution.py
+++ b/solution.py
@@ -30,7 +30,10 @@
 SLICE_ROWS = PAIR_ROWS // SLICES
 PICKS = GROUP * NV
 SLOTS = 1 + NS + NV
-TILES = CORES * WINDOW + PICKS
+CALLS = 2
+HEADS_A_CALL = GROUP // CALLS
+TILES = CORES * WINDOW + HEADS_A_CALL * NV
+COUNTS = (4, 6, SLOTS)
 HALF = CHIPS_Z // 2
 FAR_X = (0, 0, 1, 1, -1, -1, 2, 2)
 FAR_Z = (0, HALF, 0, HALF, 0, HALF, 0, HALF)
@@ -39,13 +42,13 @@
 LOG2_SCALE = float(HEAD_SIZE**-0.5 * np.log2(np.e))
 
 
-def attend_kernel(turns, tile_of, bias_of, spot, q_ref, *rest):
+def attend_kernel(half, turns, tile_of, bias_of, spot, q_ref, *rest):
     near = rest[: 1 + 2 * STEPS]
     far = rest[1 + 2 * STEPS : -3]
     out_ref, tiles, sem = rest[-3:]
-    head = pl.program_id(0)
-
-    @pl.when(head == 0)
+    head = pl.program_id(0) + half * HEADS_A_CALL
+
+    @pl.when(pl.program_id(0) == 0)
     def _():
         copies = []
         for run in range(CORES):
@@ -61,8 +64,9 @@
                 at_x = (x - x_back + CHIPS_X) % CHIPS_X
                 at_z = (z - z_back - n + CHIPS_Z) % CHIPS_Z
                 first = pl.multiple_of((at_x * CHIPS_Z + at_z) * SLICE_ROWS, SLICE_ROWS)
-                target = tiles.at[pl.ds(CORES * WINDOW, PICKS), pl.ds(first, SLICE_ROWS)]
-                copies.append((ref.at[n], target))
+                count = HEADS_A_CALL * NV
+                target = tiles.at[pl.ds(CORES * WINDOW, count), pl.ds(first, SLICE_ROWS)]
+                copies.append((ref.at[n, pl.ds(half * count, count)], target))
         copies = [
             pltpu.make_async_copy(source, target, sem.at[n])
             for n, (source, target) in enumerate(copies)
@@ -96,7 +100,7 @@
         mixed = mixed * (1.0 / total)
         out_ref[block] = mixed.T.astype(jnp.bfloat16)
 
-    for count in range(2, SLOTS + 1, 2):
+    for count in COUNTS:
 
         @pl.when(turns[head] == count)
         def _():
@@ -104,19 +108,21 @@
                 attend(block, count)
 
 
-def attend_all(turns, tile_of, bias_of, spot, q, near, far):
-    head_spec = pl.BlockSpec(
-        (PARTS, BLOCK_TOKENS, HEAD_SIZE), lambda head, *_: (0, 0, head)
-    )
+def attend_half(half, turns, tile_of, bias_of, spot, q, near, far):
+    block = (PARTS, BLOCK_TOKENS, HEAD_SIZE)
+    width = HEADS_A_CALL * HEAD_SIZE
     anywhere = pl.BlockSpec(memory_space=pltpu.HBM)
     return pl.pallas_call(
-        attend_kernel,
-        out_shape=jax.ShapeDtypeStruct(q.shape, jnp.bfloat16),
+        functools.partial(attend_kernel, half),
+        out_shape=jax.ShapeDtypeStruct((PARTS, BLOCK_TOKENS, width), jnp.bfloat16),
         grid_spec=pltpu.PrefetchScalarGridSpec(
             num_scalar_prefetch=4,
-            grid=(GROUP,),
-            in_specs=[head_spec] + [anywhere] * (len(near) + len(far)),
-            out_specs=head_spec,
+            grid=(HEADS_A_CALL,),
+            in_specs=[
+                pl.BlockSpec(block, lambda head, *_: (0, 0, head + half * HEADS_A_CALL))
+            ]
+            + [anywhere] * (len(near) + len(far)),
+            out_specs=pl.BlockSpec(block, lambda head, *_: (0, 0, head)),
             scratch_shapes=[
                 pltpu.VMEM((TILES, PAIR_ROWS, HEAD_SIZE), jnp.bfloat16),
                 pltpu.SemaphoreType.DMA((CORES * (1 + STEPS) + SLICES,)),
@@ -126,7 +132,7 @@
             dimension_semantics=("arbitrary",), vmem_limit_bytes=60 << 20
         ),
         cost_estimate=pl.CostEstimate(
-            flops=4 * 64 * 6 * 128**3, bytes_accessed=10 << 20, transcendentals=64 * 6 * 128**2
+            flops=4 * 32 * 6 * 128**3, bytes_accessed=8 << 20, transcendentals=32 * 6 * 128**2
         ),
         name="attend",
     )(turns, tile_of, bias_of, spot, q, *near, *far)
@@ -151,33 +157,61 @@
     )(keys, values)
 
 
-def move_heads_kernel(merge, from_ref, to_ref, sem):
-    parts, rows = (from_ref, to_ref) if merge else (to_ref, from_ref)
-    count, _, width = parts.shape
-    copies = []
-    for n in range(count):
-        part, columns = parts.at[n], rows.at[:, pl.ds(n * width, width)]
-        ends = (part, columns) if merge else (columns, part)
-        copies.append(pltpu.make_async_copy(*ends, sem.at[n]))
+def split_heads_kernel(rows, parts, sem):
+    width = parts.shape[2]
+    copies = [
+        pltpu.make_async_copy(rows.at[:, pl.ds(n * width, width)], parts.at[n], sem.at[n])
+        for n in range(PARTS)
+    ]
     for copy in copies:
         copy.start()
     for copy in copies:
         copy.wait()
 
 
-def move_heads(array, merge):
-    wide = (BLOCK_TOKENS, array.size // BLOCK_TOKENS)
-    split = (PARTS, BLOCK_TOKENS, wide[1] // PARTS)
-    return pl.pallas_call(
-        functools.partial(move_heads_kernel, merge),
-        out_shape=jax.ShapeDtypeStruct(wide if merge else split, array.dtype),
-        in_specs=[pl.BlockSpec(memory_space=pltpu.VMEM if merge else pltpu.HBM)],
-        out_specs=pl.BlockSpec(memory_space=pltpu.HBM if merge else pltpu.VMEM),
+def split_heads(rows):
+    return pl.pallas_call(
+        split_heads_kernel,
+        out_shape=jax.ShapeDtypeStruct(
+            (PARTS, BLOCK_TOKENS, rows.shape[1] // PARTS), rows.dtype
+        ),
+        in_specs=[pl.BlockSpec(memory_space=pltpu.HBM)],
+        out_specs=pl.BlockSpec(memory_space=pltpu.VMEM),
         scratch_shapes=[pltpu.SemaphoreType.DMA((PARTS,))],
         cost_estimate=pl.CostEstimate(flops=0, bytes_accessed=4 << 20, transcendentals=0),
         compiler_params=pltpu.CompilerParams(vmem_limit_bytes=8 << 20),
-        name="merge_heads" if merge else "split_heads",
-    )(array)
+        name="split_heads",
+    )(rows)
+
+
+def merge_heads_kernel(*refs):
+    halves, rows, sem = refs[:CALLS], refs[CALLS], refs[CALLS + 1]
+    width = halves[0].shape[2]
+    copies = []
+    for n in range(PARTS):
+        for half, parts in enumerate(halves):
+            place = n * CALLS + half
+            columns = rows.at[:, pl.ds(place * width, width)]
+            copies.append(pltpu.make_async_copy(parts.at[n], columns, sem.at[place]))
+    for copy in copies:
+        copy.start()
+    for copy in copies:
+        copy.wait()
+
+
+def merge_heads(*halves):
+    return pl.pallas_call(
+        merge_heads_kernel,
+        out_shape=jax.ShapeDtypeStruct(
+            (BLOCK_TOKENS, QUERY_HEADS * HEAD_SIZE), halves[0].dtype
+        ),
+        in_specs=[pl.BlockSpec(memory_space=pltpu.VMEM)] * CALLS,
+        out_specs=pl.BlockSpec(memory_space=pltpu.HBM),
+        scratch_shapes=[pltpu.SemaphoreType.DMA((PARTS * CALLS,))],
+        cost_estimate=pl.CostEstimate(flops=0, bytes_accessed=4 << 20, transcendentals=0),
+        compiler_params=pltpu.CompilerParams(vmem_limit_bytes=8 << 20),
+        name="merge_heads",
+    )(*halves)
 
 
 def stack_kernel(*refs):
@@ -201,7 +235,9 @@
     slash_count = jnp.sum((slash >= 1).astype(jnp.int32), axis=1)
     vert_count = jnp.sum((vert >= 0).astype(jnp.int32), axis=1)
     turns = 1 + slash_count + vert_count
-    turns = (turns + 1) // 2 * 2
+    turns = sum(
+        jnp.where(turns > low, high - low, 0) for low, high in zip((0, *COUNTS), COUNTS)
+    )
     part = np.arange(PARTS)
     numbers = first_blocks[part // ROW] + (part % ROW)
     own = jnp.asarray(part // ROW * WINDOW + SPAN + part % ROW, jnp.int32)
@@ -212,7 +248,8 @@
     held_in = jnp.where(z < back, CORES - 1 - run, run)
     near_tile = held_in * WINDOW + inside
     near_ok = (slash[:, None, :] >= 1) & (numbers[None, :, None] >= slash[:, None, :])
-    far_tile = CORES * WINDOW + np.arange(PICKS, dtype=np.int32).reshape(GROUP, 1, NV)
+    far_tile = np.arange(PICKS, dtype=np.int32).reshape(GROUP, 1, NV) % (HEADS_A_CALL * NV)
+    far_tile = CORES * WINDOW + far_tile
     far_tile = jnp.broadcast_to(far_tile, (GROUP, PARTS, NV))
     hit = jnp.any(
         near_ok[:, :, :, None]
@@ -265,8 +302,6 @@
 
     sliced = pairs.reshape(PARTS, SLICES, SLICE_ROWS, HEAD_SIZE).transpose(1, 0, 2, 3)
     sliced = lax.all_to_all(sliced, ROW_AXES, 0, 0, tiled=True)
-    one = passed_on(own[0], own[1])
-    two = passed_on(*one)
     vert = lax.dynamic_slice_in_dim(vert_blocks, key_head * GROUP, GROUP, 0)
     slash = lax.dynamic_slice_in_dim(slash_offsets, key_head * GROUP, GROUP, 0)
     listed = jnp.maximum(vert, 0).reshape(-1)
@@ -274,16 +309,17 @@
     at = (at_run // CORES * CHIPS_Z + at_z) * PARTS + at_run % CORES * ROW + place
     picked = sliced.reshape(SLICES * PARTS, SLICE_ROWS, HEAD_SIZE)[at]
 
-    queries = move_heads(queries, False)
-    queries, picked = lax.optimization_barrier((queries, picked))
+    queries = split_heads(queries)
     q = lax.all_to_all(queries, HEAD_AXES, 0, 0, tiled=True)
 
-    ahead, behind = [], []
-    for n in range(HALF):
-        behind += [shifted(behind[-1] if n else picked, "z", 1)]
-        if n < HALF - 1:
-            ahead += [shifted(ahead[-1] if n else picked, "z", -1)]
-    column = [picked] + behind + ahead[::-1]
+    behind = shifted(picked, "z", 1)
+    ahead = [picked]
+    for _ in range(CHIPS_Z - 2):
+        ahead += [shifted(ahead[-1], "z", -1)]
+    column = [picked, behind] + ahead[:0:-1]
+    first, second, behind = lax.optimization_barrier((own[0], own[1], behind))
+    one = passed_on(first, second)
+    two = passed_on(*one)
     column, two = lax.optimization_barrier((column, two))
     lower, upper = stack_halves(column)
     three = passed_on(*two)
@@ -297,10 +333,11 @@
     first_blocks = ((x * CORES + runs) * CHIPS_Z + z) * ROW
     turns, tile_of, bias_of = slot_tables(vert, slash, first_blocks, z)
     spot = jnp.stack([x, z]).astype(jnp.int32)
-    mixed = attend_all(turns, tile_of, bias_of, spot, q, near, far)
-
-    returned = lax.all_to_all(mixed, HEAD_AXES, 0, 0, tiled=True)
-    return move_heads(returned, True)
+    returned = []
+    for half in range(CALLS):
+        mixed = attend_half(half, turns, tile_of, bias_of, spot, q, near, far)
+        returned += [lax.all_to_all(mixed, HEAD_AXES, 0, 0, tiled=True)]
+    return merge_heads(*returned)
 
 
 def solution(mesh):

time: 190 us -> 184 us (0.968)
  starting transfers between devices: 44.1 us -> 58.8 us
  blocking collectives: 32.6 us -> 21.5 us
  waiting for transfers between devices: 74.8 us -> 65.2 us
    ppermute x17, waiting for transfers between devices: 50.5 us -> 35.9 us  [shifted(): lax.ppermute(value, axis, [(n, (n + by) % count) for n in range(count)])]
    all_to_all x1, blocking collectives: 32.6 us -> 21.5 us  [shards(): returned += [lax.all_to_all(mixed, HEAD_AXES, 0, 0, tiled=True)]]
    all_to_all x0 -> x1, starting transfers between devices: none -> 10.8 us  [shards(): returned += [lax.all_to_all(mixed, HEAD_AXES, 0, 0, tiled=True)]]
    ppermute x17, starting transfers between devices: 16.5 us -> 21.8 us  [shifted(): lax.ppermute(value, axis, [(n, (n + by) % count) for n in range(count)])]
    ppermute x4, waiting for transfers between devices: 3.96 us -> 6.97 us  [passed_on(): return (shifted(first, 'z', 1), lax.ppermute(second, ROW_AXES, onward))]
    all_to_all x0 -> x1, waiting for transfers between devices: none -> 1.94 us  [shards(): returned += [lax.all_to_all(mixed, HEAD_AXES, 0, 0, tiled=True)]]
    pallas_call x3 -> x4, Pallas kernels: 26 us -> 27.7 us  [the longest x2 24.7 us: attend_half(): pl.pallas_call(functools.partial(attend_kernel, half), out_shape=jax.Shap...]
  transfers between devices with their start and end apart: 24 -> 25, of which waited for: 13 -> 14; matrix products, arithmetic and copies ran while one was open for 3% -> 3% of each run, Pallas kernels for 1% -> 8%
where the time goes in v5:
time: 184 us
  waiting for transfers between devices  65.2 us (35%)
  starting transfers between devices  58.8 us (32%)
  Pallas kernels  28.7 us (16%)
  blocking collectives  21.5 us (12%)
  local copies, waits for them, and re-layouts  7.01 us (4%)
  other arithmetic  2.47 us (1%)
    ppermute x17, waiting for transfers between devices, shifted(): lax.ppermute(value, axis, [(n, (n + by) % count) for n in range(count)])  35.9 us
    pallas_call x2, Pallas kernels, attend_half(): pl.pallas_call(functools.partial(attend_kernel, half), out_shape=jax.Shap...  24.7 us
    ppermute x17, starting transfers between devices, shifted(): lax.ppermute(value, axis, [(n, (n + by) % count) for n in range(count)])  21.8 us
    all_to_all x1, blocking collectives, shards(): returned += [lax.all_to_all(mixed, HEAD_AXES, 0, 0, tiled=True)]  21.5 us
    all_to_all x1, waiting for transfers between devices, shards(): sliced = lax.all_to_all(sliced, ROW_AXES, 0, 0, tiled=True)  11.3 us
    all_to_all x1, starting transfers between devices, shards(): returned += [lax.all_to_all(mixed, HEAD_AXES, 0, 0, tiled=True)]  10.8 us
    all_to_all x1, starting transfers between devices, shards(): sliced = lax.all_to_all(sliced, ROW_AXES, 0, 0, tiled=True)  10.3 us
    all_to_all x1, waiting for transfers between devices, shards(): pairs = lax.all_to_all(pairs, HEAD_AXES, 0, 0, tiled=True)  9.06 us
  transfers between devices with their start and end apart: 25, of which 14 were waited for; matrix products, arithmetic and copies ran while one was open for 3% of the time, Pallas kernels for 8%

profile of v5, /device:TPU:1, one launch (start us, length us, event | category | flops | bytes accessed | tf_op | source)
XLA Modules:
  0.0 184.2 jit_solution(10761638885279962425)
XLA Ops:
  2.8 6.7 %all-to-all-start.1 = ((bf16[8,256,128]{2,1,0:T(8,128)(2,1)}), bf16[8,256,128]{2,1,0:T(8,128)(2,1)S(1)}, u32[]{:S(2)}, u32[]{:S(2)}) async-start(bf16[8,256,128]{2,1,0:T(8,128)(2,1)} %split_pairs.1), calls=%async_computation.1 | async-start | bytes 1048576 | tf_op jit(solution)/shard_map/all_to_all | solution.py:292
  9.8 9.1 %all-to-all-done.1 = bf16[8,256,128]{2,1,0:T(8,128)(2,1)S(1)} async-done(((bf16[8,256,128]{2,1,0:T(8,128)(2,1)}), bf16[8,256,128]{2,1,0:T(8,128)(2,1)S(1)}, u32[]{:S(2)}, u32[]{:S(2)}) %all-to-all-start.1) | async-done | bytes 524320 | tf_op jit(solution)/shard_map/all_to_all | solution.py:292
  19.8 10.3 %all-to-all-start.2 = ((bf16[32,8,8,128]{3,2,1,0:T(8,128)(2,1)}), bf16[32,8,8,128]{3,2,1,0:T(8,128)(2,1)S(1)}, u32[]{:S(2)}, u32[]{:S(2)}) async-start(bf16[32,8,8,128]{3,2,1,0:T(8,128)(2,1)} %copy_bitcast_fusion), calls=%async_computation.2 | async-start | bytes 1048576 | tf_op jit(solution)/shard_map/all_to_all | solution.py:304
  33.0 11.3 %all-to-all-done.2 = bf16[32,8,8,128]{3,2,1,0:T(8,128)(2,1)S(1)} async-done(((bf16[32,8,8,128]{3,2,1,0:T(8,128)(2,1)}), bf16[32,8,8,128]{3,2,1,0:T(8,128)(2,1)S(1)}, u32[]{:S(2)}, u32[]{:S(2)}) %all-to-all-start.2) | async-done | bytes 524320 | tf_op jit(solution)/shard_map/all_to_all | solution.py:304
  44.3 7.8 %all-to-all-start = ((bf16[8,128,1024]{2,1,0:T(8,128)(2,1)}), bf16[8,128,1024]{2,1,0:T(8,128)(2,1)}, u32[]{:S(2)}, u32[]{:S(2)}) async-start(bf16[8,128,1024]{2,1,0:T(8,128)(2,1)} %split_heads.1), calls=%async_computation | async-start | bytes 4194304 | tf_op jit(solution)/shard_map/all_to_all | solution.py:313
  55.3 3.0 %collective-permute-done.3.refs_7_ = bf16[48,8,128]{2,1,0:T(8,128)(2,1)S(1)} collective-permute-done((bf16[48,8,128]{2,1,0:T(8,128)(2,1)S(1)}, bf16[48,8,128]{2,1,0:T(8,128)(2,1)S(1)}, u32[]{:S(2)}, u32[]{:S(2)}) %collective-permute-start.3) | collective-permute-done | bytes 98336 | tf_op jit(solution)/shard_map/ppermute | solution.py:289
  62.2 2.4 %collective-permute-start.5 = (bf16[48,8,128]{2,1,0:T(8,128)(2,1)S(1)}, bf16[48,8,128]{2,1,0:T(8,128)(2,1)S(1)}, u32[]{:S(2)}, u32[]{:S(2)}) collective-permute-start(bf16[48,8,128]{2,1,0:T(8,128)(2,1)S(1)} %collective-permute-done.4.refs_6_), channel_id=1, source_target_pairs={{0,28},{4,0},{8,4},{12,8},{16,12},{20,16},{24,20},{28,24},{1,29},{... | collective-permute-start | bytes 294920 | tf_op jit(solution)/shard_map/ppermute | solution.py:289
  66.2 3.4 %collective-permute-start.6 = (bf16[48,8,128]{2,1,0:T(8,128)(2,1)S(1)}, bf16[48,8,128]{2,1,0:T(8,128)(2,1)S(1)}, u32[]{:S(2)}, u32[]{:S(2)}) collective-permute-start(bf16[48,8,128]{2,1,0:T(8,128)(2,1)S(1)} %collective-permute-done.5.refs_5_), channel_id=1, source_target_pairs={{0,28},{4,0},{8,4},{12,8},{16,12},{20,16},{24,20},{28,24},{1,29},{... | collective-permute-start | bytes 294920 | tf_op jit(solution)/shard_map/ppermute | solution.py:289
  69.9 4.7 %collective-permute-done.2.rest_2_ = bf16[4,256,128]{2,1,0:T(8,128)(2,1)S(1)} collective-permute-done((bf16[4,256,128]{2,1,0:T(8,128)(2,1)S(1)}, bf16[4,256,128]{2,1,0:T(8,128)(2,1)S(1)}, u32[]{:S(2)}, u32[]{:S(2)}) %collective-permute-start.2) | collective-permute-done | bytes 262176 | tf_op jit(solution)/shard_map/ppermute | solution.py:301
  74.6 2.1 %collective-permute-start.7 = (bf16[48,8,128]{2,1,0:T(8,128)(2,1)S(1)}, bf16[48,8,128]{2,1,0:T(8,128)(2,1)S(1)}, u32[]{:S(2)}, u32[]{:S(2)}) collective-permute-start(bf16[48,8,128]{2,1,0:T(8,128)(2,1)S(1)} %collective-permute-done.6.refs_4_), channel_id=1, source_target_pairs={{0,28},{4,0},{8,4},{12,8},{16,12},{20,16},{24,20},{28,24},{1,29},{... | collective-permute-start | bytes 294920 | tf_op jit(solution)/shard_map/ppermute | solution.py:289
  76.8 1.6 collective-permute-done.7.refs_3_
  78.5 2.9 %collective-permute-start.8 = (bf16[48,8,128]{2,1,0:T(8,128)(2,1)S(1)}, bf16[48,8,128]{2,1,0:T(8,128)(2,1)S(1)}, u32[]{:S(2)}, u32[]{:S(2)}) collective-permute-start(bf16[48,8,128]{2,1,0:T(8,128)(2,1)S(1)} %collective-permute-done.7.refs_3_), channel_id=1, source_target_pairs={{0,28},{4,0},{8,4},{12,8},{16,12},{20,16},{24,20},{28,24},{1,29},{... | collective-permute-start | bytes 294920 | tf_op jit(solution)/shard_map/ppermute | solution.py:289
  83.1 2.2 %collective-permute-done.10.rest_4_ = bf16[4,256,128]{2,1,0:T(8,128)(2,1)} collective-permute-done((bf16[4,256,128]{2,1,0:T(8,128)(2,1)S(1)}, bf16[4,256,128]{2,1,0:T(8,128)(2,1)}, u32[]{:S(2)}, u32[]{:S(2)}) %collective-permute-start.10) | collective-permute-done | bytes 262176 | tf_op jit(solution)/shard_map/ppermute | solution.py:301
  85.5 2.6 %collective-permute-start.18 = (bf16[4,48,8,128]{3,2,1,0:T(8,128)(2,1)S(1)}, bf16[4,48,8,128]{3,2,1,0:T(8,128)(2,1)S(1)}, u32[]{:S(2)}, u32[]{:S(2)}) collective-permute-start(bf16[4,48,8,128]{3,2,1,0:T(8,128)(2,1)S(1)} %get-tuple-element.32.rest_10_), channel_id=1, source_target_pairs={{0,192},{64,0},{128,64},{192,128},{1,193},{65,1},{129,65},{193,129... | collective-permute-start | bytes 1179656 | tf_op jit(solution)/shard_map/ppermute | solution.py:289
  88.9 6.3 %collective-permute-done.11.rest_5_ = bf16[4,256,128]{2,1,0:T(8,128)(2,1)S(1)} collective-permute-done((bf16[4,256,128]{2,1,0:T(8,128)(2,1)S(1)}, bf16[4,256,128]{2,1,0:T(8,128)(2,1)S(1)}, u32[]{:S(2)}, u32[]{:S(2)}) %collective-permute-start.11) | collective-permute-done | bytes 262176 | tf_op jit(solution)/shard_map/ppermute | solution.py:289
  96.4 2.6 %collective-permute-start.20 = (bf16[4,48,8,128]{3,2,1,0:T(8,128)(2,1)S(1)}, bf16[4,48,8,128]{3,2,1,0:T(8,128)(2,1)S(1)}, u32[]{:S(2)}, u32[]{:S(2)}) collective-permute-start(bf16[4,48,8,128]{3,2,1,0:T(8,128)(2,1)S(1)} %collective-permute-done.18.rest_14_), channel_id=1, source_target_pairs={{0,192},{64,0},{128,64},{192,128},{1,193},{65,1},{129,65},{193,129... | collective-permute-start | bytes 1179656 | tf_op jit(solution)/shard_map/ppermute | solution.py:289
  99.3 2.2 %collective-permute-done.17.rest_13_ = bf16[4,48,8,128]{3,2,1,0:T(8,128)(2,1)S(1)} collective-permute-done((bf16[4,48,8,128]{3,2,1,0:T(8,128)(2,1)S(1)}, bf16[4,48,8,128]{3,2,1,0:T(8,128)(2,1)S(1)}, u32[]{:S(2)}, u32[]{:S(2)}) %collective-permute-start.17) | collective-permute-done | bytes 393248 | tf_op jit(solution)/shard_map/ppermute | solution.py:289
  104.1 7.4 %collective-permute-done.16.rest_12_ = bf16[4,48,8,128]{3,2,1,0:T(8,128)(2,1)S(1)} collective-permute-done((bf16[4,48,8,128]{3,2,1,0:T(8,128)(2,1)S(1)}, bf16[4,48,8,128]{3,2,1,0:T(8,128)(2,1)S(1)}, u32[]{:S(2)}, u32[]{:S(2)}) %collective-permute-start.16) | collective-permute-done | bytes 393248 | tf_op jit(solution)/shard_map/ppermute | solution.py:289
  111.5 11.2 %collective-permute-done.19.rest_15_ = bf16[4,48,8,128]{3,2,1,0:T(8,128)(2,1)S(1)} collective-permute-done((bf16[4,48,8,128]{3,2,1,0:T(8,128)(2,1)S(1)}, bf16[4,48,8,128]{3,2,1,0:T(8,128)(2,1)S(1)}, u32[]{:S(2)}, u32[]{:S(2)}) %collective-permute-start.19) | collective-permute-done | bytes 393248 | tf_op jit(solution)/shard_map/ppermute | solution.py:289
  123.6 11.7 %attend.2 = bf16[8,128,512]{2,1,0:T(8,128)(2,1)} custom-call(s32[8]{0:T(128)} %fusion.9.turns, s32[640]{0:T(1024)} %reshape.329.tile_of, f32[640]{0:T(1024)} %select_n.125.bias_of, s32[2]{0:T(128)} %pad_add_fusion.3.spot, bf16[8,128,1024]{2,1,0:T(8,128)(2,1)} %all-to-all-done.q_ref, bf16[2,4,256,128]{3,2,1,0:T(8,128)(2,1)} %bitcast.13, ...), custom_call_target="tpu_custom_call" | custom-call | flops 1610612736 | bytes 8388608 | tf_op jit(solution)/shard_map/attend/pallas_call | solution.py:115
  135.3 10.8 %all-to-all-start.3 = ((bf16[8,128,512]{2,1,0:T(8,128)(2,1)}), bf16[8,128,512]{2,1,0:T(8,128)(2,1)S(1)}, u32[]{:S(2)}, u32[]{:S(2)}) async-start(bf16[8,128,512]{2,1,0:T(8,128)(2,1)} %attend.2), calls=%async_computation.3 | async-start | bytes 2097152 | tf_op jit(solution)/shard_map/all_to_all | solution.py:339
  146.1 13.0 %attend.3 = bf16[8,128,512]{2,1,0:T(8,128)(2,1)} custom-call(s32[8]{0:T(128)} %fusion.9.turns, s32[640]{0:T(1024)} %reshape.329.tile_of, f32[640]{0:T(1024)} %select_n.125.bias_of, s32[2]{0:T(128)} %pad_add_fusion.3.spot, bf16[8,128,1024]{2,1,0:T(8,128)(2,1)} %all-to-all-done.q_ref, bf16[2,4,256,128]{3,2,1,0:T(8,128)(2,1)} %bitcast.14, ...), custom_call_target="tpu_custom_call" | custom-call | flops 1610612736 | bytes 8388608 | tf_op jit(solution)/shard_map/attend/pallas_call | solution.py:115
  159.1 1.9 %all-to-all-done.3.refs_0_ = bf16[8,128,512]{2,1,0:T(8,128)(2,1)S(1)} async-done(((bf16[8,128,512]{2,1,0:T(8,128)(2,1)}), bf16[8,128,512]{2,1,0:T(8,128)(2,1)S(1)}, u32[]{:S(2)}, u32[]{:S(2)}) %all-to-all-start.3) | async-done | bytes 1048608 | tf_op jit(solution)/shard_map/all_to_all | solution.py:339
  161.1 21.5 %all_to_all.25.refs_1_ = bf16[8,128,512]{2,1,0:T(8,128)(2,1)S(1)} all-to-all(bf16[8,128,512]{2,1,0:T(8,128)(2,1)} %attend.3), channel_id=1, replica_groups=mesh['x'=4,'c'=2,'z'=8,'y'=4] {'c','y'}, dimensions={0} | all-to-all | bytes 2097152 | tf_op jit(solution)/shard_map/all_to_all | solution.py:339
  (121 shorter events, 24.7 us)
Async XLA Ops:
  2.8 16.0 %all-to-all-start.1 = ((bf16[8,256,128]{2,1,0:T(8,128)(2,1)}), bf16[8,256,128]{2,1,0:T(8,128)(2,1)S(1)}, u32[]{:S(2)}, u32[]{:S(2)}) async-start(bf16[8,256,128]{2,1,0:T(8,128)(2,1)} %split_pairs.1), calls=%async_computation.1 | async-start | bytes 1048576 | tf_op jit(solution)/shard_map/all_to_all | solution.py:292
  19.8 24.5 %all-to-all-start.2 = ((bf16[32,8,8,128]{3,2,1,0:T(8,128)(2,1)}), bf16[32,8,8,128]{3,2,1,0:T(8,128)(2,1)S(1)}, u32[]{:S(2)}, u32[]{:S(2)}) async-start(bf16[32,8,8,128]{3,2,1,0:T(8,128)(2,1)} %copy_bitcast_fusion), calls=%async_computation.2 | async-start | bytes 1048576 | tf_op jit(solution)/shard_map/all_to_all | solution.py:304
  44.3 59.8 %all-to-all-start = ((bf16[8,128,1024]{2,1,0:T(8,128)(2,1)}), bf16[8,128,1024]{2,1,0:T(8,128)(2,1)}, u32[]{:S(2)}, u32[]{:S(2)}) async-start(bf16[8,128,1024]{2,1,0:T(8,128)(2,1)} %split_heads.1), calls=%async_computation | async-start | bytes 4194304 | tf_op jit(solution)/shard_map/all_to_all | solution.py:313
  52.7 5.6 %collective-permute-start.3 = (bf16[48,8,128]{2,1,0:T(8,128)(2,1)S(1)}, bf16[48,8,128]{2,1,0:T(8,128)(2,1)S(1)}, u32[]{:S(2)}, u32[]{:S(2)}) collective-permute-start(bf16[48,8,128]{2,1,0:T(8,128)(2,1)S(1)} %gather_fusion.1), channel_id=1, source_target_pairs={{0,28},{4,0},{8,4},{12,8},{16,12},{20,16},{24,20},{28,24},{1,29},{... | collective-permute-start | bytes 294920 | tf_op jit(solution)/shard_map/ppermute | solution.py:289
  54.0 5.5 %collective-permute-start = (bf16[48,8,128]{2,1,0:T(8,128)(2,1)S(1)}, bf16[48,8,128]{2,1,0:T(8,128)(2,1)S(1)}, u32[]{:S(2)}, u32[]{:S(2)}) collective-permute-start(bf16[48,8,128]{2,1,0:T(8,128)(2,1)S(1)} %gather_fusion.1), channel_id=1, source_target_pairs={{0,4},{4,8},{8,12},{12,16},{16,20},{20,24},{24,28},{28,0},{1,5},{5... | collective-permute-start | bytes 294920 | tf_op jit(solution)/shard_map/ppermute | solution.py:289
  58.4 3.9 %collective-permute-start.4 = (bf16[48,8,128]{2,1,0:T(8,128)(2,1)S(1)}, bf16[48,8,128]{2,1,0:T(8,128)(2,1)S(1)}, u32[]{:S(2)}, u32[]{:S(2)}) collective-permute-start(bf16[48,8,128]{2,1,0:T(8,128)(2,1)S(1)} %collective-permute-done.3.refs_7_), channel_id=1, source_target_pairs={{0,28},{4,0},{8,4},{12,8},{16,12},{20,16},{24,20},{28,24},{1,29},{... | collective-permute-start | bytes 294920 | tf_op jit(solution)/shard_map/ppermute | solution.py:289
  59.6 10.2 %collective-permute-start.1 = (bf16[4,256,128]{2,1,0:T(8,128)(2,1)S(1)}, bf16[4,256,128]{2,1,0:T(8,128)(2,1)S(1)}, u32[]{:S(2)}, u32[]{:S(2)}) collective-permute-start(bf16[4,256,128]{2,1,0:T(8,128)(2,1)S(1)} %get-tuple-element.19), channel_id=1, source_target_pairs={{0,4},{4,8},{8,12},{12,16},{16,20},{20,24},{24,28},{28,0},{1,5},{5... | collective-permute-start | bytes 786440 | tf_op jit(solution)/shard_map/ppermute | solution.py:289
  60.0 14.7 %collective-permute-start.2 = (bf16[4,256,128]{2,1,0:T(8,128)(2,1)S(1)}, bf16[4,256,128]{2,1,0:T(8,128)(2,1)S(1)}, u32[]{:S(2)}, u32[]{:S(2)}) collective-permute-start(bf16[4,256,128]{2,1,0:T(8,128)(2,1)S(1)} %get-tuple-element.20), channel_id=1, source_target_pairs={{0,4},{4,8},{8,12},{12,16},{16,20},{20,24},{24,28},{28,64},{64,68}... | collective-permute-start | bytes 786440 | tf_op jit(solution)/shard_map/ppermute | solution.py:301
  62.2 4.0 %collective-permute-start.5 = (bf16[48,8,128]{2,1,0:T(8,128)(2,1)S(1)}, bf16[48,8,128]{2,1,0:T(8,128)(2,1)S(1)}, u32[]{:S(2)}, u32[]{:S(2)}) collective-permute-start(bf16[48,8,128]{2,1,0:T(8,128)(2,1)S(1)} %collective-permute-done.4.refs_6_), channel_id=1, source_target_pairs={{0,28},{4,0},{8,4},{12,8},{16,12},{20,16},{24,20},{28,24},{1,29},{... | collective-permute-start | bytes 294920 | tf_op jit(solution)/shard_map/ppermute | solution.py:289
  66.2 8.4 %collective-permute-start.6 = (bf16[48,8,128]{2,1,0:T(8,128)(2,1)S(1)}, bf16[48,8,128]{2,1,0:T(8,128)(2,1)S(1)}, u32[]{:S(2)}, u32[]{:S(2)}) collective-permute-start(bf16[48,8,128]{2,1,0:T(8,128)(2,1)S(1)} %collective-permute-done.5.refs_5_), channel_id=1, source_target_pairs={{0,28},{4,0},{8,4},{12,8},{16,12},{20,16},{24,20},{28,24},{1,29},{... | collective-permute-start | bytes 294920 | tf_op jit(solution)/shard_map/ppermute | solution.py:289
  69.8 13.3 %collective-permute-start.9 = (bf16[4,256,128]{2,1,0:T(8,128)(2,1)S(1)}, bf16[4,256,128]{2,1,0:T(8,128)(2,1)S(1)}, u32[]{:S(2)}, u32[]{:S(2)}) collective-permute-start(bf16[4,256,128]{2,1,0:T(8,128)(2,1)S(1)} %collective-permute-done.1.rest_1_), channel_id=1, source_target_pairs={{0,4},{4,8},{8,12},{12,16},{16,20},{20,24},{24,28},{28,0},{1,5},{5... | collective-permute-start | bytes 786440 | tf_op jit(solution)/shard_map/ppermute | solution.py:289
  74.6 10.7 %collective-permute-start.10 = (bf16[4,256,128]{2,1,0:T(8,128)(2,1)S(1)}, bf16[4,256,128]{2,1,0:T(8,128)(2,1)}, u32[]{:S(2)}, u32[]{:S(2)}) collective-permute-start(bf16[4,256,128]{2,1,0:T(8,128)(2,1)S(1)} %collective-permute-done.2.rest_2_), channel_id=1, source_target_pairs={{0,4},{4,8},{8,12},{12,16},{16,20},{20,24},{24,28},{28,64},{64,68}... | collective-permute-start | bytes 786440 | tf_op jit(solution)/shard_map/ppermute | solution.py:301
  78.5 4.6 %collective-permute-start.8 = (bf16[48,8,128]{2,1,0:T(8,128)(2,1)S(1)}, bf16[48,8,128]{2,1,0:T(8,128)(2,1)S(1)}, u32[]{:S(2)}, u32[]{:S(2)}) collective-permute-start(bf16[48,8,128]{2,1,0:T(8,128)(2,1)S(1)} %collective-permute-done.7.refs_3_), channel_id=1, source_target_pairs={{0,28},{4,0},{8,4},{12,8},{16,12},{20,16},{24,20},{28,24},{1,29},{... | collective-permute-start | bytes 294920 | tf_op jit(solution)/shard_map/ppermute | solution.py:289
  85.4 10.9 %collective-permute-start.15 = (bf16[4,48,8,128]{3,2,1,0:T(8,128)(2,1)S(1)}, bf16[4,48,8,128]{3,2,1,0:T(8,128)(2,1)S(1)}, u32[]{:S(2)}, u32[]{:S(2)}) collective-permute-start(bf16[4,48,8,128]{3,2,1,0:T(8,128)(2,1)S(1)} %get-tuple-element.31.rest_9_), channel_id=1, source_target_pairs={{0,64},{64,128},{128,192},{192,0},{1,65},{65,129},{129,193},{193,1... | collective-permute-start | bytes 1179656 | tf_op jit(solution)/shard_map/ppermute | solution.py:289
  85.5 10.9 %collective-permute-start.18 = (bf16[4,48,8,128]{3,2,1,0:T(8,128)(2,1)S(1)}, bf16[4,48,8,128]{3,2,1,0:T(8,128)(2,1)S(1)}, u32[]{:S(2)}, u32[]{:S(2)}) collective-permute-start(bf16[4,48,8,128]{3,2,1,0:T(8,128)(2,1)S(1)} %get-tuple-element.32.rest_10_), channel_id=1, source_target_pairs={{0,192},{64,0},{128,64},{192,128},{1,193},{65,1},{129,65},{193,129... | collective-permute-start | bytes 1179656 | tf_op jit(solution)/shard_map/ppermute | solution.py:289
  88.2 13.2 %collective-permute-start.17 = (bf16[4,48,8,128]{3,2,1,0:T(8,128)(2,1)S(1)}, bf16[4,48,8,128]{3,2,1,0:T(8,128)(2,1)S(1)}, u32[]{:S(2)}, u32[]{:S(2)}) collective-permute-start(bf16[4,48,8,128]{3,2,1,0:T(8,128)(2,1)S(1)} %get-tuple-element.31.rest_9_), channel_id=1, source_target_pairs={{0,192},{64,0},{128,64},{192,128},{1,193},{65,1},{129,65},{193,129... | collective-permute-start | bytes 1179656 | tf_op jit(solution)/shard_map/ppermute | solution.py:289
  88.4 6.8 %collective-permute-start.11 = (bf16[4,256,128]{2,1,0:T(8,128)(2,1)S(1)}, bf16[4,256,128]{2,1,0:T(8,128)(2,1)S(1)}, u32[]{:S(2)}, u32[]{:S(2)}) collective-permute-start(bf16[4,256,128]{2,1,0:T(8,128)(2,1)S(1)} %collective-permute-done.9.rest_3_), channel_id=1, source_target_pairs={{0,4},{4,8},{8,12},{12,16},{16,20},{20,24},{24,28},{28,0},{1,5},{5... | collective-permute-start | bytes 786440 | tf_op jit(solution)/shard_map/ppermute | solution.py:289
  88.5 10.6 %collective-permute-start.12 = (bf16[4,256,128]{2,1,0:T(8,128)(2,1)}, bf16[4,256,128]{2,1,0:T(8,128)(2,1)}, u32[]{:S(2)}, u32[]{:S(2)}) collective-permute-start(bf16[4,256,128]{2,1,0:T(8,128)(2,1)} %collective-permute-done.10.rest_4_), channel_id=1, source_target_pairs={{0,4},{4,8},{8,12},{12,16},{16,20},{20,24},{24,28},{28,64},{64,68}... | collective-permute-start | bytes 786440 | tf_op jit(solution)/shard_map/ppermute | solution.py:301
  95.2 16.3 %collective-permute-start.16 = (bf16[4,48,8,128]{3,2,1,0:T(8,128)(2,1)S(1)}, bf16[4,48,8,128]{3,2,1,0:T(8,128)(2,1)S(1)}, u32[]{:S(2)}, u32[]{:S(2)}) collective-permute-start(bf16[4,48,8,128]{3,2,1,0:T(8,128)(2,1)S(1)} %get-tuple-element.32.rest_10_), channel_id=1, source_target_pairs={{0,64},{64,128},{128,192},{192,0},{1,65},{65,129},{129,193},{193,1... | collective-permute-start | bytes 1179656 | tf_op jit(solution)/shard_map/ppermute | solution.py:289
  96.3 26.4 %collective-permute-start.19 = (bf16[4,48,8,128]{3,2,1,0:T(8,128)(2,1)S(1)}, bf16[4,48,8,128]{3,2,1,0:T(8,128)(2,1)S(1)}, u32[]{:S(2)}, u32[]{:S(2)}) collective-permute-start(bf16[4,48,8,128]{3,2,1,0:T(8,128)(2,1)S(1)} %collective-permute-done.15.rest_11_), channel_id=1, source_target_pairs={{0,64},{64,128},{128,192},{192,0},{1,65},{65,129},{129,193},{193,1... | collective-permute-start | bytes 1179656 | tf_op jit(solution)/shard_map/ppermute | solution.py:289
  96.4 26.3 %collective-permute-start.20 = (bf16[4,48,8,128]{3,2,1,0:T(8,128)(2,1)S(1)}, bf16[4,48,8,128]{3,2,1,0:T(8,128)(2,1)S(1)}, u32[]{:S(2)}, u32[]{:S(2)}) collective-permute-start(bf16[4,48,8,128]{3,2,1,0:T(8,128)(2,1)S(1)} %collective-permute-done.18.rest_14_), channel_id=1, source_target_pairs={{0,192},{64,0},{128,64},{192,128},{1,193},{65,1},{129,65},{193,129... | collective-permute-start | bytes 1179656 | tf_op jit(solution)/shard_map/ppermute | solution.py:289
  99.2 12.3 %collective-permute-start.13 = (bf16[4,256,128]{2,1,0:T(8,128)(2,1)S(1)}, bf16[4,256,128]{2,1,0:T(8,128)(2,1)}, u32[]{:S(2)}, u32[]{:S(2)}) collective-permute-start(bf16[4,256,128]{2,1,0:T(8,128)(2,1)S(1)} %collective-permute-done.11.rest_5_), channel_id=1, source_target_pairs={{0,4},{4,8},{8,12},{12,16},{16,20},{20,24},{24,28},{28,0},{1,5},{5... | collective-permute-start | bytes 786440 | tf_op jit(solution)/shard_map/ppermute | solution.py:289
  101.4 10.1 %collective-permute-start.14 = (bf16[4,256,128]{2,1,0:T(8,128)(2,1)}, bf16[4,256,128]{2,1,0:T(8,128)(2,1)}, u32[]{:S(2)}, u32[]{:S(2)}) collective-permute-start(bf16[4,256,128]{2,1,0:T(8,128)(2,1)} %collective-permute-done.12.rest_6_), channel_id=1, source_target_pairs={{0,4},{4,8},{8,12},{12,16},{16,20},{20,24},{24,28},{28,64},{64,68}... | collective-permute-start | bytes 786440 | tf_op jit(solution)/shard_map/ppermute | solution.py:301
  135.3 25.7 %all-to-all-start.3 = ((bf16[8,128,512]{2,1,0:T(8,128)(2,1)}), bf16[8,128,512]{2,1,0:T(8,128)(2,1)S(1)}, u32[]{:S(2)}, u32[]{:S(2)}) async-start(bf16[8,128,512]{2,1,0:T(8,128)(2,1)} %attend.2), calls=%async_computation.3 | async-start | bytes 2097152 | tf_op jit(solution)/shard_map/all_to_all | solution.py:339
  (25 other events, 462.3 us)

commit v6 on v5

--- a/solution.py
+++ b/solution.py
@@ -34,9 +34,7 @@
 HEADS_A_CALL = GROUP // CALLS
 TILES = CORES * WINDOW + HEADS_A_CALL * NV
 COUNTS = (4, 6, SLOTS)
-HALF = CHIPS_Z // 2
-FAR_X = (0, 0, 1, 1, -1, -1, 2, 2)
-FAR_Z = (0, HALF, 0, HALF, 0, HALF, 0, HALF)
+FAR_X = (0, 1, -1, 2)
 
 NEG = -1e30
 LOG2_SCALE = float(HEAD_SIZE**-0.5 * np.log2(np.e))
@@ -59,14 +57,14 @@
                 at = first + SPAN - ROW * (step + 1)
                 copies.append((source, tiles.at[pl.ds(at, ROW)]))
         x, z = spot[0], spot[1]
-        for ref, x_back, z_back in zip(far, FAR_X, FAR_Z):
-            for n in range(ref.shape[0]):
+        for ref, x_back in zip(far, FAR_X):
+            for n in range(CHIPS_Z):
                 at_x = (x - x_back + CHIPS_X) % CHIPS_X
-                at_z = (z - z_back - n + CHIPS_Z) % CHIPS_Z
+                at_z = (z - n + CHIPS_Z) % CHIPS_Z
                 first = pl.multiple_of((at_x * CHIPS_Z + at_z) * SLICE_ROWS, SLICE_ROWS)
                 count = HEADS_A_CALL * NV
                 target = tiles.at[pl.ds(CORES * WINDOW, count), pl.ds(first, SLICE_ROWS)]
-                copies.append((ref.at[n, pl.ds(half * count, count)], target))
+                copies.append((ref.at[n], target))
         copies = [
             pltpu.make_async_copy(source, target, sem.at[n])
             for n, (source, target) in enumerate(copies)
@@ -214,17 +212,36 @@
     )(*halves)
 
 
+def cut_kernel(tiles, slices):
+    for n in range(SLICES):
+        slices[n] = tiles[:, n * SLICE_ROWS : (n + 1) * SLICE_ROWS, :]
+
+
+def cut_slices(tiles):
+    return pl.pallas_call(
+        cut_kernel,
+        out_shape=jax.ShapeDtypeStruct(
+            (SLICES, tiles.shape[0], SLICE_ROWS, HEAD_SIZE), tiles.dtype
+        ),
+        cost_estimate=pl.CostEstimate(flops=0, bytes_accessed=1 << 20, transcendentals=0),
+        compiler_params=pltpu.CompilerParams(vmem_limit_bytes=8 << 20),
+        name="cut_slices",
+    )(tiles)
+
+
 def stack_kernel(*refs):
     halves = refs[CHIPS_Z:]
+    count = HEADS_A_CALL * NV
     for n, ref in enumerate(refs[:CHIPS_Z]):
-        halves[n // HALF][n % HALF] = ref[...]
+        for half in range(CALLS):
+            halves[half][n] = ref[half * count : (half + 1) * count]
 
 
 def stack_halves(parts):
-    half = jax.ShapeDtypeStruct((HALF, *parts[0].shape), parts[0].dtype)
+    shape = (CHIPS_Z, HEADS_A_CALL * NV, SLICE_ROWS, HEAD_SIZE)
     return pl.pallas_call(
         stack_kernel,
-        out_shape=(half, half),
+        out_shape=(jax.ShapeDtypeStruct(shape, parts[0].dtype),) * CALLS,
         cost_estimate=pl.CostEstimate(flops=0, bytes_accessed=2 << 20, transcendentals=0),
         compiler_params=pltpu.CompilerParams(vmem_limit_bytes=8 << 20),
         name="stack_halves",
@@ -300,42 +317,50 @@
     def passed_on(first, second):
         return shifted(first, "z", 1), lax.ppermute(second, ROW_AXES, onward)
 
-    sliced = pairs.reshape(PARTS, SLICES, SLICE_ROWS, HEAD_SIZE).transpose(1, 0, 2, 3)
-    sliced = lax.all_to_all(sliced, ROW_AXES, 0, 0, tiled=True)
+    sliced = lax.all_to_all(cut_slices(pairs), ROW_AXES, 0, 0, tiled=True)
     vert = lax.dynamic_slice_in_dim(vert_blocks, key_head * GROUP, GROUP, 0)
     slash = lax.dynamic_slice_in_dim(slash_offsets, key_head * GROUP, GROUP, 0)
-    listed = jnp.maximum(vert, 0).reshape(-1)
-    place, at_z, at_run = listed % ROW, listed // ROW % CHIPS_Z, listed // (ROW * CHIPS_Z)
-    at = (at_run // CORES * CHIPS_Z + at_z) * PARTS + at_run % CORES * ROW + place
-    picked = sliced.reshape(SLICES * PARTS, SLICE_ROWS, HEAD_SIZE)[at]
-
-    queries = split_heads(queries)
-    q = lax.all_to_all(queries, HEAD_AXES, 0, 0, tiled=True)
-
-    behind = shifted(picked, "z", 1)
-    ahead = [picked]
-    for _ in range(CHIPS_Z - 2):
-        ahead += [shifted(ahead[-1], "z", -1)]
-    column = [picked, behind] + ahead[:0:-1]
-    first, second, behind = lax.optimization_barrier((own[0], own[1], behind))
-    one = passed_on(first, second)
-    two = passed_on(*one)
-    column, two = lax.optimization_barrier((column, two))
-    lower, upper = stack_halves(column)
-    three = passed_on(*two)
-    four = passed_on(*three)
-    right, left = shifted(lower, "x", 1), shifted(upper, "x", -1)
-    far = [lower, upper, right, shifted(upper, "x", 1), shifted(lower, "x", -1), left]
-    far += [shifted(right, "x", 1), shifted(left, "x", -1)]
-    near = [own, *one, *two, *three, *four]
-
     runs = jnp.arange(CORES, dtype=jnp.int32)
     first_blocks = ((x * CORES + runs) * CHIPS_Z + z) * ROW
     turns, tile_of, bias_of = slot_tables(vert, slash, first_blocks, z)
     spot = jnp.stack([x, z]).astype(jnp.int32)
+    listed = jnp.maximum(vert, 0).reshape(-1)
+    place, at_z, at_run = listed % ROW, listed // ROW % CHIPS_Z, listed // (ROW * CHIPS_Z)
+    at = (at_run // CORES * CHIPS_Z + at_z) * PARTS + at_run % CORES * ROW + place
+    tables = (turns, tile_of, bias_of, spot)
+    sliced, tables = lax.optimization_barrier((sliced, tables))
+    picked = sliced.reshape(SLICES * PARTS, SLICE_ROWS, HEAD_SIZE)[at]
+
+    queries = split_heads(queries)
+    q = lax.all_to_all(queries, HEAD_AXES, 0, 0, tiled=True)
+
+    behind = shifted(picked, "z", 1)
+    ahead = [picked]
+    chain = [(own[0], own[1])]
+    chain += [passed_on(*chain[-1])]
+    for step in range(1, CHIPS_Z - 1):
+        ahead += [shifted(ahead[-1], "z", -1)]
+        if step in (1, 3):
+            ahead[-1], chain[-1] = lax.optimization_barrier((ahead[-1], chain[-1]))
+            chain += [passed_on(*chain[-1])]
+    column = [picked, behind] + ahead[:0:-1]
+    column, chain[-1] = lax.optimization_barrier((column, chain[-1]))
+    columns = stack_halves(column)
+    chain += [passed_on(*chain[-1])]
+    _, one, two, three, four = chain
+    (lower, upper), far = columns, []
+    right, left = shifted(lower, "x", 1), shifted(lower, "x", -1)
+    far += [(lower, right, left, shifted(right, "x", 1))]
+    left, right = shifted(upper, "x", -1), shifted(upper, "x", 1)
+    far[0], four, left = lax.optimization_barrier((far[0], four, left))
+    far += [(upper, right, left, shifted(left, "x", -1))]
+    near = [own, *one, *two, *three, *four]
+
     returned = []
     for half in range(CALLS):
-        mixed = attend_half(half, turns, tile_of, bias_of, spot, q, near, far)
+        mixed = attend_half(half, *tables, q, near, far[half])
+        if half == 0:
+            mixed, far[1] = lax.optimization_barrier((mixed, far[1]))
         returned += [lax.all_to_all(mixed, HEAD_AXES, 0, 0, tiled=True)]
     return merge_heads(*returned)
 

time: 184 us -> 181 us (0.984)
  waiting for transfers between devices: 65.2 us -> 59 us
  local copies, waits for them, and re-layouts: 7.01 us -> 10.6 us
    ppermute x17, starting transfers between devices: 21.8 us -> 15 us  [shifted(): lax.ppermute(value, axis, [(n, (n + by) % count) for n in range(count)])]
    ppermute x17, waiting for transfers between devices: 35.9 us -> 29.7 us  [shifted(): lax.ppermute(value, axis, [(n, (n + by) % count) for n in range(count)])]
    all_to_all x1, starting transfers between devices: 10.8 us -> 16.7 us  [shards(): returned += [lax.all_to_all(mixed, HEAD_AXES, 0, 0, tiled=True)]]
    all_to_all x1, waiting for transfers between devices: 9.06 us -> 5.4 us  [shards(): pairs = lax.all_to_all(pairs, HEAD_AXES, 0, 0, tiled=True)]
    unnamed x48 -> x54, local copies, waits for them, and re-layouts: 2.8 us -> 5.58 us
    ppermute x4, waiting for transfers between devices: 6.97 us -> 9.71 us  [passed_on(): return (shifted(first, 'z', 1), lax.ppermute(second, ROW_AXES, onward))]
    all_to_all x1, waiting for transfers between devices: 1.94 us -> 3.94 us  [shards(): returned += [lax.all_to_all(mixed, HEAD_AXES, 0, 0, tiled=True)]]
  transfers between devices with their start and end apart: 25 -> 25, of which waited for: 14 -> 13; matrix products, arithmetic and copies ran while one was open for 3% -> 4% of each run, Pallas kernels for 8% -> 14%
where the time goes in v6:
time: 181 us
  starting transfers between devices  59.9 us (33%)
  waiting for transfers between devices  59 us (33%)
  Pallas kernels  28.3 us (16%)
  blocking collectives  19.8 us (11%)
  local copies, waits for them, and re-layouts  10.6 us (6%)
  other arithmetic  2.45 us (1%)
    ppermute x17, waiting for transfers between devices, shifted(): lax.ppermute(value, axis, [(n, (n + by) % count) for n in range(count)])  29.7 us
    pallas_call x2, Pallas kernels, attend_half(): pl.pallas_call(functools.partial(attend_kernel, half), out_shape=jax.Shap...  23.4 us
    all_to_all x1, blocking collectives, shards(): returned += [lax.all_to_all(mixed, HEAD_AXES, 0, 0, tiled=True)]  19.8 us
    all_to_all x1, starting transfers between devices, shards(): returned += [lax.all_to_all(mixed, HEAD_AXES, 0, 0, tiled=True)]  16.7 us
    ppermute x17, starting transfers between devices, shifted(): lax.ppermute(value, axis, [(n, (n + by) % count) for n in range(count)])  15 us
    all_to_all x1, starting transfers between devices, shards(): sliced = lax.all_to_all(cut_slices(pairs), ROW_AXES, 0, 0, tiled=True)  10.4 us
    all_to_all x1, waiting for transfers between devices, shards(): sliced = lax.all_to_all(cut_slices(pairs), ROW_AXES, 0, 0, tiled=True)  10.2 us
    ppermute x4, waiting for transfers between devices, passed_on(): return (shifted(first, 'z', 1), lax.ppermute(second, ROW_AXES, onward))  9.71 us
  transfers between devices with their start and end apart: 25, of which 13 were waited for; matrix products, arithmetic and copies ran while one was open for 4% of the time, Pallas kernels for 14%

profile of v6, /device:TPU:1, one launch (start us, length us, event | category | flops | bytes accessed | tf_op | source)
XLA Modules:
  0.0 180.7 jit_solution(8322708397605326120)
XLA Ops:
  2.9 6.7 %all-to-all-start = ((bf16[8,256,128]{2,1,0:T(8,128)(2,1)}), bf16[8,256,128]{2,1,0:T(8,128)(2,1)S(1)}, u32[]{:S(2)}, u32[]{:S(2)}) async-start(bf16[8,256,128]{2,1,0:T(8,128)(2,1)} %split_pairs.1), calls=%async_computation | async-start | bytes 1048576 | tf_op jit(solution)/shard_map/all_to_all | solution.py:309
  13.5 5.4 %all-to-all-done.tiles = bf16[8,256,128]{2,1,0:T(8,128)(2,1)S(1)} async-done(((bf16[8,256,128]{2,1,0:T(8,128)(2,1)}), bf16[8,256,128]{2,1,0:T(8,128)(2,1)S(1)}, u32[]{:S(2)}, u32[]{:S(2)}) %all-to-all-start) | async-done | bytes 524320 | tf_op jit(solution)/shard_map/all_to_all | solution.py:309
  19.9 10.4 %all-to-all-start.1 = ((bf16[32,8,8,128]{3,2,1,0:T(8,128)(2,1)}), bf16[32,8,8,128]{3,2,1,0:T(8,128)(2,1)S(1)}, u32[]{:S(2)}, u32[]{:S(2)}) async-start(bf16[32,8,8,128]{3,2,1,0:T(8,128)(2,1)} %cut_slices.1), calls=%async_computation.1 | async-start | bytes 1048576 | tf_op jit(solution)/shard_map/all_to_all | solution.py:320
  34.1 10.2 %all-to-all-done.1 = bf16[32,8,8,128]{3,2,1,0:T(8,128)(2,1)S(1)} async-done(((bf16[32,8,8,128]{3,2,1,0:T(8,128)(2,1)}), bf16[32,8,8,128]{3,2,1,0:T(8,128)(2,1)S(1)}, u32[]{:S(2)}, u32[]{:S(2)}) %all-to-all-start.1) | async-done | bytes 524320 | tf_op jit(solution)/shard_map/all_to_all | solution.py:320
  45.1 9.4 %all-to-all-start.2 = ((bf16[8,128,1024]{2,1,0:T(8,128)(2,1)}), bf16[8,128,1024]{2,1,0:T(8,128)(2,1)S(1)}, u32[]{:S(2)}, u32[]{:S(2)}) async-start(bf16[8,128,1024]{2,1,0:T(8,128)(2,1)} %split_heads.1), calls=%async_computation.2 | async-start | bytes 4194304 | tf_op jit(solution)/shard_map/all_to_all | solution.py:335
  56.6 1.6 gather_fusion.1
  58.4 4.3 %collective-permute-done.refs_7_ = bf16[48,8,128]{2,1,0:T(8,128)(2,1)S(1)} collective-permute-done((bf16[48,8,128]{2,1,0:T(8,128)(2,1)S(1)}, bf16[48,8,128]{2,1,0:T(8,128)(2,1)S(1)}, u32[]{:S(2)}, u32[]{:S(2)}) %collective-permute-start) | collective-permute-done | bytes 98336 | tf_op jit(solution)/shard_map/ppermute | solution.py:306
  63.1 2.5 %collective-permute-start.3 = (bf16[48,8,128]{2,1,0:T(8,128)(2,1)S(1)}, bf16[48,8,128]{2,1,0:T(8,128)(2,1)S(1)}, u32[]{:S(2)}, u32[]{:S(2)}) collective-permute-start(bf16[48,8,128]{2,1,0:T(8,128)(2,1)S(1)} %collective-permute-done.refs_7_), channel_id=1, source_target_pairs={{0,28},{4,0},{8,4},{12,8},{16,12},{20,16},{24,20},{28,24},{1,29},{... | collective-permute-start | bytes 294920 | tf_op jit(solution)/shard_map/ppermute | solution.py:306
  65.6 1.9 %collective-permute-done.3.refs_6_ = bf16[48,8,128]{2,1,0:T(8,128)(2,1)S(1)} collective-permute-done((bf16[48,8,128]{2,1,0:T(8,128)(2,1)S(1)}, bf16[48,8,128]{2,1,0:T(8,128)(2,1)S(1)}, u32[]{:S(2)}, u32[]{:S(2)}) %collective-permute-start.3) | collective-permute-done | bytes 98336 | tf_op jit(solution)/shard_map/ppermute | solution.py:306
  67.5 3.0 %collective-permute-start.4 = (bf16[48,8,128]{2,1,0:T(8,128)(2,1)S(1)}, bf16[48,8,128]{2,1,0:T(8,128)(2,1)S(1)}, u32[]{:S(2)}, u32[]{:S(2)}) collective-permute-start(bf16[48,8,128]{2,1,0:T(8,128)(2,1)S(1)} %collective-permute-done.3.refs_6_), channel_id=1, source_target_pairs={{0,28},{4,0},{8,4},{12,8},{16,12},{20,16},{24,20},{28,24},{1,29},{... | collective-permute-start | bytes 294920 | tf_op jit(solution)/shard_map/ppermute | solution.py:306
  70.5 1.6 collective-permute-done.4.refs_5_
  72.2 4.6 %collective-permute-done.6.rest_4_ = bf16[4,256,128]{2,1,0:T(8,128)(2,1)S(1)} collective-permute-done((bf16[4,256,128]{2,1,0:T(8,128)(2,1)S(1)}, bf16[4,256,128]{2,1,0:T(8,128)(2,1)S(1)}, u32[]{:S(2)}, u32[]{:S(2)}) %collective-permute-start.6) | collective-permute-done | bytes 262176 | tf_op jit(solution)/shard_map/ppermute | solution.py:318
  78.2 2.3 %collective-permute-done.8.refs_4_ = bf16[48,8,128]{2,1,0:T(8,128)(2,1)S(1)} collective-permute-done((bf16[48,8,128]{2,1,0:T(8,128)(2,1)S(1)}, bf16[48,8,128]{2,1,0:T(8,128)(2,1)S(1)}, u32[]{:S(2)}, u32[]{:S(2)}) %collective-permute-start.8) | collective-permute-done | bytes 98336 | tf_op jit(solution)/shard_map/ppermute | solution.py:306
  82.0 2.3 %collective-permute-done.9.refs_3_ = bf16[48,8,128]{2,1,0:T(8,128)(2,1)S(1)} collective-permute-done((bf16[48,8,128]{2,1,0:T(8,128)(2,1)S(1)}, bf16[48,8,128]{2,1,0:T(8,128)(2,1)S(1)}, u32[]{:S(2)}, u32[]{:S(2)}) %collective-permute-start.9) | collective-permute-done | bytes 98336 | tf_op jit(solution)/shard_map/ppermute | solution.py:306
  84.3 2.0 %collective-permute-start.10 = (bf16[48,8,128]{2,1,0:T(8,128)(2,1)S(1)}, bf16[48,8,128]{2,1,0:T(8,128)(2,1)S(1)}, u32[]{:S(2)}, u32[]{:S(2)}) collective-permute-start(bf16[48,8,128]{2,1,0:T(8,128)(2,1)S(1)} %collective-permute-done.9.refs_3_), channel_id=1, source_target_pairs={{0,28},{4,0},{8,4},{12,8},{16,12},{20,16},{24,20},{28,24},{1,29},{... | collective-permute-start | bytes 294920 | tf_op jit(solution)/shard_map/ppermute | solution.py:306
  86.3 5.3 %collective-permute-done.7.refs_1_ = bf16[48,8,128]{2,1,0:T(8,128)(2,1)S(1)} collective-permute-done((bf16[48,8,128]{2,1,0:T(8,128)(2,1)S(1)}, bf16[48,8,128]{2,1,0:T(8,128)(2,1)S(1)}, u32[]{:S(2)}, u32[]{:S(2)}) %collective-permute-start.7) | collective-permute-done | bytes 98336 | tf_op jit(solution)/shard_map/ppermute | solution.py:306
  94.5 6.1 %collective-permute-done.13.rest_10_ = bf16[8,24,8,128]{3,2,1,0:T(8,128)(2,1)S(1)} collective-permute-done((bf16[8,24,8,128]{3,2,1,0:T(8,128)(2,1)S(1)}, bf16[8,24,8,128]{3,2,1,0:T(8,128)(2,1)S(1)}, u32[]{:S(2)}, u32[]{:S(2)}) %collective-permute-start.13) | collective-permute-done | bytes 393248 | tf_op jit(solution)/shard_map/ppermute | solution.py:306
  101.3 5.9 %collective-permute-done.16.rest_7_ = bf16[4,256,128]{2,1,0:T(8,128)(2,1)S(1)} collective-permute-done((bf16[4,256,128]{2,1,0:T(8,128)(2,1)S(1)}, bf16[4,256,128]{2,1,0:T(8,128)(2,1)S(1)}, u32[]{:S(2)}, u32[]{:S(2)}) %collective-permute-start.16) | collective-permute-done | bytes 262176 | tf_op jit(solution)/shard_map/ppermute | solution.py:306
  107.2 5.1 %collective-permute-done.17.rest_8_ = bf16[4,256,128]{2,1,0:T(8,128)(2,1)S(1)} collective-permute-done((bf16[4,256,128]{2,1,0:T(8,128)(2,1)S(1)}, bf16[4,256,128]{2,1,0:T(8,128)(2,1)S(1)}, u32[]{:S(2)}, u32[]{:S(2)}) %collective-permute-start.17) | collective-permute-done | bytes 262176 | tf_op jit(solution)/shard_map/ppermute | solution.py:318
  115.2 12.4 %attend.2 = bf16[8,128,512]{2,1,0:T(8,128)(2,1)} custom-call(s32[8]{0:T(128)} %fusion.9.turns, s32[640]{0:T(1024)} %reshape.326.tile_of, f32[640]{0:T(1024)} %select_n.125.bias_of, s32[2]{0:T(128)} %pad_add_fusion.3.spot, bf16[8,128,1024]{2,1,0:T(8,128)(2,1)} %copy-done.6, bf16[2,4,256,128]{3,2,1,0:T(8,128)(2,1)} %bitcast.8, bf16[4,256,128]{2,1,0:T(8,128)(2,1)} %copy-done.7, ...), custom_call_target="tpu_custom_call" | custom-call | flops 1610612736 | bytes 8388608 | tf_op jit(solution)/shard_map/attend/pallas_call | solution.py:113
  127.6 16.7 %all-to-all-start.3 = ((bf16[8,128,512]{2,1,0:T(8,128)(2,1)}), bf16[8,128,512]{2,1,0:T(8,128)(2,1)S(1)}, u32[]{:S(2)}, u32[]{:S(2)}) async-start(bf16[8,128,512]{2,1,0:T(8,128)(2,1)} %attend.2), calls=%async_computation.3 | async-start | bytes 2097152 | tf_op jit(solution)/shard_map/all_to_all | solution.py:364
  144.3 11.0 %attend.3 = bf16[8,128,512]{2,1,0:T(8,128)(2,1)} custom-call(s32[8]{0:T(128)} %fusion.9.turns, s32[640]{0:T(1024)} %reshape.326.tile_of, f32[640]{0:T(1024)} %select_n.125.bias_of, s32[2]{0:T(128)} %pad_add_fusion.3.spot, bf16[8,128,1024]{2,1,0:T(8,128)(2,1)} %copy-done.6, bf16[2,4,256,128]{3,2,1,0:T(8,128)(2,1)} %bitcast.9, bf16[4,256,128]{2,1,0:T(8,128)(2,1)} %copy-done.7, ...), custom_call_target="tpu_custom_call" | custom-call | flops 1610612736 | bytes 8388608 | tf_op jit(solution)/shard_map/attend/pallas_call | solution.py:113
  155.3 3.9 %all-to-all-done.3.refs_0_ = bf16[8,128,512]{2,1,0:T(8,128)(2,1)S(1)} async-done(((bf16[8,128,512]{2,1,0:T(8,128)(2,1)}), bf16[8,128,512]{2,1,0:T(8,128)(2,1)S(1)}, u32[]{:S(2)}, u32[]{:S(2)}) %all-to-all-start.3) | async-done | bytes 1048608 | tf_op jit(solution)/shard_map/all_to_all | solution.py:364
  159.3 19.8 %all_to_all.25.refs_1_ = bf16[8,128,512]{2,1,0:T(8,128)(2,1)S(1)} all-to-all(bf16[8,128,512]{2,1,0:T(8,128)(2,1)} %attend.3), channel_id=1, replica_groups=mesh['x'=4,'c'=2,'z'=8,'y'=4] {'c','y'}, dimensions={0} | all-to-all | bytes 2097152 | tf_op jit(solution)/shard_map/all_to_all | solution.py:364
  (127 shorter events, 25.7 us)
Async XLA Ops:
  2.9 16.0 %all-to-all-start = ((bf16[8,256,128]{2,1,0:T(8,128)(2,1)}), bf16[8,256,128]{2,1,0:T(8,128)(2,1)S(1)}, u32[]{:S(2)}, u32[]{:S(2)}) async-start(bf16[8,256,128]{2,1,0:T(8,128)(2,1)} %split_pairs.1), calls=%async_computation | async-start | bytes 1048576 | tf_op jit(solution)/shard_map/all_to_all | solution.py:309
  19.9 24.5 %all-to-all-start.1 = ((bf16[32,8,8,128]{3,2,1,0:T(8,128)(2,1)}), bf16[32,8,8,128]{3,2,1,0:T(8,128)(2,1)S(1)}, u32[]{:S(2)}, u32[]{:S(2)}) async-start(bf16[32,8,8,128]{3,2,1,0:T(8,128)(2,1)} %cut_slices.1), calls=%async_computation.1 | async-start | bytes 1048576 | tf_op jit(solution)/shard_map/all_to_all | solution.py:320
  31.7 26.7 %collective-permute-start.1 = (bf16[4,256,128]{2,1,0:T(8,128)(2,1)}, bf16[4,256,128]{2,1,0:T(8,128)(2,1)S(1)}, u32[]{:S(2)}, u32[]{:S(2)}) collective-permute-start(bf16[4,256,128]{2,1,0:T(8,128)(2,1)} %get-tuple-element.84), channel_id=1, source_target_pairs={{0,4},{4,8},{8,12},{12,16},{16,20},{20,24},{24,28},{28,0},{1,5},{5... | collective-permute-start | bytes 786440 | tf_op jit(solution)/shard_map/ppermute | solution.py:306
  32.9 25.5 %collective-permute-start.2 = (bf16[4,256,128]{2,1,0:T(8,128)(2,1)S(1)}, bf16[4,256,128]{2,1,0:T(8,128)(2,1)S(1)}, u32[]{:S(2)}, u32[]{:S(2)}) collective-permute-start(bf16[4,256,128]{2,1,0:T(8,128)(2,1)S(1)} %get-tuple-element.83), channel_id=1, source_target_pairs={{0,4},{4,8},{8,12},{12,16},{16,20},{20,24},{24,28},{28,64},{64,68}... | collective-permute-start | bytes 786440 | tf_op jit(solution)/shard_map/ppermute | solution.py:318
  45.1 68.7 %all-to-all-start.2 = ((bf16[8,128,1024]{2,1,0:T(8,128)(2,1)}), bf16[8,128,1024]{2,1,0:T(8,128)(2,1)S(1)}, u32[]{:S(2)}, u32[]{:S(2)}) async-start(bf16[8,128,1024]{2,1,0:T(8,128)(2,1)} %split_heads.1), calls=%async_computation.2 | async-start | bytes 4194304 | tf_op jit(solution)/shard_map/all_to_all | solution.py:335
  58.3 4.4 %collective-permute-start = (bf16[48,8,128]{2,1,0:T(8,128)(2,1)S(1)}, bf16[48,8,128]{2,1,0:T(8,128)(2,1)S(1)}, u32[]{:S(2)}, u32[]{:S(2)}) collective-permute-start(bf16[48,8,128]{2,1,0:T(8,128)(2,1)S(1)} %gather_fusion.1), channel_id=1, source_target_pairs={{0,28},{4,0},{8,4},{12,8},{16,12},{20,16},{24,20},{28,24},{1,29},{... | collective-permute-start | bytes 294920 | tf_op jit(solution)/shard_map/ppermute | solution.py:306
  62.7 9.5 %collective-permute-start.5 = (bf16[4,256,128]{2,1,0:T(8,128)(2,1)S(1)}, bf16[4,256,128]{2,1,0:T(8,128)(2,1)S(1)}, u32[]{:S(2)}, u32[]{:S(2)}) collective-permute-start(bf16[4,256,128]{2,1,0:T(8,128)(2,1)S(1)} %collective-permute-done.1.rest_1_), channel_id=1, source_target_pairs={{0,4},{4,8},{8,12},{12,16},{16,20},{20,24},{24,28},{28,0},{1,5},{5... | collective-permute-start | bytes 786440 | tf_op jit(solution)/shard_map/ppermute | solution.py:306
  63.0 13.8 %collective-permute-start.6 = (bf16[4,256,128]{2,1,0:T(8,128)(2,1)S(1)}, bf16[4,256,128]{2,1,0:T(8,128)(2,1)S(1)}, u32[]{:S(2)}, u32[]{:S(2)}) collective-permute-start(bf16[4,256,128]{2,1,0:T(8,128)(2,1)S(1)} %collective-permute-done.2.rest_2_), channel_id=1, source_target_pairs={{0,4},{4,8},{8,12},{12,16},{16,20},{20,24},{24,28},{28,64},{64,68}... | collective-permute-start | bytes 786440 | tf_op jit(solution)/shard_map/ppermute | solution.py:318
  63.1 4.4 %collective-permute-start.3 = (bf16[48,8,128]{2,1,0:T(8,128)(2,1)S(1)}, bf16[48,8,128]{2,1,0:T(8,128)(2,1)S(1)}, u32[]{:S(2)}, u32[]{:S(2)}) collective-permute-start(bf16[48,8,128]{2,1,0:T(8,128)(2,1)S(1)} %collective-permute-done.refs_7_), channel_id=1, source_target_pairs={{0,28},{4,0},{8,4},{12,8},{16,12},{20,16},{24,20},{28,24},{1,29},{... | collective-permute-start | bytes 294920 | tf_op jit(solution)/shard_map/ppermute | solution.py:306
  67.5 4.7 %collective-permute-start.4 = (bf16[48,8,128]{2,1,0:T(8,128)(2,1)S(1)}, bf16[48,8,128]{2,1,0:T(8,128)(2,1)S(1)}, u32[]{:S(2)}, u32[]{:S(2)}) collective-permute-start(bf16[48,8,128]{2,1,0:T(8,128)(2,1)S(1)} %collective-permute-done.3.refs_6_), channel_id=1, source_target_pairs={{0,28},{4,0},{8,4},{12,8},{16,12},{20,16},{24,20},{28,24},{1,29},{... | collective-permute-start | bytes 294920 | tf_op jit(solution)/shard_map/ppermute | solution.py:306
  76.9 14.6 %collective-permute-start.11 = (bf16[4,256,128]{2,1,0:T(8,128)(2,1)S(1)}, bf16[4,256,128]{2,1,0:T(8,128)(2,1)S(1)}, u32[]{:S(2)}, u32[]{:S(2)}) collective-permute-start(bf16[4,256,128]{2,1,0:T(8,128)(2,1)S(1)} %collective-permute-done.5.rest_3_), channel_id=1, source_target_pairs={{0,4},{4,8},{8,12},{12,16},{16,20},{20,24},{24,28},{28,0},{1,5},{5... | collective-permute-start | bytes 786440 | tf_op jit(solution)/shard_map/ppermute | solution.py:306
  78.2 13.4 %collective-permute-start.12 = (bf16[4,256,128]{2,1,0:T(8,128)(2,1)S(1)}, bf16[4,256,128]{2,1,0:T(8,128)(2,1)S(1)}, u32[]{:S(2)}, u32[]{:S(2)}) collective-permute-start(bf16[4,256,128]{2,1,0:T(8,128)(2,1)S(1)} %collective-permute-done.6.rest_4_), channel_id=1, source_target_pairs={{0,4},{4,8},{8,12},{12,16},{16,20},{20,24},{24,28},{28,64},{64,68}... | collective-permute-start | bytes 786440 | tf_op jit(solution)/shard_map/ppermute | solution.py:318
  80.5 3.8 %collective-permute-start.9 = (bf16[48,8,128]{2,1,0:T(8,128)(2,1)S(1)}, bf16[48,8,128]{2,1,0:T(8,128)(2,1)S(1)}, u32[]{:S(2)}, u32[]{:S(2)}) collective-permute-start(bf16[48,8,128]{2,1,0:T(8,128)(2,1)S(1)} %collective-permute-done.8.refs_4_), channel_id=1, source_target_pairs={{0,28},{4,0},{8,4},{12,8},{16,12},{20,16},{24,20},{28,24},{1,29},{... | collective-permute-start | bytes 294920 | tf_op jit(solution)/shard_map/ppermute | solution.py:306
  81.6 10.0 %collective-permute-start.7 = (bf16[48,8,128]{2,1,0:T(8,128)(2,1)S(1)}, bf16[48,8,128]{2,1,0:T(8,128)(2,1)S(1)}, u32[]{:S(2)}, u32[]{:S(2)}) collective-permute-start(bf16[48,8,128]{2,1,0:T(8,128)(2,1)S(1)} %gather_fusion.1), channel_id=1, source_target_pairs={{0,4},{4,8},{8,12},{12,16},{16,20},{20,24},{24,28},{28,0},{1,5},{5... | collective-permute-start | bytes 294920 | tf_op jit(solution)/shard_map/ppermute | solution.py:306
  84.3 7.4 %collective-permute-start.10 = (bf16[48,8,128]{2,1,0:T(8,128)(2,1)S(1)}, bf16[48,8,128]{2,1,0:T(8,128)(2,1)S(1)}, u32[]{:S(2)}, u32[]{:S(2)}) collective-permute-start(bf16[48,8,128]{2,1,0:T(8,128)(2,1)S(1)} %collective-permute-done.9.refs_3_), channel_id=1, source_target_pairs={{0,28},{4,0},{8,4},{12,8},{16,12},{20,16},{24,20},{28,24},{1,29},{... | collective-permute-start | bytes 294920 | tf_op jit(solution)/shard_map/ppermute | solution.py:306
  91.7 8.9 %collective-permute-start.13 = (bf16[8,24,8,128]{3,2,1,0:T(8,128)(2,1)S(1)}, bf16[8,24,8,128]{3,2,1,0:T(8,128)(2,1)S(1)}, u32[]{:S(2)}, u32[]{:S(2)}) collective-permute-start(bf16[8,24,8,128]{3,2,1,0:T(8,128)(2,1)S(1)} %get-tuple-element.65.rest_9_), channel_id=1, source_target_pairs={{0,64},{64,128},{128,192},{192,0},{1,65},{65,129},{129,193},{193,1... | collective-permute-start | bytes 1179656 | tf_op jit(solution)/shard_map/ppermute | solution.py:306
  92.9 19.5 %collective-permute-start.14 = (bf16[8,24,8,128]{3,2,1,0:T(8,128)(2,1)S(1)}, bf16[8,24,8,128]{3,2,1,0:T(8,128)(2,1)S(1)}, u32[]{:S(2)}, u32[]{:S(2)}) collective-permute-start(bf16[8,24,8,128]{3,2,1,0:T(8,128)(2,1)S(1)} %get-tuple-element.65.rest_9_), channel_id=1, source_target_pairs={{0,192},{64,0},{128,64},{192,128},{1,193},{65,1},{129,65},{193,129... | collective-permute-start | bytes 1179656 | tf_op jit(solution)/shard_map/ppermute | solution.py:306
  94.5 17.9 %collective-permute-start.18 = (bf16[8,24,8,128]{3,2,1,0:T(8,128)(2,1)S(1)}, bf16[8,24,8,128]{3,2,1,0:T(8,128)(2,1)}, u32[]{:S(2)}, u32[]{:S(2)}) collective-permute-start(bf16[8,24,8,128]{3,2,1,0:T(8,128)(2,1)S(1)} %get-tuple-element.71.rest_9_), channel_id=1, source_target_pairs={{0,192},{64,0},{128,64},{192,128},{1,193},{65,1},{129,65},{193,129... | collective-permute-start | bytes 1179656 | tf_op jit(solution)/shard_map/ppermute | solution.py:306
  100.6 11.8 %collective-permute-start.15 = (bf16[8,24,8,128]{3,2,1,0:T(8,128)(2,1)S(1)}, bf16[8,24,8,128]{3,2,1,0:T(8,128)(2,1)S(1)}, u32[]{:S(2)}, u32[]{:S(2)}) collective-permute-start(bf16[8,24,8,128]{3,2,1,0:T(8,128)(2,1)S(1)} %collective-permute-done.13.rest_10_), channel_id=1, source_target_pairs={{0,64},{64,128},{128,192},{192,0},{1,65},{65,129},{129,193},{193,1... | collective-permute-start | bytes 1179656 | tf_op jit(solution)/shard_map/ppermute | solution.py:306
  100.8 6.4 %collective-permute-start.16 = (bf16[4,256,128]{2,1,0:T(8,128)(2,1)S(1)}, bf16[4,256,128]{2,1,0:T(8,128)(2,1)S(1)}, u32[]{:S(2)}, u32[]{:S(2)}) collective-permute-start(bf16[4,256,128]{2,1,0:T(8,128)(2,1)S(1)} %collective-permute-done.11.rest_5_), channel_id=1, source_target_pairs={{0,4},{4,8},{8,12},{12,16},{16,20},{20,24},{24,28},{28,0},{1,5},{5... | collective-permute-start | bytes 786440 | tf_op jit(solution)/shard_map/ppermute | solution.py:306
  100.8 11.6 %collective-permute-start.17 = (bf16[4,256,128]{2,1,0:T(8,128)(2,1)S(1)}, bf16[4,256,128]{2,1,0:T(8,128)(2,1)S(1)}, u32[]{:S(2)}, u32[]{:S(2)}) collective-permute-start(bf16[4,256,128]{2,1,0:T(8,128)(2,1)S(1)} %collective-permute-done.12.rest_6_), channel_id=1, source_target_pairs={{0,4},{4,8},{8,12},{12,16},{16,20},{20,24},{24,28},{28,64},{64,68}... | collective-permute-start | bytes 786440 | tf_op jit(solution)/shard_map/ppermute | solution.py:318
  107.2 20.4 %collective-permute-start.19 = (bf16[8,24,8,128]{3,2,1,0:T(8,128)(2,1)S(1)}, bf16[8,24,8,128]{3,2,1,0:T(8,128)(2,1)}, u32[]{:S(2)}, u32[]{:S(2)}) collective-permute-start(bf16[8,24,8,128]{3,2,1,0:T(8,128)(2,1)S(1)} %get-tuple-element.71.rest_9_), channel_id=1, source_target_pairs={{0,64},{64,128},{128,192},{192,0},{1,65},{65,129},{129,193},{193,1... | collective-permute-start | bytes 1179656 | tf_op jit(solution)/shard_map/ppermute | solution.py:306
  113.9 13.7 %collective-permute-start.20 = (bf16[8,24,8,128]{3,2,1,0:T(8,128)(2,1)}, bf16[8,24,8,128]{3,2,1,0:T(8,128)(2,1)}, u32[]{:S(2)}, u32[]{:S(2)}) collective-permute-start(bf16[8,24,8,128]{3,2,1,0:T(8,128)(2,1)} %collective-permute-done.18.rest_11_), channel_id=1, source_target_pairs={{0,192},{64,0},{128,64},{192,128},{1,193},{65,1},{129,65},{193,129... | collective-permute-start | bytes 1179656 | tf_op jit(solution)/shard_map/ppermute | solution.py:306
  127.6 31.7 %all-to-all-start.3 = ((bf16[8,128,512]{2,1,0:T(8,128)(2,1)}), bf16[8,128,512]{2,1,0:T(8,128)(2,1)S(1)}, u32[]{:S(2)}, u32[]{:S(2)}) async-start(bf16[8,128,512]{2,1,0:T(8,128)(2,1)} %attend.2), calls=%async_computation.3 | async-start | bytes 2097152 | tf_op jit(solution)/shard_map/all_to_all | solution.py:364
  (28 other events, 308.1 us)

commit v7 on v6

--- a/solution.py
+++ b/solution.py
@@ -328,7 +328,8 @@
     place, at_z, at_run = listed % ROW, listed // ROW % CHIPS_Z, listed // (ROW * CHIPS_Z)
     at = (at_run // CORES * CHIPS_Z + at_z) * PARTS + at_run % CORES * ROW + place
     tables = (turns, tile_of, bias_of, spot)
-    sliced, tables = lax.optimization_barrier((sliced, tables))
+    chain = [(own[0], own[1]), passed_on(own[0], own[1])]
+    sliced, tables, at, chain = lax.optimization_barrier((sliced, tables, at, chain))
     picked = sliced.reshape(SLICES * PARTS, SLICE_ROWS, HEAD_SIZE)[at]
 
     queries = split_heads(queries)
@@ -336,11 +337,10 @@
 
     behind = shifted(picked, "z", 1)
     ahead = [picked]
-    chain = [(own[0], own[1])]
     chain += [passed_on(*chain[-1])]
     for step in range(1, CHIPS_Z - 1):
         ahead += [shifted(ahead[-1], "z", -1)]
-        if step in (1, 3):
+        if step == 3:
             ahead[-1], chain[-1] = lax.optimization_barrier((ahead[-1], chain[-1]))
             chain += [passed_on(*chain[-1])]
     column = [picked, behind] + ahead[:0:-1]
@@ -348,12 +348,8 @@
     columns = stack_halves(column)
     chain += [passed_on(*chain[-1])]
     _, one, two, three, four = chain
-    (lower, upper), far = columns, []
-    right, left = shifted(lower, "x", 1), shifted(lower, "x", -1)
-    far += [(lower, right, left, shifted(right, "x", 1))]
-    left, right = shifted(upper, "x", -1), shifted(upper, "x", 1)
-    far[0], four, left = lax.optimization_barrier((far[0], four, left))
-    far += [(upper, right, left, shifted(left, "x", -1))]
+    far = [(c, *(shifted(c, "x", by) for by in (1, -1, 2))) for c in columns]
+    far[0], four = lax.optimization_barrier((far[0], four))
     near = [own, *one, *two, *three, *four]
 
     returned = []

time: 181 us -> 178 us (0.983)
  waiting for transfers between devices: 59 us -> 56 us
  local copies, waits for them, and re-layouts: 10.6 us -> 8.62 us
    ppermute x17, waiting for transfers between devices: 29.7 us -> 25 us  [shifted(): lax.ppermute(value, axis, [(n, (n + by) % count) for n in range(count)])]
    ppermute x17, starting transfers between devices: 15 us -> 18.1 us  [shifted(): lax.ppermute(value, axis, [(n, (n + by) % count) for n in range(count)])]
    all_to_all x1, waiting for transfers between devices: 5.4 us -> 7.46 us  [shards(): pairs = lax.all_to_all(pairs, HEAD_AXES, 0, 0, tiled=True)]
    all_to_all x1, starting transfers between devices: 16.7 us -> 14.7 us  [shards(): returned += [lax.all_to_all(mixed, HEAD_AXES, 0, 0, tiled=True)]]
    unnamed x54 -> x50, local copies, waits for them, and re-layouts: 5.58 us -> 4.25 us
  transfers between devices with their start and end apart: 25 -> 25, of which waited for: 13 -> 14; matrix products, arithmetic and copies ran while one was open for 4% -> 4% of each run, Pallas kernels for 14% -> 14%
where the time goes in v7:
time: 178 us; the launch traced here: 179 us
  starting transfers between devices  61.4 us (34%)
  waiting for transfers between devices  56 us (31%)
  Pallas kernels  29 us (16%)
  blocking collectives  20.8 us (12%)
  local copies, waits for them, and re-layouts  8.62 us (5%)
  other arithmetic  2.38 us (1%)
    ppermute x17, waiting for transfers between devices, shifted(): lax.ppermute(value, axis, [(n, (n + by) % count) for n in range(count)])  25 us
    pallas_call x2, Pallas kernels, attend_half(): pl.pallas_call(functools.partial(attend_kernel, half), out_shape=jax.Shap...  24 us
    all_to_all x1, blocking collectives, shards(): returned += [lax.all_to_all(mixed, HEAD_AXES, 0, 0, tiled=True)]  20.8 us
    ppermute x17, starting transfers between devices, shifted(): lax.ppermute(value, axis, [(n, (n + by) % count) for n in range(count)])  18.1 us
    all_to_all x1, starting transfers between devices, shards(): returned += [lax.all_to_all(mixed, HEAD_AXES, 0, 0, tiled=True)]  14.7 us
    all_to_all x1, starting transfers between devices, shards(): sliced = lax.all_to_all(cut_slices(pairs), ROW_AXES, 0, 0, tiled=True)  10.5 us
    ppermute x4, waiting for transfers between devices, passed_on(): return (shifted(first, 'z', 1), lax.ppermute(second, ROW_AXES, onward))  9.58 us
    all_to_all x1, waiting for transfers between devices, shards(): sliced = lax.all_to_all(cut_slices(pairs), ROW_AXES, 0, 0, tiled=True)  9.39 us
  transfers between devices with their start and end apart: 25, of which 14 were waited for; matrix products, arithmetic and copies ran while one was open for 4% of the time, Pallas kernels for 14%

profile of v7, /device:TPU:1, one launch (start us, length us, event | category | flops | bytes accessed | tf_op | source)
XLA Modules:
  0.0 178.8 jit_solution(1197008708863639815)
XLA Ops:
  2.9 6.8 %all-to-all-start = ((bf16[8,256,128]{2,1,0:T(8,128)(2,1)}), bf16[8,256,128]{2,1,0:T(8,128)(2,1)S(1)}, u32[]{:S(2)}, u32[]{:S(2)}) async-start(bf16[8,256,128]{2,1,0:T(8,128)(2,1)} %split_pairs.1), calls=%async_computation | async-start | bytes 1048576 | tf_op jit(solution)/shard_map/all_to_all | solution.py:309
  11.6 7.5 %all-to-all-done.tiles = bf16[8,256,128]{2,1,0:T(8,128)(2,1)S(1)} async-done(((bf16[8,256,128]{2,1,0:T(8,128)(2,1)}), bf16[8,256,128]{2,1,0:T(8,128)(2,1)S(1)}, u32[]{:S(2)}, u32[]{:S(2)}) %all-to-all-start) | async-done | bytes 524320 | tf_op jit(solution)/shard_map/all_to_all | solution.py:309
  20.1 10.5 %all-to-all-start.1 = ((bf16[32,8,8,128]{3,2,1,0:T(8,128)(2,1)}), bf16[32,8,8,128]{3,2,1,0:T(8,128)(2,1)}, u32[]{:S(2)}, u32[]{:S(2)}) async-start(bf16[32,8,8,128]{3,2,1,0:T(8,128)(2,1)} %cut_slices.1), calls=%async_computation.1 | async-start | bytes 1048576 | tf_op jit(solution)/shard_map/all_to_all | solution.py:320
  35.2 9.4 %all-to-all-done.1 = bf16[32,8,8,128]{3,2,1,0:T(8,128)(2,1)} async-done(((bf16[32,8,8,128]{3,2,1,0:T(8,128)(2,1)}), bf16[32,8,8,128]{3,2,1,0:T(8,128)(2,1)}, u32[]{:S(2)}, u32[]{:S(2)}) %all-to-all-start.1) | async-done | bytes 524320 | tf_op jit(solution)/shard_map/all_to_all | solution.py:320
  44.6 9.4 %all-to-all-start.2 = ((bf16[8,128,1024]{2,1,0:T(8,128)(2,1)}), bf16[8,128,1024]{2,1,0:T(8,128)(2,1)S(1)}, u32[]{:S(2)}, u32[]{:S(2)}) async-start(bf16[8,128,1024]{2,1,0:T(8,128)(2,1)} %split_heads.1), calls=%async_computation.2 | async-start | bytes 4194304 | tf_op jit(solution)/shard_map/all_to_all | solution.py:336
  61.2 2.3 %collective-permute-done.2.refs_7_ = bf16[48,8,128]{2,1,0:T(8,128)(2,1)S(1)} collective-permute-done((bf16[48,8,128]{2,1,0:T(8,128)(2,1)S(1)}, bf16[48,8,128]{2,1,0:T(8,128)(2,1)S(1)}, u32[]{:S(2)}, u32[]{:S(2)}) %collective-permute-start.2) | collective-permute-done | bytes 98336 | tf_op jit(solution)/shard_map/ppermute | solution.py:306
  64.7 2.5 %collective-permute-done.3.refs_6_ = bf16[48,8,128]{2,1,0:T(8,128)(2,1)S(1)} collective-permute-done((bf16[48,8,128]{2,1,0:T(8,128)(2,1)S(1)}, bf16[48,8,128]{2,1,0:T(8,128)(2,1)S(1)}, u32[]{:S(2)}, u32[]{:S(2)}) %collective-permute-start.3) | collective-permute-done | bytes 98336 | tf_op jit(solution)/shard_map/ppermute | solution.py:306
  67.2 2.4 %collective-permute-start.4 = (bf16[48,8,128]{2,1,0:T(8,128)(2,1)S(1)}, bf16[48,8,128]{2,1,0:T(8,128)(2,1)S(1)}, u32[]{:S(2)}, u32[]{:S(2)}) collective-permute-start(bf16[48,8,128]{2,1,0:T(8,128)(2,1)S(1)} %collective-permute-done.3.refs_6_), channel_id=1, source_target_pairs={{0,28},{4,0},{8,4},{12,8},{16,12},{20,16},{24,20},{28,24},{1,29},{... | collective-permute-start | bytes 294920 | tf_op jit(solution)/shard_map/ppermute | solution.py:306
  69.7 4.2 %collective-permute-done.6.rest_4_ = bf16[4,256,128]{2,1,0:T(8,128)(2,1)S(1)} collective-permute-done((bf16[4,256,128]{2,1,0:T(8,128)(2,1)S(1)}, bf16[4,256,128]{2,1,0:T(8,128)(2,1)S(1)}, u32[]{:S(2)}, u32[]{:S(2)}) %collective-permute-start.6) | collective-permute-done | bytes 262176 | tf_op jit(solution)/shard_map/ppermute | solution.py:318
  75.3 2.3 %collective-permute-done.8.refs_4_ = bf16[48,8,128]{2,1,0:T(8,128)(2,1)S(1)} collective-permute-done((bf16[48,8,128]{2,1,0:T(8,128)(2,1)S(1)}, bf16[48,8,128]{2,1,0:T(8,128)(2,1)S(1)}, u32[]{:S(2)}, u32[]{:S(2)}) %collective-permute-start.8) | collective-permute-done | bytes 98336 | tf_op jit(solution)/shard_map/ppermute | solution.py:306
  77.6 2.0 %collective-permute-start.9 = (bf16[48,8,128]{2,1,0:T(8,128)(2,1)S(1)}, bf16[48,8,128]{2,1,0:T(8,128)(2,1)S(1)}, u32[]{:S(2)}, u32[]{:S(2)}) collective-permute-start(bf16[48,8,128]{2,1,0:T(8,128)(2,1)S(1)} %collective-permute-done.8.refs_4_), channel_id=1, source_target_pairs={{0,28},{4,0},{8,4},{12,8},{16,12},{20,16},{24,20},{28,24},{1,29},{... | collective-permute-start | bytes 294920 | tf_op jit(solution)/shard_map/ppermute | solution.py:306
  79.6 1.8 %collective-permute-done.9.refs_3_ = bf16[48,8,128]{2,1,0:T(8,128)(2,1)S(1)} collective-permute-done((bf16[48,8,128]{2,1,0:T(8,128)(2,1)S(1)}, bf16[48,8,128]{2,1,0:T(8,128)(2,1)S(1)}, u32[]{:S(2)}, u32[]{:S(2)}) %collective-permute-start.9) | collective-permute-done | bytes 98336 | tf_op jit(solution)/shard_map/ppermute | solution.py:306
  81.4 3.1 %collective-permute-start.10 = (bf16[48,8,128]{2,1,0:T(8,128)(2,1)S(1)}, bf16[48,8,128]{2,1,0:T(8,128)(2,1)S(1)}, u32[]{:S(2)}, u32[]{:S(2)}) collective-permute-start(bf16[48,8,128]{2,1,0:T(8,128)(2,1)S(1)} %collective-permute-done.9.refs_3_), channel_id=1, source_target_pairs={{0,28},{4,0},{8,4},{12,8},{16,12},{20,16},{24,20},{28,24},{1,29},{... | collective-permute-start | bytes 294920 | tf_op jit(solution)/shard_map/ppermute | solution.py:306
  84.5 2.9 %collective-permute-done.7.refs_1_ = bf16[48,8,128]{2,1,0:T(8,128)(2,1)S(1)} collective-permute-done((bf16[48,8,128]{2,1,0:T(8,128)(2,1)S(1)}, bf16[48,8,128]{2,1,0:T(8,128)(2,1)S(1)}, u32[]{:S(2)}, u32[]{:S(2)}) %collective-permute-start.7) | collective-permute-done | bytes 98336 | tf_op jit(solution)/shard_map/ppermute | solution.py:306
  89.1 2.0 %collective-permute-start.14 = (bf16[8,24,8,128]{3,2,1,0:T(8,128)(2,1)S(1)}, bf16[8,24,8,128]{3,2,1,0:T(8,128)(2,1)S(1)}, u32[]{:S(2)}, u32[]{:S(2)}) collective-permute-start(bf16[8,24,8,128]{3,2,1,0:T(8,128)(2,1)S(1)} %get-tuple-element.63.rest_9_), channel_id=1, source_target_pairs={{0,192},{64,0},{128,64},{192,128},{1,193},{65,1},{129,65},{193,129... | collective-permute-start | bytes 1179656 | tf_op jit(solution)/shard_map/ppermute | solution.py:306
  91.6 2.8 %collective-permute-done.16.rest_7_ = bf16[4,256,128]{2,1,0:T(8,128)(2,1)S(1)} collective-permute-done((bf16[4,256,128]{2,1,0:T(8,128)(2,1)S(1)}, bf16[4,256,128]{2,1,0:T(8,128)(2,1)S(1)}, u32[]{:S(2)}, u32[]{:S(2)}) %collective-permute-start.16) | collective-permute-done | bytes 262176 | tf_op jit(solution)/shard_map/ppermute | solution.py:306
  95.5 4.1 %collective-permute-done.17.rest_8_ = bf16[4,256,128]{2,1,0:T(8,128)(2,1)S(1)} collective-permute-done((bf16[4,256,128]{2,1,0:T(8,128)(2,1)S(1)}, bf16[4,256,128]{2,1,0:T(8,128)(2,1)S(1)}, u32[]{:S(2)}, u32[]{:S(2)}) %collective-permute-start.17) | collective-permute-done | bytes 262176 | tf_op jit(solution)/shard_map/ppermute | solution.py:318
  101.3 8.5 %collective-permute-done.15.rest_12_ = bf16[8,24,8,128]{3,2,1,0:T(8,128)(2,1)} collective-permute-done((bf16[8,24,8,128]{3,2,1,0:T(8,128)(2,1)S(1)}, bf16[8,24,8,128]{3,2,1,0:T(8,128)(2,1)}, u32[]{:S(2)}, u32[]{:S(2)}) %collective-permute-start.15) | collective-permute-done | bytes 393248 | tf_op jit(solution)/shard_map/ppermute | solution.py:306
  111.1 13.7 %attend.2 = bf16[8,128,512]{2,1,0:T(8,128)(2,1)} custom-call(s32[8]{0:T(128)} %fusion.9.turns, s32[640]{0:T(1024)} %reshape.77.tile_of, f32[640]{0:T(1024)} %select_n.76.bias_of, s32[2]{0:T(128)} %pad_add_fusion.3.spot, bf16[8,128,1024]{2,1,0:T(8,128)(2,1)} %copy-done.6, bf16[2,4,256,128]{3,2,1,0:T(8,128)(2,1)} %bitcast.6, bf16[4,256,128]{2,1,0:T(8,128)(2,1)} %copy-done.7, ...), custom_call_target="tpu_custom_call" | custom-call | flops 1610612736 | bytes 8388608 | tf_op jit(solution)/shard_map/attend/pallas_call | solution.py:113
  124.8 1.9 %collective-permute-done.20.rest_12_ = bf16[8,24,8,128]{3,2,1,0:T(8,128)(2,1)} collective-permute-done((bf16[8,24,8,128]{3,2,1,0:T(8,128)(2,1)S(1)}, bf16[8,24,8,128]{3,2,1,0:T(8,128)(2,1)}, u32[]{:S(2)}, u32[]{:S(2)}) %collective-permute-start.20) | collective-permute-done | bytes 393248 | tf_op jit(solution)/shard_map/ppermute | solution.py:306
  126.6 14.7 %all-to-all-start.3 = ((bf16[8,128,512]{2,1,0:T(8,128)(2,1)}), bf16[8,128,512]{2,1,0:T(8,128)(2,1)S(1)}, u32[]{:S(2)}, u32[]{:S(2)}) async-start(bf16[8,128,512]{2,1,0:T(8,128)(2,1)} %attend.2), calls=%async_computation.3 | async-start | bytes 2097152 | tf_op jit(solution)/shard_map/all_to_all | solution.py:360
  141.4 10.4 %attend.3 = bf16[8,128,512]{2,1,0:T(8,128)(2,1)} custom-call(s32[8]{0:T(128)} %fusion.9.turns, s32[640]{0:T(1024)} %reshape.77.tile_of, f32[640]{0:T(1024)} %select_n.76.bias_of, s32[2]{0:T(128)} %pad_add_fusion.3.spot, bf16[8,128,1024]{2,1,0:T(8,128)(2,1)} %copy-done.6, bf16[2,4,256,128]{3,2,1,0:T(8,128)(2,1)} %bitcast.7, bf16[4,256,128]{2,1,0:T(8,128)(2,1)} %copy-done.7, ...), custom_call_target="tpu_custom_call" | custom-call | flops 1610612736 | bytes 8388608 | tf_op jit(solution)/shard_map/attend/pallas_call | solution.py:113
  151.8 4.6 %all-to-all-done.3.refs_0_ = bf16[8,128,512]{2,1,0:T(8,128)(2,1)S(1)} async-done(((bf16[8,128,512]{2,1,0:T(8,128)(2,1)}), bf16[8,128,512]{2,1,0:T(8,128)(2,1)S(1)}, u32[]{:S(2)}, u32[]{:S(2)}) %all-to-all-start.3) | async-done | bytes 1048608 | tf_op jit(solution)/shard_map/all_to_all | solution.py:360
  156.3 20.8 %all_to_all.25.refs_1_ = bf16[8,128,512]{2,1,0:T(8,128)(2,1)S(1)} all-to-all(bf16[8,128,512]{2,1,0:T(8,128)(2,1)} %attend.3), channel_id=1, replica_groups=mesh['x'=4,'c'=2,'z'=8,'y'=4] {'c','y'}, dimensions={0} | all-to-all | bytes 2097152 | tf_op jit(solution)/shard_map/all_to_all | solution.py:360
  (124 shorter events, 27.8 us)
Async XLA Ops:
  2.9 16.2 %all-to-all-start = ((bf16[8,256,128]{2,1,0:T(8,128)(2,1)}), bf16[8,256,128]{2,1,0:T(8,128)(2,1)S(1)}, u32[]{:S(2)}, u32[]{:S(2)}) async-start(bf16[8,256,128]{2,1,0:T(8,128)(2,1)} %split_pairs.1), calls=%async_computation | async-start | bytes 1048576 | tf_op jit(solution)/shard_map/all_to_all | solution.py:309
  20.1 24.6 %all-to-all-start.1 = ((bf16[32,8,8,128]{3,2,1,0:T(8,128)(2,1)}), bf16[32,8,8,128]{3,2,1,0:T(8,128)(2,1)}, u32[]{:S(2)}, u32[]{:S(2)}) async-start(bf16[32,8,8,128]{3,2,1,0:T(8,128)(2,1)} %cut_slices.1), calls=%async_computation.1 | async-start | bytes 1048576 | tf_op jit(solution)/shard_map/all_to_all | solution.py:320
  32.8 23.7 %collective-permute-start = (bf16[4,256,128]{2,1,0:T(8,128)(2,1)S(1)}, bf16[4,256,128]{2,1,0:T(8,128)(2,1)S(1)}, u32[]{:S(2)}, u32[]{:S(2)}) collective-permute-start(bf16[4,256,128]{2,1,0:T(8,128)(2,1)S(1)} %get-tuple-element.82), channel_id=1, source_target_pairs={{0,4},{4,8},{8,12},{12,16},{16,20},{20,24},{24,28},{28,0},{1,5},{5... | collective-permute-start | bytes 786440 | tf_op jit(solution)/shard_map/ppermute | solution.py:306
  34.1 23.8 %collective-permute-start.1 = (bf16[4,256,128]{2,1,0:T(8,128)(2,1)S(1)}, bf16[4,256,128]{2,1,0:T(8,128)(2,1)S(1)}, u32[]{:S(2)}, u32[]{:S(2)}) collective-permute-start(bf16[4,256,128]{2,1,0:T(8,128)(2,1)S(1)} %get-tuple-element.81), channel_id=1, source_target_pairs={{0,4},{4,8},{8,12},{12,16},{16,20},{20,24},{24,28},{28,64},{64,68}... | collective-permute-start | bytes 786440 | tf_op jit(solution)/shard_map/ppermute | solution.py:318
  44.6 65.1 %all-to-all-start.2 = ((bf16[8,128,1024]{2,1,0:T(8,128)(2,1)}), bf16[8,128,1024]{2,1,0:T(8,128)(2,1)S(1)}, u32[]{:S(2)}, u32[]{:S(2)}) async-start(bf16[8,128,1024]{2,1,0:T(8,128)(2,1)} %split_heads.1), calls=%async_computation.2 | async-start | bytes 4194304 | tf_op jit(solution)/shard_map/all_to_all | solution.py:336
  59.6 3.8 %collective-permute-start.2 = (bf16[48,8,128]{2,1,0:T(8,128)(2,1)S(1)}, bf16[48,8,128]{2,1,0:T(8,128)(2,1)S(1)}, u32[]{:S(2)}, u32[]{:S(2)}) collective-permute-start(bf16[48,8,128]{2,1,0:T(8,128)(2,1)S(1)} %gather_fusion.1), channel_id=1, source_target_pairs={{0,28},{4,0},{8,4},{12,8},{16,12},{20,16},{24,20},{28,24},{1,29},{... | collective-permute-start | bytes 294920 | tf_op jit(solution)/shard_map/ppermute | solution.py:306
  59.7 9.9 %collective-permute-start.5 = (bf16[4,256,128]{2,1,0:T(8,128)(2,1)S(1)}, bf16[4,256,128]{2,1,0:T(8,128)(2,1)S(1)}, u32[]{:S(2)}, u32[]{:S(2)}) collective-permute-start(bf16[4,256,128]{2,1,0:T(8,128)(2,1)S(1)} %collective-permute-done.rest_1_), channel_id=1, source_target_pairs={{0,4},{4,8},{8,12},{12,16},{16,20},{20,24},{24,28},{28,0},{1,5},{5... | collective-permute-start | bytes 786440 | tf_op jit(solution)/shard_map/ppermute | solution.py:306
  61.2 12.7 %collective-permute-start.6 = (bf16[4,256,128]{2,1,0:T(8,128)(2,1)S(1)}, bf16[4,256,128]{2,1,0:T(8,128)(2,1)S(1)}, u32[]{:S(2)}, u32[]{:S(2)}) collective-permute-start(bf16[4,256,128]{2,1,0:T(8,128)(2,1)S(1)} %collective-permute-done.1.rest_2_), channel_id=1, source_target_pairs={{0,4},{4,8},{8,12},{12,16},{16,20},{20,24},{24,28},{28,64},{64,68}... | collective-permute-start | bytes 786440 | tf_op jit(solution)/shard_map/ppermute | solution.py:318
  67.2 6.6 %collective-permute-start.4 = (bf16[48,8,128]{2,1,0:T(8,128)(2,1)S(1)}, bf16[48,8,128]{2,1,0:T(8,128)(2,1)S(1)}, u32[]{:S(2)}, u32[]{:S(2)}) collective-permute-start(bf16[48,8,128]{2,1,0:T(8,128)(2,1)S(1)} %collective-permute-done.3.refs_6_), channel_id=1, source_target_pairs={{0,28},{4,0},{8,4},{12,8},{16,12},{20,16},{24,20},{28,24},{1,29},{... | collective-permute-start | bytes 294920 | tf_op jit(solution)/shard_map/ppermute | solution.py:306
  73.8 3.8 %collective-permute-start.8 = (bf16[48,8,128]{2,1,0:T(8,128)(2,1)S(1)}, bf16[48,8,128]{2,1,0:T(8,128)(2,1)S(1)}, u32[]{:S(2)}, u32[]{:S(2)}) collective-permute-start(bf16[48,8,128]{2,1,0:T(8,128)(2,1)S(1)} %collective-permute-done.4.refs_5_), channel_id=1, source_target_pairs={{0,28},{4,0},{8,4},{12,8},{16,12},{20,16},{24,20},{28,24},{1,29},{... | collective-permute-start | bytes 294920 | tf_op jit(solution)/shard_map/ppermute | solution.py:306
  74.6 12.8 %collective-permute-start.11 = (bf16[4,256,128]{2,1,0:T(8,128)(2,1)S(1)}, bf16[4,256,128]{2,1,0:T(8,128)(2,1)S(1)}, u32[]{:S(2)}, u32[]{:S(2)}) collective-permute-start(bf16[4,256,128]{2,1,0:T(8,128)(2,1)S(1)} %collective-permute-done.5.rest_3_), channel_id=1, source_target_pairs={{0,4},{4,8},{8,12},{12,16},{16,20},{20,24},{24,28},{28,0},{1,5},{5... | collective-permute-start | bytes 786440 | tf_op jit(solution)/shard_map/ppermute | solution.py:306
  75.3 12.1 %collective-permute-start.12 = (bf16[4,256,128]{2,1,0:T(8,128)(2,1)S(1)}, bf16[4,256,128]{2,1,0:T(8,128)(2,1)S(1)}, u32[]{:S(2)}, u32[]{:S(2)}) collective-permute-start(bf16[4,256,128]{2,1,0:T(8,128)(2,1)S(1)} %collective-permute-done.6.rest_4_), channel_id=1, source_target_pairs={{0,4},{4,8},{8,12},{12,16},{16,20},{20,24},{24,28},{28,64},{64,68}... | collective-permute-start | bytes 786440 | tf_op jit(solution)/shard_map/ppermute | solution.py:318
  77.6 3.8 %collective-permute-start.9 = (bf16[48,8,128]{2,1,0:T(8,128)(2,1)S(1)}, bf16[48,8,128]{2,1,0:T(8,128)(2,1)S(1)}, u32[]{:S(2)}, u32[]{:S(2)}) collective-permute-start(bf16[48,8,128]{2,1,0:T(8,128)(2,1)S(1)} %collective-permute-done.8.refs_4_), channel_id=1, source_target_pairs={{0,28},{4,0},{8,4},{12,8},{16,12},{20,16},{24,20},{28,24},{1,29},{... | collective-permute-start | bytes 294920 | tf_op jit(solution)/shard_map/ppermute | solution.py:306
  79.6 7.8 %collective-permute-start.7 = (bf16[48,8,128]{2,1,0:T(8,128)(2,1)S(1)}, bf16[48,8,128]{2,1,0:T(8,128)(2,1)S(1)}, u32[]{:S(2)}, u32[]{:S(2)}) collective-permute-start(bf16[48,8,128]{2,1,0:T(8,128)(2,1)S(1)} %gather_fusion.1), channel_id=1, source_target_pairs={{0,4},{4,8},{8,12},{12,16},{16,20},{20,24},{24,28},{28,0},{1,5},{5... | collective-permute-start | bytes 294920 | tf_op jit(solution)/shard_map/ppermute | solution.py:306
  81.4 6.0 %collective-permute-start.10 = (bf16[48,8,128]{2,1,0:T(8,128)(2,1)S(1)}, bf16[48,8,128]{2,1,0:T(8,128)(2,1)S(1)}, u32[]{:S(2)}, u32[]{:S(2)}) collective-permute-start(bf16[48,8,128]{2,1,0:T(8,128)(2,1)S(1)} %collective-permute-done.9.refs_3_), channel_id=1, source_target_pairs={{0,28},{4,0},{8,4},{12,8},{16,12},{20,16},{24,20},{28,24},{1,29},{... | collective-permute-start | bytes 294920 | tf_op jit(solution)/shard_map/ppermute | solution.py:306
  87.5 12.2 %collective-permute-start.13 = (bf16[8,24,8,128]{3,2,1,0:T(8,128)(2,1)S(1)}, bf16[8,24,8,128]{3,2,1,0:T(8,128)(2,1)S(1)}, u32[]{:S(2)}, u32[]{:S(2)}) collective-permute-start(bf16[8,24,8,128]{3,2,1,0:T(8,128)(2,1)S(1)} %get-tuple-element.63.rest_9_), channel_id=1, source_target_pairs={{0,64},{64,128},{128,192},{192,0},{1,65},{65,129},{129,193},{193,1... | collective-permute-start | bytes 1179656 | tf_op jit(solution)/shard_map/ppermute | solution.py:306
  87.6 6.8 %collective-permute-start.16 = (bf16[4,256,128]{2,1,0:T(8,128)(2,1)S(1)}, bf16[4,256,128]{2,1,0:T(8,128)(2,1)S(1)}, u32[]{:S(2)}, u32[]{:S(2)}) collective-permute-start(bf16[4,256,128]{2,1,0:T(8,128)(2,1)S(1)} %collective-permute-done.11.rest_5_), channel_id=1, source_target_pairs={{0,4},{4,8},{8,12},{12,16},{16,20},{20,24},{24,28},{28,0},{1,5},{5... | collective-permute-start | bytes 786440 | tf_op jit(solution)/shard_map/ppermute | solution.py:306
  88.3 11.2 %collective-permute-start.17 = (bf16[4,256,128]{2,1,0:T(8,128)(2,1)S(1)}, bf16[4,256,128]{2,1,0:T(8,128)(2,1)S(1)}, u32[]{:S(2)}, u32[]{:S(2)}) collective-permute-start(bf16[4,256,128]{2,1,0:T(8,128)(2,1)S(1)} %collective-permute-done.12.rest_6_), channel_id=1, source_target_pairs={{0,4},{4,8},{8,12},{12,16},{16,20},{20,24},{24,28},{28,64},{64,68}... | collective-permute-start | bytes 786440 | tf_op jit(solution)/shard_map/ppermute | solution.py:318
  89.1 11.2 %collective-permute-start.14 = (bf16[8,24,8,128]{3,2,1,0:T(8,128)(2,1)S(1)}, bf16[8,24,8,128]{3,2,1,0:T(8,128)(2,1)S(1)}, u32[]{:S(2)}, u32[]{:S(2)}) collective-permute-start(bf16[8,24,8,128]{3,2,1,0:T(8,128)(2,1)S(1)} %get-tuple-element.63.rest_9_), channel_id=1, source_target_pairs={{0,192},{64,0},{128,64},{192,128},{1,193},{65,1},{129,65},{193,129... | collective-permute-start | bytes 1179656 | tf_op jit(solution)/shard_map/ppermute | solution.py:306
  91.1 18.6 %collective-permute-start.15 = (bf16[8,24,8,128]{3,2,1,0:T(8,128)(2,1)S(1)}, bf16[8,24,8,128]{3,2,1,0:T(8,128)(2,1)}, u32[]{:S(2)}, u32[]{:S(2)}) collective-permute-start(bf16[8,24,8,128]{3,2,1,0:T(8,128)(2,1)S(1)} %get-tuple-element.63.rest_9_), channel_id=1, source_target_pairs={{0,128},{64,192},{128,0},{192,64},{1,129},{65,193},{129,1},{193,65... | collective-permute-start | bytes 1179656 | tf_op jit(solution)/shard_map/ppermute | solution.py:306
  94.4 30.3 %collective-permute-start.18 = (bf16[8,24,8,128]{3,2,1,0:T(8,128)(2,1)S(1)}, bf16[8,24,8,128]{3,2,1,0:T(8,128)(2,1)}, u32[]{:S(2)}, u32[]{:S(2)}) collective-permute-start(bf16[8,24,8,128]{3,2,1,0:T(8,128)(2,1)S(1)} %get-tuple-element.69.rest_9_), channel_id=1, source_target_pairs={{0,64},{64,128},{128,192},{192,0},{1,65},{65,129},{129,193},{193,1... | collective-permute-start | bytes 1179656 | tf_op jit(solution)/shard_map/ppermute | solution.py:306
  99.6 25.2 %collective-permute-start.19 = (bf16[8,24,8,128]{3,2,1,0:T(8,128)(2,1)S(1)}, bf16[8,24,8,128]{3,2,1,0:T(8,128)(2,1)}, u32[]{:S(2)}, u32[]{:S(2)}) collective-permute-start(bf16[8,24,8,128]{3,2,1,0:T(8,128)(2,1)S(1)} %get-tuple-element.69.rest_9_), channel_id=1, source_target_pairs={{0,192},{64,0},{128,64},{192,128},{1,193},{65,1},{129,65},{193,129... | collective-permute-start | bytes 1179656 | tf_op jit(solution)/shard_map/ppermute | solution.py:306
  99.8 26.9 %collective-permute-start.20 = (bf16[8,24,8,128]{3,2,1,0:T(8,128)(2,1)S(1)}, bf16[8,24,8,128]{3,2,1,0:T(8,128)(2,1)}, u32[]{:S(2)}, u32[]{:S(2)}) collective-permute-start(bf16[8,24,8,128]{3,2,1,0:T(8,128)(2,1)S(1)} %get-tuple-element.69.rest_9_), channel_id=1, source_target_pairs={{0,128},{64,192},{128,0},{192,64},{1,129},{65,193},{129,1},{193,65... | collective-permute-start | bytes 1179656 | tf_op jit(solution)/shard_map/ppermute | solution.py:306
  126.6 29.7 %all-to-all-start.3 = ((bf16[8,128,512]{2,1,0:T(8,128)(2,1)}), bf16[8,128,512]{2,1,0:T(8,128)(2,1)S(1)}, u32[]{:S(2)}, u32[]{:S(2)}) async-start(bf16[8,128,512]{2,1,0:T(8,128)(2,1)} %attend.2), calls=%async_computation.3 | async-start | bytes 2097152 | tf_op jit(solution)/shard_map/all_to_all | solution.py:360
  (26 other events, 392.9 us)

commit v8 on v7

--- a/solution.py
+++ b/solution.py
@@ -150,7 +150,7 @@
             (KEY_VALUE_HEADS, PAIR_ROWS, HEAD_SIZE), jnp.bfloat16
         ),
         cost_estimate=pl.CostEstimate(flops=0, bytes_accessed=1 << 20, transcendentals=0),
-        compiler_params=pltpu.CompilerParams(vmem_limit_bytes=8 << 20),
+        compiler_params=pltpu.CompilerParams(vmem_limit_bytes=60 << 20),
         name="split_pairs",
     )(keys, values)
 

time: 178 us -> 178 us (level); the launches traced: 179 us -> 176 us
  Pallas kernels: 29 us -> 32.7 us
  waiting for transfers between devices: 56 us -> 53.3 us
  local copies, waits for them, and re-layouts: 8.62 us -> 6.67 us
    all_to_all x1, waiting for transfers between devices: 4.59 us -> 0.04 us  [shards(): returned += [lax.all_to_all(mixed, HEAD_AXES, 0, 0, tiled=True)]]
    pallas_call x2, Pallas kernels: 24 us -> 26.6 us  [attend_half(): pl.pallas_call(functools.partial(attend_kernel, half), out_shape=jax.Shap...]
    ppermute x17, waiting for transfers between devices: 25 us -> 26.9 us  [shifted(): lax.ppermute(value, axis, [(n, (n + by) % count) for n in range(count)])]
    unnamed x50 -> x46, local copies, waits for them, and re-layouts: 4.25 us -> 2.3 us
  transfers between devices with their start and end apart: 25 -> 25, of which waited for: 14 -> 13; matrix products, arithmetic and copies ran while one was open for 4% -> 4% of each run, Pallas kernels for 14% -> 16%
where the time goes in v8:
time: 178 us; the launch traced here: 176 us
  starting transfers between devices  60.8 us (34%)
  waiting for transfers between devices  53.3 us (30%)
  Pallas kernels  32.7 us (18%)
  blocking collectives  19.8 us (11%)
  local copies, waits for them, and re-layouts  6.67 us (4%)
  other arithmetic  2.45 us (1%)
    ppermute x17, waiting for transfers between devices, shifted(): lax.ppermute(value, axis, [(n, (n + by) % count) for n in range(count)])  26.9 us
    pallas_call x2, Pallas kernels, attend_half(): pl.pallas_call(functools.partial(attend_kernel, half), out_shape=jax.Shap...  26.6 us
    all_to_all x1, blocking collectives, shards(): returned += [lax.all_to_all(mixed, HEAD_AXES, 0, 0, tiled=True)]  19.8 us
    ppermute x17, starting transfers between devices, shifted(): lax.ppermute(value, axis, [(n, (n + by) % count) for n in range(count)])  18.1 us
    all_to_all x1, starting transfers between devices, shards(): returned += [lax.all_to_all(mixed, HEAD_AXES, 0, 0, tiled=True)]  14.1 us
    all_to_all x1, starting transfers between devices, shards(): sliced = lax.all_to_all(cut_slices(pairs), ROW_AXES, 0, 0, tiled=True)  10.5 us
    ppermute x4, waiting for transfers between devices, passed_on(): return (shifted(first, 'z', 1), lax.ppermute(second, ROW_AXES, onward))  9.51 us
    all_to_all x1, waiting for transfers between devices, shards(): sliced = lax.all_to_all(cut_slices(pairs), ROW_AXES, 0, 0, tiled=True)  9.39 us
  transfers between devices with their start and end apart: 25, of which 13 were waited for; matrix products, arithmetic and copies ran while one was open for 4% of the time, Pallas kernels for 16%

profile of v8, /device:TPU:1, one launch (start us, length us, event | category | flops | bytes accessed | tf_op | source)
XLA Modules:
  0.0 176.3 jit_solution(7678625995035220479)
XLA Ops:
  0.0 2.0 %split_pairs.1 = bf16[8,256,128]{2,1,0:T(8,128)(2,1)} custom-call(bf16[128,1024]{1,0:T(8,128)(2,1)} %key_ref.1, bf16[128,1024]{1,0:T(8,128)(2,1)} %value_ref.1), custom_call_target="tpu_custom_call" | custom-call | bytes 1048576 | tf_op jit(solution)/shard_map/split_pairs/pallas_call | solution.py:147
  2.0 6.8 %all-to-all-start = ((bf16[8,256,128]{2,1,0:T(8,128)(2,1)}), bf16[8,256,128]{2,1,0:T(8,128)(2,1)S(1)}, u32[]{:S(2)}, u32[]{:S(2)}) async-start(bf16[8,256,128]{2,1,0:T(8,128)(2,1)} %split_pairs.1), calls=%async_computation | async-start | bytes 1048576 | tf_op jit(solution)/shard_map/all_to_all | solution.py:309
  10.8 7.5 %all-to-all-done.tiles = bf16[8,256,128]{2,1,0:T(8,128)(2,1)S(1)} async-done(((bf16[8,256,128]{2,1,0:T(8,128)(2,1)}), bf16[8,256,128]{2,1,0:T(8,128)(2,1)S(1)}, u32[]{:S(2)}, u32[]{:S(2)}) %all-to-all-start) | async-done | bytes 524320 | tf_op jit(solution)/shard_map/all_to_all | solution.py:309
  19.2 10.5 %all-to-all-start.1 = ((bf16[32,8,8,128]{3,2,1,0:T(8,128)(2,1)}), bf16[32,8,8,128]{3,2,1,0:T(8,128)(2,1)}, u32[]{:S(2)}, u32[]{:S(2)}) async-start(bf16[32,8,8,128]{3,2,1,0:T(8,128)(2,1)} %cut_slices.1), calls=%async_computation.1 | async-start | bytes 1048576 | tf_op jit(solution)/shard_map/all_to_all | solution.py:320
  34.4 9.4 %all-to-all-done.1 = bf16[32,8,8,128]{3,2,1,0:T(8,128)(2,1)} async-done(((bf16[32,8,8,128]{3,2,1,0:T(8,128)(2,1)}), bf16[32,8,8,128]{3,2,1,0:T(8,128)(2,1)}, u32[]{:S(2)}, u32[]{:S(2)}) %all-to-all-start.1) | async-done | bytes 524320 | tf_op jit(solution)/shard_map/all_to_all | solution.py:320
  43.8 9.4 %all-to-all-start.2 = ((bf16[8,128,1024]{2,1,0:T(8,128)(2,1)}), bf16[8,128,1024]{2,1,0:T(8,128)(2,1)S(1)}, u32[]{:S(2)}, u32[]{:S(2)}) async-start(bf16[8,128,1024]{2,1,0:T(8,128)(2,1)} %split_heads.1), calls=%async_computation.2 | async-start | bytes 4194304 | tf_op jit(solution)/shard_map/all_to_all | solution.py:336
  60.3 2.3 %collective-permute-done.2.refs_7_ = bf16[48,8,128]{2,1,0:T(8,128)(2,1)S(1)} collective-permute-done((bf16[48,8,128]{2,1,0:T(8,128)(2,1)S(1)}, bf16[48,8,128]{2,1,0:T(8,128)(2,1)S(1)}, u32[]{:S(2)}, u32[]{:S(2)}) %collective-permute-start.2) | collective-permute-done | bytes 98336 | tf_op jit(solution)/shard_map/ppermute | solution.py:306
  63.8 2.5 %collective-permute-done.3.refs_6_ = bf16[48,8,128]{2,1,0:T(8,128)(2,1)S(1)} collective-permute-done((bf16[48,8,128]{2,1,0:T(8,128)(2,1)S(1)}, bf16[48,8,128]{2,1,0:T(8,128)(2,1)S(1)}, u32[]{:S(2)}, u32[]{:S(2)}) %collective-permute-start.3) | collective-permute-done | bytes 98336 | tf_op jit(solution)/shard_map/ppermute | solution.py:306
  66.4 2.4 %collective-permute-start.4 = (bf16[48,8,128]{2,1,0:T(8,128)(2,1)S(1)}, bf16[48,8,128]{2,1,0:T(8,128)(2,1)S(1)}, u32[]{:S(2)}, u32[]{:S(2)}) collective-permute-start(bf16[48,8,128]{2,1,0:T(8,128)(2,1)S(1)} %collective-permute-done.3.refs_6_), channel_id=1, source_target_pairs={{0,28},{4,0},{8,4},{12,8},{16,12},{20,16},{24,20},{28,24},{1,29},{... | collective-permute-start | bytes 294920 | tf_op jit(solution)/shard_map/ppermute | solution.py:306
  68.8 4.2 %collective-permute-done.6.rest_4_ = bf16[4,256,128]{2,1,0:T(8,128)(2,1)S(1)} collective-permute-done((bf16[4,256,128]{2,1,0:T(8,128)(2,1)S(1)}, bf16[4,256,128]{2,1,0:T(8,128)(2,1)S(1)}, u32[]{:S(2)}, u32[]{:S(2)}) %collective-permute-start.6) | collective-permute-done | bytes 262176 | tf_op jit(solution)/shard_map/ppermute | solution.py:318
  74.5 2.3 %collective-permute-done.8.refs_4_ = bf16[48,8,128]{2,1,0:T(8,128)(2,1)S(1)} collective-permute-done((bf16[48,8,128]{2,1,0:T(8,128)(2,1)S(1)}, bf16[48,8,128]{2,1,0:T(8,128)(2,1)S(1)}, u32[]{:S(2)}, u32[]{:S(2)}) %collective-permute-start.8) | collective-permute-done | bytes 98336 | tf_op jit(solution)/shard_map/ppermute | solution.py:306
  76.7 2.0 %collective-permute-start.9 = (bf16[48,8,128]{2,1,0:T(8,128)(2,1)S(1)}, bf16[48,8,128]{2,1,0:T(8,128)(2,1)S(1)}, u32[]{:S(2)}, u32[]{:S(2)}) collective-permute-start(bf16[48,8,128]{2,1,0:T(8,128)(2,1)S(1)} %collective-permute-done.8.refs_4_), channel_id=1, source_target_pairs={{0,28},{4,0},{8,4},{12,8},{16,12},{20,16},{24,20},{28,24},{1,29},{... | collective-permute-start | bytes 294920 | tf_op jit(solution)/shard_map/ppermute | solution.py:306
  78.7 1.8 %collective-permute-done.9.refs_3_ = bf16[48,8,128]{2,1,0:T(8,128)(2,1)S(1)} collective-permute-done((bf16[48,8,128]{2,1,0:T(8,128)(2,1)S(1)}, bf16[48,8,128]{2,1,0:T(8,128)(2,1)S(1)}, u32[]{:S(2)}, u32[]{:S(2)}) %collective-permute-start.9) | collective-permute-done | bytes 98336 | tf_op jit(solution)/shard_map/ppermute | solution.py:306
  80.5 3.1 %collective-permute-start.10 = (bf16[48,8,128]{2,1,0:T(8,128)(2,1)S(1)}, bf16[48,8,128]{2,1,0:T(8,128)(2,1)S(1)}, u32[]{:S(2)}, u32[]{:S(2)}) collective-permute-start(bf16[48,8,128]{2,1,0:T(8,128)(2,1)S(1)} %collective-permute-done.9.refs_3_), channel_id=1, source_target_pairs={{0,28},{4,0},{8,4},{12,8},{16,12},{20,16},{24,20},{28,24},{1,29},{... | collective-permute-start | bytes 294920 | tf_op jit(solution)/shard_map/ppermute | solution.py:306
  83.6 2.9 %collective-permute-done.7.refs_1_ = bf16[48,8,128]{2,1,0:T(8,128)(2,1)S(1)} collective-permute-done((bf16[48,8,128]{2,1,0:T(8,128)(2,1)S(1)}, bf16[48,8,128]{2,1,0:T(8,128)(2,1)S(1)}, u32[]{:S(2)}, u32[]{:S(2)}) %collective-permute-start.7) | collective-permute-done | bytes 98336 | tf_op jit(solution)/shard_map/ppermute | solution.py:306
  88.2 2.0 %collective-permute-start.14 = (bf16[8,24,8,128]{3,2,1,0:T(8,128)(2,1)S(1)}, bf16[8,24,8,128]{3,2,1,0:T(8,128)(2,1)S(1)}, u32[]{:S(2)}, u32[]{:S(2)}) collective-permute-start(bf16[8,24,8,128]{3,2,1,0:T(8,128)(2,1)S(1)} %get-tuple-element.63.rest_9_), channel_id=1, source_target_pairs={{0,192},{64,0},{128,64},{192,128},{1,193},{65,1},{129,65},{193,129... | collective-permute-start | bytes 1179656 | tf_op jit(solution)/shard_map/ppermute | solution.py:306
  90.7 2.8 %collective-permute-done.16.rest_7_ = bf16[4,256,128]{2,1,0:T(8,128)(2,1)S(1)} collective-permute-done((bf16[4,256,128]{2,1,0:T(8,128)(2,1)S(1)}, bf16[4,256,128]{2,1,0:T(8,128)(2,1)S(1)}, u32[]{:S(2)}, u32[]{:S(2)}) %collective-permute-start.16) | collective-permute-done | bytes 262176 | tf_op jit(solution)/shard_map/ppermute | solution.py:306
  94.6 4.1 %collective-permute-done.17.rest_8_ = bf16[4,256,128]{2,1,0:T(8,128)(2,1)S(1)} collective-permute-done((bf16[4,256,128]{2,1,0:T(8,128)(2,1)S(1)}, bf16[4,256,128]{2,1,0:T(8,128)(2,1)S(1)}, u32[]{:S(2)}, u32[]{:S(2)}) %collective-permute-start.17) | collective-permute-done | bytes 262176 | tf_op jit(solution)/shard_map/ppermute | solution.py:318
  100.4 8.5 %collective-permute-done.15.rest_12_ = bf16[8,24,8,128]{3,2,1,0:T(8,128)(2,1)} collective-permute-done((bf16[8,24,8,128]{3,2,1,0:T(8,128)(2,1)S(1)}, bf16[8,24,8,128]{3,2,1,0:T(8,128)(2,1)}, u32[]{:S(2)}, u32[]{:S(2)}) %collective-permute-start.15) | collective-permute-done | bytes 393248 | tf_op jit(solution)/shard_map/ppermute | solution.py:306
  110.2 11.7 %attend.2 = bf16[8,128,512]{2,1,0:T(8,128)(2,1)} custom-call(s32[8]{0:T(128)} %fusion.9.turns, s32[640]{0:T(1024)} %reshape.77.tile_of, f32[640]{0:T(1024)} %select_n.76.bias_of, s32[2]{0:T(128)} %pad_add_fusion.3.spot, bf16[8,128,1024]{2,1,0:T(8,128)(2,1)} %copy-done.4, bf16[2,4,256,128]{3,2,1,0:T(8,128)(2,1)} %bitcast.6, bf16[4,256,128]{2,1,0:T(8,128)(2,1)} %copy-done.5, ...), custom_call_target="tpu_custom_call" | custom-call | flops 1610612736 | bytes 8388608 | tf_op jit(solution)/shard_map/attend/pallas_call | solution.py:113
  121.9 3.8 %collective-permute-done.20.rest_12_ = bf16[8,24,8,128]{3,2,1,0:T(8,128)(2,1)} collective-permute-done((bf16[8,24,8,128]{3,2,1,0:T(8,128)(2,1)S(1)}, bf16[8,24,8,128]{3,2,1,0:T(8,128)(2,1)}, u32[]{:S(2)}, u32[]{:S(2)}) %collective-permute-start.20) | collective-permute-done | bytes 393248 | tf_op jit(solution)/shard_map/ppermute | solution.py:306
  125.8 14.1 %all-to-all-start.3 = ((bf16[8,128,512]{2,1,0:T(8,128)(2,1)}), bf16[8,128,512]{2,1,0:T(8,128)(2,1)S(1)}, u32[]{:S(2)}, u32[]{:S(2)}) async-start(bf16[8,128,512]{2,1,0:T(8,128)(2,1)} %attend.2), calls=%async_computation.3 | async-start | bytes 2097152 | tf_op jit(solution)/shard_map/all_to_all | solution.py:360
  139.9 14.9 %attend.3 = bf16[8,128,512]{2,1,0:T(8,128)(2,1)} custom-call(s32[8]{0:T(128)} %fusion.9.turns, s32[640]{0:T(1024)} %reshape.77.tile_of, f32[640]{0:T(1024)} %select_n.76.bias_of, s32[2]{0:T(128)} %pad_add_fusion.3.spot, bf16[8,128,1024]{2,1,0:T(8,128)(2,1)} %copy-done.4, bf16[2,4,256,128]{3,2,1,0:T(8,128)(2,1)} %bitcast.7, bf16[4,256,128]{2,1,0:T(8,128)(2,1)} %copy-done.5, ...), custom_call_target="tpu_custom_call" | custom-call | flops 1610612736 | bytes 8388608 | tf_op jit(solution)/shard_map/attend/pallas_call | solution.py:113
  154.9 19.8 %all_to_all.25.refs_1_ = bf16[8,128,512]{2,1,0:T(8,128)(2,1)S(1)} all-to-all(bf16[8,128,512]{2,1,0:T(8,128)(2,1)} %attend.3), channel_id=1, replica_groups=mesh['x'=4,'c'=2,'z'=8,'y'=4] {'c','y'}, dimensions={0} | all-to-all | bytes 2097152 | tf_op jit(solution)/shard_map/all_to_all | solution.py:360
  (120 shorter events, 25.0 us)
Async XLA Ops:
  2.0 16.2 %all-to-all-start = ((bf16[8,256,128]{2,1,0:T(8,128)(2,1)}), bf16[8,256,128]{2,1,0:T(8,128)(2,1)S(1)}, u32[]{:S(2)}, u32[]{:S(2)}) async-start(bf16[8,256,128]{2,1,0:T(8,128)(2,1)} %split_pairs.1), calls=%async_computation | async-start | bytes 1048576 | tf_op jit(solution)/shard_map/all_to_all | solution.py:309
  19.2 24.6 %all-to-all-start.1 = ((bf16[32,8,8,128]{3,2,1,0:T(8,128)(2,1)}), bf16[32,8,8,128]{3,2,1,0:T(8,128)(2,1)}, u32[]{:S(2)}, u32[]{:S(2)}) async-start(bf16[32,8,8,128]{3,2,1,0:T(8,128)(2,1)} %cut_slices.1), calls=%async_computation.1 | async-start | bytes 1048576 | tf_op jit(solution)/shard_map/all_to_all | solution.py:320
  32.0 23.8 %collective-permute-start = (bf16[4,256,128]{2,1,0:T(8,128)(2,1)S(1)}, bf16[4,256,128]{2,1,0:T(8,128)(2,1)S(1)}, u32[]{:S(2)}, u32[]{:S(2)}) collective-permute-start(bf16[4,256,128]{2,1,0:T(8,128)(2,1)S(1)} %get-tuple-element.82), channel_id=1, source_target_pairs={{0,4},{4,8},{8,12},{12,16},{16,20},{20,24},{24,28},{28,0},{1,5},{5... | collective-permute-start | bytes 786440 | tf_op jit(solution)/shard_map/ppermute | solution.py:306
  33.2 23.8 %collective-permute-start.1 = (bf16[4,256,128]{2,1,0:T(8,128)(2,1)S(1)}, bf16[4,256,128]{2,1,0:T(8,128)(2,1)S(1)}, u32[]{:S(2)}, u32[]{:S(2)}) collective-permute-start(bf16[4,256,128]{2,1,0:T(8,128)(2,1)S(1)} %get-tuple-element.81), channel_id=1, source_target_pairs={{0,4},{4,8},{8,12},{12,16},{16,20},{20,24},{24,28},{28,64},{64,68}... | collective-permute-start | bytes 786440 | tf_op jit(solution)/shard_map/ppermute | solution.py:318
  43.8 65.1 %all-to-all-start.2 = ((bf16[8,128,1024]{2,1,0:T(8,128)(2,1)}), bf16[8,128,1024]{2,1,0:T(8,128)(2,1)S(1)}, u32[]{:S(2)}, u32[]{:S(2)}) async-start(bf16[8,128,1024]{2,1,0:T(8,128)(2,1)} %split_heads.1), calls=%async_computation.2 | async-start | bytes 4194304 | tf_op jit(solution)/shard_map/all_to_all | solution.py:336
  58.8 3.8 %collective-permute-start.2 = (bf16[48,8,128]{2,1,0:T(8,128)(2,1)S(1)}, bf16[48,8,128]{2,1,0:T(8,128)(2,1)S(1)}, u32[]{:S(2)}, u32[]{:S(2)}) collective-permute-start(bf16[48,8,128]{2,1,0:T(8,128)(2,1)S(1)} %gather_fusion.1), channel_id=1, source_target_pairs={{0,28},{4,0},{8,4},{12,8},{16,12},{20,16},{24,20},{28,24},{1,29},{... | collective-permute-start | bytes 294920 | tf_op jit(solution)/shard_map/ppermute | solution.py:306
  58.8 9.9 %collective-permute-start.5 = (bf16[4,256,128]{2,1,0:T(8,128)(2,1)S(1)}, bf16[4,256,128]{2,1,0:T(8,128)(2,1)S(1)}, u32[]{:S(2)}, u32[]{:S(2)}) collective-permute-start(bf16[4,256,128]{2,1,0:T(8,128)(2,1)S(1)} %collective-permute-done.rest_1_), channel_id=1, source_target_pairs={{0,4},{4,8},{8,12},{12,16},{16,20},{20,24},{24,28},{28,0},{1,5},{5... | collective-permute-start | bytes 786440 | tf_op jit(solution)/shard_map/ppermute | solution.py:306
  60.3 12.7 %collective-permute-start.6 = (bf16[4,256,128]{2,1,0:T(8,128)(2,1)S(1)}, bf16[4,256,128]{2,1,0:T(8,128)(2,1)S(1)}, u32[]{:S(2)}, u32[]{:S(2)}) collective-permute-start(bf16[4,256,128]{2,1,0:T(8,128)(2,1)S(1)} %collective-permute-done.1.rest_2_), channel_id=1, source_target_pairs={{0,4},{4,8},{8,12},{12,16},{16,20},{20,24},{24,28},{28,64},{64,68}... | collective-permute-start | bytes 786440 | tf_op jit(solution)/shard_map/ppermute | solution.py:318
  66.4 6.6 %collective-permute-start.4 = (bf16[48,8,128]{2,1,0:T(8,128)(2,1)S(1)}, bf16[48,8,128]{2,1,0:T(8,128)(2,1)S(1)}, u32[]{:S(2)}, u32[]{:S(2)}) collective-permute-start(bf16[48,8,128]{2,1,0:T(8,128)(2,1)S(1)} %collective-permute-done.3.refs_6_), channel_id=1, source_target_pairs={{0,28},{4,0},{8,4},{12,8},{16,12},{20,16},{24,20},{28,24},{1,29},{... | collective-permute-start | bytes 294920 | tf_op jit(solution)/shard_map/ppermute | solution.py:306
  73.0 3.8 %collective-permute-start.8 = (bf16[48,8,128]{2,1,0:T(8,128)(2,1)S(1)}, bf16[48,8,128]{2,1,0:T(8,128)(2,1)S(1)}, u32[]{:S(2)}, u32[]{:S(2)}) collective-permute-start(bf16[48,8,128]{2,1,0:T(8,128)(2,1)S(1)} %collective-permute-done.4.refs_5_), channel_id=1, source_target_pairs={{0,28},{4,0},{8,4},{12,8},{16,12},{20,16},{24,20},{28,24},{1,29},{... | collective-permute-start | bytes 294920 | tf_op jit(solution)/shard_map/ppermute | solution.py:306
  73.8 12.8 %collective-permute-start.11 = (bf16[4,256,128]{2,1,0:T(8,128)(2,1)S(1)}, bf16[4,256,128]{2,1,0:T(8,128)(2,1)S(1)}, u32[]{:S(2)}, u32[]{:S(2)}) collective-permute-start(bf16[4,256,128]{2,1,0:T(8,128)(2,1)S(1)} %collective-permute-done.5.rest_3_), channel_id=1, source_target_pairs={{0,4},{4,8},{8,12},{12,16},{16,20},{20,24},{24,28},{28,0},{1,5},{5... | collective-permute-start | bytes 786440 | tf_op jit(solution)/shard_map/ppermute | solution.py:306
  74.4 12.1 %collective-permute-start.12 = (bf16[4,256,128]{2,1,0:T(8,128)(2,1)S(1)}, bf16[4,256,128]{2,1,0:T(8,128)(2,1)S(1)}, u32[]{:S(2)}, u32[]{:S(2)}) collective-permute-start(bf16[4,256,128]{2,1,0:T(8,128)(2,1)S(1)} %collective-permute-done.6.rest_4_), channel_id=1, source_target_pairs={{0,4},{4,8},{8,12},{12,16},{16,20},{20,24},{24,28},{28,64},{64,68}... | collective-permute-start | bytes 786440 | tf_op jit(solution)/shard_map/ppermute | solution.py:318
  76.7 3.8 %collective-permute-start.9 = (bf16[48,8,128]{2,1,0:T(8,128)(2,1)S(1)}, bf16[48,8,128]{2,1,0:T(8,128)(2,1)S(1)}, u32[]{:S(2)}, u32[]{:S(2)}) collective-permute-start(bf16[48,8,128]{2,1,0:T(8,128)(2,1)S(1)} %collective-permute-done.8.refs_4_), channel_id=1, source_target_pairs={{0,28},{4,0},{8,4},{12,8},{16,12},{20,16},{24,20},{28,24},{1,29},{... | collective-permute-start | bytes 294920 | tf_op jit(solution)/shard_map/ppermute | solution.py:306
  78.7 7.8 %collective-permute-start.7 = (bf16[48,8,128]{2,1,0:T(8,128)(2,1)S(1)}, bf16[48,8,128]{2,1,0:T(8,128)(2,1)S(1)}, u32[]{:S(2)}, u32[]{:S(2)}) collective-permute-start(bf16[48,8,128]{2,1,0:T(8,128)(2,1)S(1)} %gather_fusion.1), channel_id=1, source_target_pairs={{0,4},{4,8},{8,12},{12,16},{16,20},{20,24},{24,28},{28,0},{1,5},{5... | collective-permute-start | bytes 294920 | tf_op jit(solution)/shard_map/ppermute | solution.py:306
  80.5 6.0 %collective-permute-start.10 = (bf16[48,8,128]{2,1,0:T(8,128)(2,1)S(1)}, bf16[48,8,128]{2,1,0:T(8,128)(2,1)S(1)}, u32[]{:S(2)}, u32[]{:S(2)}) collective-permute-start(bf16[48,8,128]{2,1,0:T(8,128)(2,1)S(1)} %collective-permute-done.9.refs_3_), channel_id=1, source_target_pairs={{0,28},{4,0},{8,4},{12,8},{16,12},{20,16},{24,20},{28,24},{1,29},{... | collective-permute-start | bytes 294920 | tf_op jit(solution)/shard_map/ppermute | solution.py:306
  86.7 12.2 %collective-permute-start.13 = (bf16[8,24,8,128]{3,2,1,0:T(8,128)(2,1)S(1)}, bf16[8,24,8,128]{3,2,1,0:T(8,128)(2,1)S(1)}, u32[]{:S(2)}, u32[]{:S(2)}) collective-permute-start(bf16[8,24,8,128]{3,2,1,0:T(8,128)(2,1)S(1)} %get-tuple-element.63.rest_9_), channel_id=1, source_target_pairs={{0,64},{64,128},{128,192},{192,0},{1,65},{65,129},{129,193},{193,1... | collective-permute-start | bytes 1179656 | tf_op jit(solution)/shard_map/ppermute | solution.py:306
  86.7 6.8 %collective-permute-start.16 = (bf16[4,256,128]{2,1,0:T(8,128)(2,1)S(1)}, bf16[4,256,128]{2,1,0:T(8,128)(2,1)S(1)}, u32[]{:S(2)}, u32[]{:S(2)}) collective-permute-start(bf16[4,256,128]{2,1,0:T(8,128)(2,1)S(1)} %collective-permute-done.11.rest_5_), channel_id=1, source_target_pairs={{0,4},{4,8},{8,12},{12,16},{16,20},{20,24},{24,28},{28,0},{1,5},{5... | collective-permute-start | bytes 786440 | tf_op jit(solution)/shard_map/ppermute | solution.py:306
  87.5 11.2 %collective-permute-start.17 = (bf16[4,256,128]{2,1,0:T(8,128)(2,1)S(1)}, bf16[4,256,128]{2,1,0:T(8,128)(2,1)S(1)}, u32[]{:S(2)}, u32[]{:S(2)}) collective-permute-start(bf16[4,256,128]{2,1,0:T(8,128)(2,1)S(1)} %collective-permute-done.12.rest_6_), channel_id=1, source_target_pairs={{0,4},{4,8},{8,12},{12,16},{16,20},{20,24},{24,28},{28,64},{64,68}... | collective-permute-start | bytes 786440 | tf_op jit(solution)/shard_map/ppermute | solution.py:318
  88.2 11.2 %collective-permute-start.14 = (bf16[8,24,8,128]{3,2,1,0:T(8,128)(2,1)S(1)}, bf16[8,24,8,128]{3,2,1,0:T(8,128)(2,1)S(1)}, u32[]{:S(2)}, u32[]{:S(2)}) collective-permute-start(bf16[8,24,8,128]{3,2,1,0:T(8,128)(2,1)S(1)} %get-tuple-element.63.rest_9_), channel_id=1, source_target_pairs={{0,192},{64,0},{128,64},{192,128},{1,193},{65,1},{129,65},{193,129... | collective-permute-start | bytes 1179656 | tf_op jit(solution)/shard_map/ppermute | solution.py:306
  90.2 18.6 %collective-permute-start.15 = (bf16[8,24,8,128]{3,2,1,0:T(8,128)(2,1)S(1)}, bf16[8,24,8,128]{3,2,1,0:T(8,128)(2,1)}, u32[]{:S(2)}, u32[]{:S(2)}) collective-permute-start(bf16[8,24,8,128]{3,2,1,0:T(8,128)(2,1)S(1)} %get-tuple-element.63.rest_9_), channel_id=1, source_target_pairs={{0,128},{64,192},{128,0},{192,64},{1,129},{65,193},{129,1},{193,65... | collective-permute-start | bytes 1179656 | tf_op jit(solution)/shard_map/ppermute | solution.py:306
  93.5 28.4 %collective-permute-start.18 = (bf16[8,24,8,128]{3,2,1,0:T(8,128)(2,1)S(1)}, bf16[8,24,8,128]{3,2,1,0:T(8,128)(2,1)}, u32[]{:S(2)}, u32[]{:S(2)}) collective-permute-start(bf16[8,24,8,128]{3,2,1,0:T(8,128)(2,1)S(1)} %get-tuple-element.69.rest_9_), channel_id=1, source_target_pairs={{0,64},{64,128},{128,192},{192,0},{1,65},{65,129},{129,193},{193,1... | collective-permute-start | bytes 1179656 | tf_op jit(solution)/shard_map/ppermute | solution.py:306
  98.7 23.2 %collective-permute-start.19 = (bf16[8,24,8,128]{3,2,1,0:T(8,128)(2,1)S(1)}, bf16[8,24,8,128]{3,2,1,0:T(8,128)(2,1)}, u32[]{:S(2)}, u32[]{:S(2)}) collective-permute-start(bf16[8,24,8,128]{3,2,1,0:T(8,128)(2,1)S(1)} %get-tuple-element.69.rest_9_), channel_id=1, source_target_pairs={{0,192},{64,0},{128,64},{192,128},{1,193},{65,1},{129,65},{193,129... | collective-permute-start | bytes 1179656 | tf_op jit(solution)/shard_map/ppermute | solution.py:306
  98.9 26.9 %collective-permute-start.20 = (bf16[8,24,8,128]{3,2,1,0:T(8,128)(2,1)S(1)}, bf16[8,24,8,128]{3,2,1,0:T(8,128)(2,1)}, u32[]{:S(2)}, u32[]{:S(2)}) collective-permute-start(bf16[8,24,8,128]{3,2,1,0:T(8,128)(2,1)S(1)} %get-tuple-element.69.rest_9_), channel_id=1, source_target_pairs={{0,128},{64,192},{128,0},{192,64},{1,129},{65,193},{129,1},{193,65... | collective-permute-start | bytes 1179656 | tf_op jit(solution)/shard_map/ppermute | solution.py:306
  125.8 29.1 %all-to-all-start.3 = ((bf16[8,128,512]{2,1,0:T(8,128)(2,1)}), bf16[8,128,512]{2,1,0:T(8,128)(2,1)S(1)}, u32[]{:S(2)}, u32[]{:S(2)}) async-start(bf16[8,128,512]{2,1,0:T(8,128)(2,1)} %attend.2), calls=%async_computation.3 | async-start | bytes 2097152 | tf_op jit(solution)/shard_map/all_to_all | solution.py:360
  (24 other events, 387.6 us)

commit v9 on v8

--- a/solution.py
+++ b/solution.py
@@ -307,6 +307,7 @@
 
     pairs = split_pairs(key_state_rows, value_state_rows)
     pairs = lax.all_to_all(pairs, HEAD_AXES, 0, 0, tiled=True)
+    pairs, queries = lax.optimization_barrier((pairs, split_heads(queries)))
     own = pairs.reshape(CORES, ROW, PAIR_ROWS, HEAD_SIZE)
 
     onward = [
@@ -332,7 +333,6 @@
     sliced, tables, at, chain = lax.optimization_barrier((sliced, tables, at, chain))
     picked = sliced.reshape(SLICES * PARTS, SLICE_ROWS, HEAD_SIZE)[at]
 
-    queries = split_heads(queries)
     q = lax.all_to_all(queries, HEAD_AXES, 0, 0, tiled=True)
 
     behind = shifted(picked, "z", 1)

time: 178 us -> 180 us (1.011); the launches traced: 176 us -> 181 us
  waiting for transfers between devices: 53.3 us -> 60.9 us
  Pallas kernels: 32.7 us -> 28.2 us
    ppermute x17, waiting for transfers between devices: 26.9 us -> 33.6 us  [shifted(): lax.ppermute(value, axis, [(n, (n + by) % count) for n in range(count)])]
    pallas_call x2, Pallas kernels: 26.6 us -> 22.1 us  [attend_half(): pl.pallas_call(functools.partial(attend_kernel, half), out_shape=jax.Shap...]
    all_to_all x1, waiting for transfers between devices: 0.04 us -> 3.95 us  [shards(): returned += [lax.all_to_all(mixed, HEAD_AXES, 0, 0, tiled=True)]]
    ppermute x4, waiting for transfers between devices: 9.51 us -> 7.11 us  [passed_on(): return (shifted(first, 'z', 1), lax.ppermute(second, ROW_AXES, onward))]
  transfers between devices with their start and end apart: 25 -> 25, of which waited for: 13 -> 13; matrix products, arithmetic and copies ran while one was open for 4% -> 4% of each run, Pallas kernels for 16% -> 13%
where the time goes in v9:
time: 180 us; the launch traced here: 181 us
  waiting for transfers between devices  60.9 us (34%)
  starting transfers between devices  60.4 us (34%)
  Pallas kernels  28.2 us (16%)
  blocking collectives  20.2 us (11%)
  local copies, waits for them, and re-layouts  8.1 us (4%)
  other arithmetic  2.39 us (1%)
    ppermute x17, waiting for transfers between devices, shifted(): lax.ppermute(value, axis, [(n, (n + by) % count) for n in range(count)])  33.6 us
    pallas_call x2, Pallas kernels, attend_half(): pl.pallas_call(functools.partial(attend_kernel, half), out_shape=jax.Shap...  22.1 us
    all_to_all x1, blocking collectives, shards(): returned += [lax.all_to_all(mixed, HEAD_AXES, 0, 0, tiled=True)]  20.2 us
    ppermute x17, starting transfers between devices, shifted(): lax.ppermute(value, axis, [(n, (n + by) % count) for n in range(count)])  16.3 us
    all_to_all x1, starting transfers between devices, shards(): returned += [lax.all_to_all(mixed, HEAD_AXES, 0, 0, tiled=True)]  15.1 us
    all_to_all x1, starting transfers between devices, shards(): sliced = lax.all_to_all(cut_slices(pairs), ROW_AXES, 0, 0, tiled=True)  10.4 us
    all_to_all x1, waiting for transfers between devices, shards(): sliced = lax.all_to_all(cut_slices(pairs), ROW_AXES, 0, 0, tiled=True)  10.3 us
    all_to_all x1, starting transfers between devices, shards(): q = lax.all_to_all(queries, HEAD_AXES, 0, 0, tiled=True)  9.37 us
  transfers between devices with their start and end apart: 25, of which 13 were waited for; matrix products, arithmetic and copies ran while one was open for 4% of the time, Pallas kernels for 13%

profile of v9, /device:TPU:1, one launch (start us, length us, event | category | flops | bytes accessed | tf_op | source)
XLA Modules:
  0.0 180.7 jit_solution(10901223117458470902)
XLA Ops:
  0.0 2.1 %split_pairs.1 = bf16[8,256,128]{2,1,0:T(8,128)(2,1)} custom-call(bf16[128,1024]{1,0:T(8,128)(2,1)} %key_ref.1, bf16[128,1024]{1,0:T(8,128)(2,1)} %value_ref.1), custom_call_target="tpu_custom_call" | custom-call | bytes 1048576 | tf_op jit(solution)/shard_map/split_pairs/pallas_call | solution.py:147
  2.1 6.6 %all-to-all-start = ((bf16[8,256,128]{2,1,0:T(8,128)(2,1)}), bf16[8,256,128]{2,1,0:T(8,128)(2,1)S(1)}, u32[]{:S(2)}, u32[]{:S(2)}) async-start(bf16[8,256,128]{2,1,0:T(8,128)(2,1)} %split_pairs.1), calls=%async_computation | async-start | bytes 1048576 | tf_op jit(solution)/shard_map/all_to_all | solution.py:309
  12.2 5.9 %all-to-all-done.tiles = bf16[8,256,128]{2,1,0:T(8,128)(2,1)S(1)} async-done(((bf16[8,256,128]{2,1,0:T(8,128)(2,1)}), bf16[8,256,128]{2,1,0:T(8,128)(2,1)S(1)}, u32[]{:S(2)}, u32[]{:S(2)}) %all-to-all-start) | async-done | bytes 524320 | tf_op jit(solution)/shard_map/all_to_all | solution.py:309
  19.1 10.4 %all-to-all-start.1 = ((bf16[32,8,8,128]{3,2,1,0:T(8,128)(2,1)}), bf16[32,8,8,128]{3,2,1,0:T(8,128)(2,1)S(1)}, u32[]{:S(2)}, u32[]{:S(2)}) async-start(bf16[32,8,8,128]{3,2,1,0:T(8,128)(2,1)} %cut_slices.1), calls=%async_computation.1 | async-start | bytes 1048576 | tf_op jit(solution)/shard_map/all_to_all | solution.py:321
  33.3 10.3 %all-to-all-done.1 = bf16[32,8,8,128]{3,2,1,0:T(8,128)(2,1)S(1)} async-done(((bf16[32,8,8,128]{3,2,1,0:T(8,128)(2,1)}), bf16[32,8,8,128]{3,2,1,0:T(8,128)(2,1)S(1)}, u32[]{:S(2)}, u32[]{:S(2)}) %all-to-all-start.1) | async-done | bytes 524320 | tf_op jit(solution)/shard_map/all_to_all | solution.py:321
  44.4 9.4 %all-to-all-start.2 = ((bf16[8,128,1024]{2,1,0:T(8,128)(2,1)}), bf16[8,128,1024]{2,1,0:T(8,128)(2,1)S(1)}, u32[]{:S(2)}, u32[]{:S(2)}) async-start(bf16[8,128,1024]{2,1,0:T(8,128)(2,1)} %split_heads.1), calls=%async_computation.2 | async-start | bytes 4194304 | tf_op jit(solution)/shard_map/all_to_all | solution.py:336
  56.4 1.8 %gather_fusion.1 = bf16[48,8,128]{2,1,0:T(8,128)(2,1)S(1)} fusion(bf16[256,8,128]{2,1,0:T(8,128)(2,1)} %bitcast.8, s32[1024]{0:T(1024)S(1)} %pad_clamp_fusion), kind=kCustom, calls=%fused_computation.1 | custom fusion | bytes 196800 | tf_op jit(solution)/shard_map/gather | solution.py:334
  60.0 2.6 %collective-permute-done.2.refs_7_ = bf16[48,8,128]{2,1,0:T(8,128)(2,1)S(1)} collective-permute-done((bf16[48,8,128]{2,1,0:T(8,128)(2,1)S(1)}, bf16[48,8,128]{2,1,0:T(8,128)(2,1)S(1)}, u32[]{:S(2)}, u32[]{:S(2)}) %collective-permute-start.2) | collective-permute-done | bytes 98336 | tf_op jit(solution)/shard_map/ppermute | solution.py:306
  63.3 3.1 %collective-permute-done.3.refs_6_ = bf16[48,8,128]{2,1,0:T(8,128)(2,1)S(1)} collective-permute-done((bf16[48,8,128]{2,1,0:T(8,128)(2,1)S(1)}, bf16[48,8,128]{2,1,0:T(8,128)(2,1)S(1)}, u32[]{:S(2)}, u32[]{:S(2)}) %collective-permute-start.3) | collective-permute-done | bytes 98336 | tf_op jit(solution)/shard_map/ppermute | solution.py:306
  66.4 1.8 %collective-permute-start.4 = (bf16[48,8,128]{2,1,0:T(8,128)(2,1)S(1)}, bf16[48,8,128]{2,1,0:T(8,128)(2,1)S(1)}, u32[]{:S(2)}, u32[]{:S(2)}) collective-permute-start(bf16[48,8,128]{2,1,0:T(8,128)(2,1)S(1)} %collective-permute-done.3.refs_6_), channel_id=1, source_target_pairs={{0,28},{4,0},{8,4},{12,8},{16,12},{20,16},{24,20},{28,24},{1,29},{... | collective-permute-start | bytes 294920 | tf_op jit(solution)/shard_map/ppermute | solution.py:306
  68.2 4.7 %collective-permute-done.6.rest_4_ = bf16[4,256,128]{2,1,0:T(8,128)(2,1)S(1)} collective-permute-done((bf16[4,256,128]{2,1,0:T(8,128)(2,1)S(1)}, bf16[4,256,128]{2,1,0:T(8,128)(2,1)S(1)}, u32[]{:S(2)}, u32[]{:S(2)}) %collective-permute-start.6) | collective-permute-done | bytes 262176 | tf_op jit(solution)/shard_map/ppermute | solution.py:319
  74.4 2.3 %collective-permute-done.8.refs_4_ = bf16[48,8,128]{2,1,0:T(8,128)(2,1)S(1)} collective-permute-done((bf16[48,8,128]{2,1,0:T(8,128)(2,1)S(1)}, bf16[48,8,128]{2,1,0:T(8,128)(2,1)S(1)}, u32[]{:S(2)}, u32[]{:S(2)}) %collective-permute-start.8) | collective-permute-done | bytes 98336 | tf_op jit(solution)/shard_map/ppermute | solution.py:306
  78.2 2.3 %collective-permute-done.9.refs_3_ = bf16[48,8,128]{2,1,0:T(8,128)(2,1)S(1)} collective-permute-done((bf16[48,8,128]{2,1,0:T(8,128)(2,1)S(1)}, bf16[48,8,128]{2,1,0:T(8,128)(2,1)S(1)}, u32[]{:S(2)}, u32[]{:S(2)}) %collective-permute-start.9) | collective-permute-done | bytes 98336 | tf_op jit(solution)/shard_map/ppermute | solution.py:306
  80.5 2.4 %collective-permute-start.10 = (bf16[48,8,128]{2,1,0:T(8,128)(2,1)S(1)}, bf16[48,8,128]{2,1,0:T(8,128)(2,1)S(1)}, u32[]{:S(2)}, u32[]{:S(2)}) collective-permute-start(bf16[48,8,128]{2,1,0:T(8,128)(2,1)S(1)} %collective-permute-done.9.refs_3_), channel_id=1, source_target_pairs={{0,28},{4,0},{8,4},{12,8},{16,12},{20,16},{24,20},{28,24},{1,29},{... | collective-permute-start | bytes 294920 | tf_op jit(solution)/shard_map/ppermute | solution.py:306
  82.9 3.4 %collective-permute-done.7.refs_1_ = bf16[48,8,128]{2,1,0:T(8,128)(2,1)S(1)} collective-permute-done((bf16[48,8,128]{2,1,0:T(8,128)(2,1)S(1)}, bf16[48,8,128]{2,1,0:T(8,128)(2,1)S(1)}, u32[]{:S(2)}, u32[]{:S(2)}) %collective-permute-start.7) | collective-permute-done | bytes 98336 | tf_op jit(solution)/shard_map/ppermute | solution.py:306
  86.4 1.7 collective-permute-start.15
  90.8 4.1 %collective-permute-done.16.rest_7_ = bf16[4,256,128]{2,1,0:T(8,128)(2,1)S(1)} collective-permute-done((bf16[4,256,128]{2,1,0:T(8,128)(2,1)S(1)}, bf16[4,256,128]{2,1,0:T(8,128)(2,1)S(1)}, u32[]{:S(2)}, u32[]{:S(2)}) %collective-permute-start.16) | collective-permute-done | bytes 262176 | tf_op jit(solution)/shard_map/ppermute | solution.py:306
  95.9 2.4 %collective-permute-done.17.rest_8_ = bf16[4,256,128]{2,1,0:T(8,128)(2,1)S(1)} collective-permute-done((bf16[4,256,128]{2,1,0:T(8,128)(2,1)S(1)}, bf16[4,256,128]{2,1,0:T(8,128)(2,1)S(1)}, u32[]{:S(2)}, u32[]{:S(2)}) %collective-permute-start.17) | collective-permute-done | bytes 262176 | tf_op jit(solution)/shard_map/ppermute | solution.py:319
  100.6 14.2 %collective-permute-done.13.rest_10_ = bf16[8,24,8,128]{3,2,1,0:T(8,128)(2,1)} collective-permute-done((bf16[8,24,8,128]{3,2,1,0:T(8,128)(2,1)S(1)}, bf16[8,24,8,128]{3,2,1,0:T(8,128)(2,1)}, u32[]{:S(2)}, u32[]{:S(2)}) %collective-permute-start.13) | collective-permute-done | bytes 393248 | tf_op jit(solution)/shard_map/ppermute | solution.py:306
  116.1 11.1 %attend.2 = bf16[8,128,512]{2,1,0:T(8,128)(2,1)} custom-call(s32[8]{0:T(128)} %fusion.9.turns, s32[640]{0:T(1024)} %reshape.77.tile_of, f32[640]{0:T(1024)} %select_n.76.bias_of, s32[2]{0:T(128)} %pad_add_fusion.3.spot, bf16[8,128,1024]{2,1,0:T(8,128)(2,1)} %copy-done.4, bf16[2,4,256,128]{3,2,1,0:T(8,128)(2,1)} %bitcast.6, bf16[4,256,128]{2,1,0:T(8,128)(2,1)} %copy-done.6, ...), custom_call_target="tpu_custom_call" | custom-call | flops 1610612736 | bytes 8388608 | tf_op jit(solution)/shard_map/attend/pallas_call | solution.py:113
  128.8 15.1 %all-to-all-start.3 = ((bf16[8,128,512]{2,1,0:T(8,128)(2,1)}), bf16[8,128,512]{2,1,0:T(8,128)(2,1)S(1)}, u32[]{:S(2)}, u32[]{:S(2)}) async-start(bf16[8,128,512]{2,1,0:T(8,128)(2,1)} %attend.2), calls=%async_computation.3 | async-start | bytes 2097152 | tf_op jit(solution)/shard_map/all_to_all | solution.py:360
  143.9 11.0 %attend.3 = bf16[8,128,512]{2,1,0:T(8,128)(2,1)} custom-call(s32[8]{0:T(128)} %fusion.9.turns, s32[640]{0:T(1024)} %reshape.77.tile_of, f32[640]{0:T(1024)} %select_n.76.bias_of, s32[2]{0:T(128)} %pad_add_fusion.3.spot, bf16[8,128,1024]{2,1,0:T(8,128)(2,1)} %copy-done.4, bf16[2,4,256,128]{3,2,1,0:T(8,128)(2,1)} %bitcast.7, bf16[4,256,128]{2,1,0:T(8,128)(2,1)} %copy-done.6, ...), custom_call_target="tpu_custom_call" | custom-call | flops 1610612736 | bytes 8388608 | tf_op jit(solution)/shard_map/attend/pallas_call | solution.py:113
  154.9 4.0 %all-to-all-done.3.refs_0_ = bf16[8,128,512]{2,1,0:T(8,128)(2,1)S(1)} async-done(((bf16[8,128,512]{2,1,0:T(8,128)(2,1)}), bf16[8,128,512]{2,1,0:T(8,128)(2,1)S(1)}, u32[]{:S(2)}, u32[]{:S(2)}) %all-to-all-start.3) | async-done | bytes 1048608 | tf_op jit(solution)/shard_map/all_to_all | solution.py:360
  158.9 20.2 %all_to_all.25.refs_1_ = bf16[8,128,512]{2,1,0:T(8,128)(2,1)S(1)} all-to-all(bf16[8,128,512]{2,1,0:T(8,128)(2,1)} %attend.3), channel_id=1, replica_groups=mesh['x'=4,'c'=2,'z'=8,'y'=4] {'c','y'}, dimensions={0} | all-to-all | bytes 2097152 | tf_op jit(solution)/shard_map/all_to_all | solution.py:360
  (122 shorter events, 27.3 us)
Async XLA Ops:
  2.1 16.0 %all-to-all-start = ((bf16[8,256,128]{2,1,0:T(8,128)(2,1)}), bf16[8,256,128]{2,1,0:T(8,128)(2,1)S(1)}, u32[]{:S(2)}, u32[]{:S(2)}) async-start(bf16[8,256,128]{2,1,0:T(8,128)(2,1)} %split_pairs.1), calls=%async_computation | async-start | bytes 1048576 | tf_op jit(solution)/shard_map/all_to_all | solution.py:309
  19.1 24.5 %all-to-all-start.1 = ((bf16[32,8,8,128]{3,2,1,0:T(8,128)(2,1)}), bf16[32,8,8,128]{3,2,1,0:T(8,128)(2,1)S(1)}, u32[]{:S(2)}, u32[]{:S(2)}) async-start(bf16[32,8,8,128]{3,2,1,0:T(8,128)(2,1)} %cut_slices.1), calls=%async_computation.1 | async-start | bytes 1048576 | tf_op jit(solution)/shard_map/all_to_all | solution.py:321
  30.9 25.4 %collective-permute-start.1 = (bf16[4,256,128]{2,1,0:T(8,128)(2,1)}, bf16[4,256,128]{2,1,0:T(8,128)(2,1)S(1)}, u32[]{:S(2)}, u32[]{:S(2)}) collective-permute-start(bf16[4,256,128]{2,1,0:T(8,128)(2,1)} %get-tuple-element.85), channel_id=1, source_target_pairs={{0,4},{4,8},{8,12},{12,16},{16,20},{20,24},{24,28},{28,64},{64,68}... | collective-permute-start | bytes 786440 | tf_op jit(solution)/shard_map/ppermute | solution.py:319
  32.2 24.2 %collective-permute-start = (bf16[4,256,128]{2,1,0:T(8,128)(2,1)S(1)}, bf16[4,256,128]{2,1,0:T(8,128)(2,1)S(1)}, u32[]{:S(2)}, u32[]{:S(2)}) collective-permute-start(bf16[4,256,128]{2,1,0:T(8,128)(2,1)S(1)} %get-tuple-element.86), channel_id=1, source_target_pairs={{0,4},{4,8},{8,12},{12,16},{16,20},{20,24},{24,28},{28,0},{1,5},{5... | collective-permute-start | bytes 786440 | tf_op jit(solution)/shard_map/ppermute | solution.py:306
  44.4 70.4 %all-to-all-start.2 = ((bf16[8,128,1024]{2,1,0:T(8,128)(2,1)}), bf16[8,128,1024]{2,1,0:T(8,128)(2,1)S(1)}, u32[]{:S(2)}, u32[]{:S(2)}) async-start(bf16[8,128,1024]{2,1,0:T(8,128)(2,1)} %split_heads.1), calls=%async_computation.2 | async-start | bytes 4194304 | tf_op jit(solution)/shard_map/all_to_all | solution.py:336
  58.2 4.4 %collective-permute-start.2 = (bf16[48,8,128]{2,1,0:T(8,128)(2,1)S(1)}, bf16[48,8,128]{2,1,0:T(8,128)(2,1)S(1)}, u32[]{:S(2)}, u32[]{:S(2)}) collective-permute-start(bf16[48,8,128]{2,1,0:T(8,128)(2,1)S(1)} %gather_fusion.1), channel_id=1, source_target_pairs={{0,28},{4,0},{8,4},{12,8},{16,12},{20,16},{24,20},{28,24},{1,29},{... | collective-permute-start | bytes 294920 | tf_op jit(solution)/shard_map/ppermute | solution.py:306
  58.3 9.9 %collective-permute-start.5 = (bf16[4,256,128]{2,1,0:T(8,128)(2,1)S(1)}, bf16[4,256,128]{2,1,0:T(8,128)(2,1)S(1)}, u32[]{:S(2)}, u32[]{:S(2)}) collective-permute-start(bf16[4,256,128]{2,1,0:T(8,128)(2,1)S(1)} %collective-permute-done.rest_1_), channel_id=1, source_target_pairs={{0,4},{4,8},{8,12},{12,16},{16,20},{20,24},{24,28},{28,0},{1,5},{5... | collective-permute-start | bytes 786440 | tf_op jit(solution)/shard_map/ppermute | solution.py:306
  59.8 13.1 %collective-permute-start.6 = (bf16[4,256,128]{2,1,0:T(8,128)(2,1)S(1)}, bf16[4,256,128]{2,1,0:T(8,128)(2,1)S(1)}, u32[]{:S(2)}, u32[]{:S(2)}) collective-permute-start(bf16[4,256,128]{2,1,0:T(8,128)(2,1)S(1)} %collective-permute-done.1.rest_2_), channel_id=1, source_target_pairs={{0,4},{4,8},{8,12},{12,16},{16,20},{20,24},{24,28},{28,64},{64,68}... | collective-permute-start | bytes 786440 | tf_op jit(solution)/shard_map/ppermute | solution.py:319
  66.4 6.5 %collective-permute-start.4 = (bf16[48,8,128]{2,1,0:T(8,128)(2,1)S(1)}, bf16[48,8,128]{2,1,0:T(8,128)(2,1)S(1)}, u32[]{:S(2)}, u32[]{:S(2)}) collective-permute-start(bf16[48,8,128]{2,1,0:T(8,128)(2,1)S(1)} %collective-permute-done.3.refs_6_), channel_id=1, source_target_pairs={{0,28},{4,0},{8,4},{12,8},{16,12},{20,16},{24,20},{28,24},{1,29},{... | collective-permute-start | bytes 294920 | tf_op jit(solution)/shard_map/ppermute | solution.py:306
  72.9 3.8 %collective-permute-start.8 = (bf16[48,8,128]{2,1,0:T(8,128)(2,1)S(1)}, bf16[48,8,128]{2,1,0:T(8,128)(2,1)S(1)}, u32[]{:S(2)}, u32[]{:S(2)}) collective-permute-start(bf16[48,8,128]{2,1,0:T(8,128)(2,1)S(1)} %collective-permute-done.4.refs_5_), channel_id=1, source_target_pairs={{0,28},{4,0},{8,4},{12,8},{16,12},{20,16},{24,20},{28,24},{1,29},{... | collective-permute-start | bytes 294920 | tf_op jit(solution)/shard_map/ppermute | solution.py:306
  73.2 13.0 %collective-permute-start.11 = (bf16[4,256,128]{2,1,0:T(8,128)(2,1)S(1)}, bf16[4,256,128]{2,1,0:T(8,128)(2,1)S(1)}, u32[]{:S(2)}, u32[]{:S(2)}) collective-permute-start(bf16[4,256,128]{2,1,0:T(8,128)(2,1)S(1)} %collective-permute-done.5.rest_3_), channel_id=1, source_target_pairs={{0,4},{4,8},{8,12},{12,16},{16,20},{20,24},{24,28},{28,0},{1,5},{5... | collective-permute-start | bytes 786440 | tf_op jit(solution)/shard_map/ppermute | solution.py:306
  74.4 11.9 %collective-permute-start.12 = (bf16[4,256,128]{2,1,0:T(8,128)(2,1)S(1)}, bf16[4,256,128]{2,1,0:T(8,128)(2,1)S(1)}, u32[]{:S(2)}, u32[]{:S(2)}) collective-permute-start(bf16[4,256,128]{2,1,0:T(8,128)(2,1)S(1)} %collective-permute-done.6.rest_4_), channel_id=1, source_target_pairs={{0,4},{4,8},{8,12},{12,16},{16,20},{20,24},{24,28},{28,64},{64,68}... | collective-permute-start | bytes 786440 | tf_op jit(solution)/shard_map/ppermute | solution.py:319
  76.7 3.8 %collective-permute-start.9 = (bf16[48,8,128]{2,1,0:T(8,128)(2,1)S(1)}, bf16[48,8,128]{2,1,0:T(8,128)(2,1)S(1)}, u32[]{:S(2)}, u32[]{:S(2)}) collective-permute-start(bf16[48,8,128]{2,1,0:T(8,128)(2,1)S(1)} %collective-permute-done.8.refs_4_), channel_id=1, source_target_pairs={{0,28},{4,0},{8,4},{12,8},{16,12},{20,16},{24,20},{28,24},{1,29},{... | collective-permute-start | bytes 294920 | tf_op jit(solution)/shard_map/ppermute | solution.py:306
  78.2 8.0 %collective-permute-start.7 = (bf16[48,8,128]{2,1,0:T(8,128)(2,1)S(1)}, bf16[48,8,128]{2,1,0:T(8,128)(2,1)S(1)}, u32[]{:S(2)}, u32[]{:S(2)}) collective-permute-start(bf16[48,8,128]{2,1,0:T(8,128)(2,1)S(1)} %gather_fusion.1), channel_id=1, source_target_pairs={{0,4},{4,8},{8,12},{12,16},{16,20},{20,24},{24,28},{28,0},{1,5},{5... | collective-permute-start | bytes 294920 | tf_op jit(solution)/shard_map/ppermute | solution.py:306
  80.5 5.8 %collective-permute-start.10 = (bf16[48,8,128]{2,1,0:T(8,128)(2,1)S(1)}, bf16[48,8,128]{2,1,0:T(8,128)(2,1)S(1)}, u32[]{:S(2)}, u32[]{:S(2)}) collective-permute-start(bf16[48,8,128]{2,1,0:T(8,128)(2,1)S(1)} %collective-permute-done.9.refs_3_), channel_id=1, source_target_pairs={{0,28},{4,0},{8,4},{12,8},{16,12},{20,16},{24,20},{28,24},{1,29},{... | collective-permute-start | bytes 294920 | tf_op jit(solution)/shard_map/ppermute | solution.py:306
  86.4 12.4 %collective-permute-start.15 = (bf16[8,24,8,128]{3,2,1,0:T(8,128)(2,1)S(1)}, bf16[8,24,8,128]{3,2,1,0:T(8,128)(2,1)S(1)}, u32[]{:S(2)}, u32[]{:S(2)}) collective-permute-start(bf16[8,24,8,128]{3,2,1,0:T(8,128)(2,1)S(1)} %get-tuple-element.67.rest_9_), channel_id=1, source_target_pairs={{0,128},{64,192},{128,0},{192,64},{1,129},{65,193},{129,1},{193,65... | collective-permute-start | bytes 1179656 | tf_op jit(solution)/shard_map/ppermute | solution.py:306
  88.1 6.8 %collective-permute-start.16 = (bf16[4,256,128]{2,1,0:T(8,128)(2,1)S(1)}, bf16[4,256,128]{2,1,0:T(8,128)(2,1)S(1)}, u32[]{:S(2)}, u32[]{:S(2)}) collective-permute-start(bf16[4,256,128]{2,1,0:T(8,128)(2,1)S(1)} %collective-permute-done.11.rest_5_), channel_id=1, source_target_pairs={{0,4},{4,8},{8,12},{12,16},{16,20},{20,24},{24,28},{28,0},{1,5},{5... | collective-permute-start | bytes 786440 | tf_op jit(solution)/shard_map/ppermute | solution.py:306
  88.1 10.2 %collective-permute-start.17 = (bf16[4,256,128]{2,1,0:T(8,128)(2,1)S(1)}, bf16[4,256,128]{2,1,0:T(8,128)(2,1)S(1)}, u32[]{:S(2)}, u32[]{:S(2)}) collective-permute-start(bf16[4,256,128]{2,1,0:T(8,128)(2,1)S(1)} %collective-permute-done.12.rest_6_), channel_id=1, source_target_pairs={{0,4},{4,8},{8,12},{12,16},{16,20},{20,24},{24,28},{28,64},{64,68}... | collective-permute-start | bytes 786440 | tf_op jit(solution)/shard_map/ppermute | solution.py:319
  89.2 10.6 %collective-permute-start.14 = (bf16[8,24,8,128]{3,2,1,0:T(8,128)(2,1)S(1)}, bf16[8,24,8,128]{3,2,1,0:T(8,128)(2,1)S(1)}, u32[]{:S(2)}, u32[]{:S(2)}) collective-permute-start(bf16[8,24,8,128]{3,2,1,0:T(8,128)(2,1)S(1)} %get-tuple-element.67.rest_9_), channel_id=1, source_target_pairs={{0,192},{64,0},{128,64},{192,128},{1,193},{65,1},{129,65},{193,129... | collective-permute-start | bytes 1179656 | tf_op jit(solution)/shard_map/ppermute | solution.py:306
  90.8 24.0 %collective-permute-start.13 = (bf16[8,24,8,128]{3,2,1,0:T(8,128)(2,1)S(1)}, bf16[8,24,8,128]{3,2,1,0:T(8,128)(2,1)}, u32[]{:S(2)}, u32[]{:S(2)}) collective-permute-start(bf16[8,24,8,128]{3,2,1,0:T(8,128)(2,1)S(1)} %get-tuple-element.67.rest_9_), channel_id=1, source_target_pairs={{0,64},{64,128},{128,192},{192,0},{1,65},{65,129},{129,193},{193,1... | collective-permute-start | bytes 1179656 | tf_op jit(solution)/shard_map/ppermute | solution.py:306
  94.9 32.3 %collective-permute-start.20 = (bf16[8,24,8,128]{3,2,1,0:T(8,128)(2,1)S(1)}, bf16[8,24,8,128]{3,2,1,0:T(8,128)(2,1)}, u32[]{:S(2)}, u32[]{:S(2)}) collective-permute-start(bf16[8,24,8,128]{3,2,1,0:T(8,128)(2,1)S(1)} %get-tuple-element.73.rest_9_), channel_id=1, source_target_pairs={{0,128},{64,192},{128,0},{192,64},{1,129},{65,193},{129,1},{193,65... | collective-permute-start | bytes 1179656 | tf_op jit(solution)/shard_map/ppermute | solution.py:306
  98.3 28.9 %collective-permute-start.19 = (bf16[8,24,8,128]{3,2,1,0:T(8,128)(2,1)S(1)}, bf16[8,24,8,128]{3,2,1,0:T(8,128)(2,1)}, u32[]{:S(2)}, u32[]{:S(2)}) collective-permute-start(bf16[8,24,8,128]{3,2,1,0:T(8,128)(2,1)S(1)} %get-tuple-element.73.rest_9_), channel_id=1, source_target_pairs={{0,192},{64,0},{128,64},{192,128},{1,193},{65,1},{129,65},{193,129... | collective-permute-start | bytes 1179656 | tf_op jit(solution)/shard_map/ppermute | solution.py:306
  98.8 30.0 %collective-permute-start.18 = (bf16[8,24,8,128]{3,2,1,0:T(8,128)(2,1)S(1)}, bf16[8,24,8,128]{3,2,1,0:T(8,128)(2,1)}, u32[]{:S(2)}, u32[]{:S(2)}) collective-permute-start(bf16[8,24,8,128]{3,2,1,0:T(8,128)(2,1)S(1)} %get-tuple-element.73.rest_9_), channel_id=1, source_target_pairs={{0,64},{64,128},{128,192},{192,0},{1,65},{65,129},{129,193},{193,1... | collective-permute-start | bytes 1179656 | tf_op jit(solution)/shard_map/ppermute | solution.py:306
  128.8 30.1 %all-to-all-start.3 = ((bf16[8,128,512]{2,1,0:T(8,128)(2,1)}), bf16[8,128,512]{2,1,0:T(8,128)(2,1)S(1)}, u32[]{:S(2)}, u32[]{:S(2)}) async-start(bf16[8,128,512]{2,1,0:T(8,128)(2,1)} %attend.2), calls=%async_computation.3 | async-start | bytes 2097152 | tf_op jit(solution)/shard_map/all_to_all | solution.py:360
  (25 other events, 343.5 us)
